TPU v7x, 32 devices: a whole 2x2x4 slice. The times are simulated.
32 devices in a mesh: sweep: 8 (over z, y), tile: 4 (over x, core).
Axes of the slice: x: 2, y: 2, z: 4, core: 2. Of those that a mesh axis runs over, the one named last changes fastest.
Arguments:
- sources: float32 [8, 8, 4096], P('sweep', None, 'tile'), may hold values from -6 to 6
- blocks: bfloat16 [8, 32, 4, 64, 128], P('sweep', 'tile'), may hold values from -1.1 to 1.1
- pattern: int32 [8, 32, 3], P('sweep', 'tile'), may hold values from 0 to 31, as said below
Outputs:
- upper: float32 [8, 8, 4096], P('sweep', None, 'tile')
Inputs may be any that keep to these rules, and one draw needn't show every extreme that they name: `pattern`: the column blocks of one block row are distinct and differ from the row block.
All inputs are finite; a program needn't handle non-finite values.
Results may differ from a plain program's by a relative error of at most 0.0048.
Values may be sent and summed in bfloat16 or wider, within the bound.
No kernel may reach another device: no remote copies, remote signals or barrier semaphores. Data moves between devices by JAX's collectives and lax.ppermute only.
A program may use at most 64 MiB of HBM per device.

v0:
```python
import jax
import jax.numpy as jnp
from jax import lax
from jax.sharding import PartitionSpec as P

SEG = 4


def from_behind(block, axis, distance):
    devices = range(lax.axis_size(axis))
    route = [(i - distance, i) for i in devices if i - distance in devices]
    return lax.ppermute(block, axis, route)


def layer_apply(vector, layer_blocks, layer_pattern):
    gathered = lax.all_gather(vector, "tile", axis=1, tiled=True)
    nb_dev = layer_blocks.shape[0]
    width = layer_blocks.shape[-1]
    half_width = width // 2
    row_ids = lax.axis_index("tile") * nb_dev + jnp.arange(nb_dev, dtype=jnp.int32)
    tiles = gathered.reshape(gathered.shape[0], -1, width)
    column_ids = jnp.concatenate([row_ids[:, None], layer_pattern], axis=1)
    picked = jnp.take(tiles, column_ids, axis=1)
    real_in = jnp.concatenate([picked[..., :half_width], -picked[..., half_width:]], axis=-1)
    imag_in = jnp.concatenate([picked[..., half_width:], picked[..., :half_width]], axis=-1)
    real_out = jnp.einsum(
        "rbkc,bkoc->rbo", real_in, layer_blocks, preferred_element_type=jnp.float32
    )
    imag_out = jnp.einsum(
        "rbkc,bkoc->rbo", imag_in, layer_blocks, preferred_element_type=jnp.float32
    )
    return jnp.concatenate([real_out, imag_out], axis=-1).reshape(vector.shape[0], -1)


def per_device(sources, blocks, pattern):
    groups = 1
    per_group = sources.shape[1] // groups
    lay_count = sources.shape[0]
    seg_pos = (lax.axis_index("sweep") + SEG // 2) % SEG
    keep_down = (seg_pos != 0).astype(jnp.float32)
    keep_up = (seg_pos != SEG - 1).astype(jnp.float32)
    front_zero = jnp.zeros((per_group, sources.shape[2]), jnp.float32)

    def descend(turn, loop_state):
        stored, front_val = loop_state
        received = from_behind(front_val, "sweep", 1) * keep_down
        group_now = turn - seg_pos
        active = (group_now >= 0) & (group_now < groups)
        offset = jnp.clip(group_now, 0, groups - 1) * per_group
        summed = (sources[0] + received).astype(jnp.bfloat16)
        received = layer_apply(summed, blocks[0], pattern[0])
        results = [received]
        updated = lax.dynamic_update_slice_in_dim(stored, jnp.stack(results), offset, 1)
        return (jnp.where(active, updated, stored), received)

    down, _ = lax.fori_loop(0, SEG + groups - 1, descend, (jnp.zeros_like(sources), front_zero))

    def ascend(turn, loop_state):
        stored, front_val = loop_state
        received = (
            from_behind(front_val.astype(jnp.bfloat16), "sweep", -1).astype(front_val.dtype)
            * keep_up
        )
        group_now = turn - (SEG - 1 - seg_pos)
        active = (group_now >= 0) & (group_now < groups)
        offset = jnp.clip(group_now, 0, groups - 1) * per_group
        results = [front_zero] * lay_count
        for layer in reversed(range(lay_count)):
            received = down[layer] + layer_apply(
                received.astype(jnp.bfloat16), blocks[layer], pattern[layer]
            )
            results[layer] = received
        updated = lax.dynamic_update_slice_in_dim(stored, jnp.stack(results), offset, 1)
        return (jnp.where(active, updated, stored), received)

    upper, _ = lax.fori_loop(0, SEG + groups - 1, ascend, (jnp.zeros_like(sources), front_zero))
    return upper


def solution(mesh):
    return jax.shard_map(
        per_device,
        mesh=mesh,
        in_specs=(
            P("sweep", None, "tile"),
            P("sweep", "tile", None, None, None),
            P("sweep", "tile", None),
        ),
        out_specs=P("sweep", None, "tile"),
        check_vma=False,
    )
```

profile of v0, /device:TPU:0, one launch (start us, length us, event | category | flops | bytes accessed | tf_op | source)
XLA Modules:
  0.0 108.9 jit_solution(11279773425922796382)
XLA Ops:
  0.0 0.7 copy-done.4
  0.8 52.8 %while.34 = (s32[]{:T(128)}, f32[1,8,1024]{2,1,0:T(8,128)S(1)}, f32[8,1024]{1,0:T(8,128)S(1)}, s32[]{:T(128)}, f32[1,8,1024]{2,1,0:T(8,128)S(1)}, /*index=5*/f32...) while((s32[]{:T(128)}, f32[1,8,1024]{2,1,0:T(8,128)S(1)}, ...), condition=%wide.region_1.3_spmd.clone, body=%wide.region_0.2_spmd.clone.sunk | while | flops 8758514 | bytes 4199853 | solution.py:56
  0.8 5.0 %collective-permute-start = (f32[8,1024]{1,0:T(8,128)S(1)}, f32[8,1024]{1,0:T(8,128)S(1)}, u32[]{:S(2)}, u32[]{:S(2)}) collective-permute-start(f32[8,1024]{1,0:T(8,128)S(1)} %get-tuple-element.598), channel_id=1, source_target_pairs={{0,4},{4,8},{8,12},{12,16},{16,20},{20,24},{24,28},{1,5},{5,9},{9,... | collective-permute-start | bytes 98312 | tf_op jit(solution)/shard_map/while/body/eval_jaxpr/ppermute | solution.py:12
  6.1 1.3 %collective-permute-done = f32[8,1024]{1,0:T(8,128)S(1)} collective-permute-done((f32[8,1024]{1,0:T(8,128)S(1)}, f32[8,1024]{1,0:T(8,128)S(1)}, u32[]{:S(2)}, u32[]{:S(2)}) %collective-permute-start) | collective-permute-done | bytes 32800 | tf_op jit(solution)/shard_map/while/body/eval_jaxpr/ppermute | solution.py:12
  7.4 5.2 %all_gather.20 = bf16[8,4096]{1,0:T(8,128)(2,1)S(1)} all-gather(bf16[8,1024]{1,0:T(8,128)(2,1)S(1)} %fusion.38), channel_id=1, replica_groups=mesh['sweep'=8,'tile'=4] {'tile'}, dimensions={1}, use_global_device_ids=true | all-gather | bytes 81920 | tf_op jit(solution)/shard_map/while/body/eval_jaxpr/all_gather | solution.py:16
  14.2 4.4 %collective-permute-start = (f32[8,1024]{1,0:T(8,128)S(1)}, f32[8,1024]{1,0:T(8,128)S(1)}, u32[]{:S(2)}, u32[]{:S(2)}) collective-permute-start(f32[8,1024]{1,0:T(8,128)S(1)} %get-tuple-element.598), channel_id=1, source_target_pairs={{0,4},{4,8},{8,12},{12,16},{16,20},{20,24},{24,28},{1,5},{5,9},{9,... | collective-permute-start | bytes 98312 | tf_op jit(solution)/shard_map/while/body/eval_jaxpr/ppermute | solution.py:12
  18.9 1.3 %collective-permute-done = f32[8,1024]{1,0:T(8,128)S(1)} collective-permute-done((f32[8,1024]{1,0:T(8,128)S(1)}, f32[8,1024]{1,0:T(8,128)S(1)}, u32[]{:S(2)}, u32[]{:S(2)}) %collective-permute-start) | collective-permute-done | bytes 32800 | tf_op jit(solution)/shard_map/while/body/eval_jaxpr/ppermute | solution.py:12
  20.2 5.2 %all_gather.20 = bf16[8,4096]{1,0:T(8,128)(2,1)S(1)} all-gather(bf16[8,1024]{1,0:T(8,128)(2,1)S(1)} %fusion.38), channel_id=1, replica_groups=mesh['sweep'=8,'tile'=4] {'tile'}, dimensions={1}, use_global_device_ids=true | all-gather | bytes 81920 | tf_op jit(solution)/shard_map/while/body/eval_jaxpr/all_gather | solution.py:16
  25.4 0.6 gather_fusion
  27.0 4.5 %collective-permute-start = (f32[8,1024]{1,0:T(8,128)S(1)}, f32[8,1024]{1,0:T(8,128)S(1)}, u32[]{:S(2)}, u32[]{:S(2)}) collective-permute-start(f32[8,1024]{1,0:T(8,128)S(1)} %get-tuple-element.598), channel_id=1, source_target_pairs={{0,4},{4,8},{8,12},{12,16},{16,20},{20,24},{24,28},{1,5},{5,9},{9,... | collective-permute-start | bytes 98312 | tf_op jit(solution)/shard_map/while/body/eval_jaxpr/ppermute | solution.py:12
  31.8 1.3 %collective-permute-done = f32[8,1024]{1,0:T(8,128)S(1)} collective-permute-done((f32[8,1024]{1,0:T(8,128)S(1)}, f32[8,1024]{1,0:T(8,128)S(1)}, u32[]{:S(2)}, u32[]{:S(2)}) %collective-permute-start) | collective-permute-done | bytes 32800 | tf_op jit(solution)/shard_map/while/body/eval_jaxpr/ppermute | solution.py:12
  33.0 5.2 %all_gather.20 = bf16[8,4096]{1,0:T(8,128)(2,1)S(1)} all-gather(bf16[8,1024]{1,0:T(8,128)(2,1)S(1)} %fusion.38), channel_id=1, replica_groups=mesh['sweep'=8,'tile'=4] {'tile'}, dimensions={1}, use_global_device_ids=true | all-gather | bytes 81920 | tf_op jit(solution)/shard_map/while/body/eval_jaxpr/all_gather | solution.py:16
  38.3 0.6 gather_fusion
  39.9 5.3 %collective-permute-start = (f32[8,1024]{1,0:T(8,128)S(1)}, f32[8,1024]{1,0:T(8,128)S(1)}, u32[]{:S(2)}, u32[]{:S(2)}) collective-permute-start(f32[8,1024]{1,0:T(8,128)S(1)} %get-tuple-element.598), channel_id=1, source_target_pairs={{0,4},{4,8},{8,12},{12,16},{16,20},{20,24},{24,28},{1,5},{5,9},{9,... | collective-permute-start | bytes 98312 | tf_op jit(solution)/shard_map/while/body/eval_jaxpr/ppermute | solution.py:12
  45.5 1.3 %collective-permute-done = f32[8,1024]{1,0:T(8,128)S(1)} collective-permute-done((f32[8,1024]{1,0:T(8,128)S(1)}, f32[8,1024]{1,0:T(8,128)S(1)}, u32[]{:S(2)}, u32[]{:S(2)}) %collective-permute-start) | collective-permute-done | bytes 32800 | tf_op jit(solution)/shard_map/while/body/eval_jaxpr/ppermute | solution.py:12
  46.7 5.2 %all_gather.20 = bf16[8,4096]{1,0:T(8,128)(2,1)S(1)} all-gather(bf16[8,1024]{1,0:T(8,128)(2,1)S(1)} %fusion.38), channel_id=1, replica_groups=mesh['sweep'=8,'tile'=4] {'tile'}, dimensions={1}, use_global_device_ids=true | all-gather | bytes 81920 | tf_op jit(solution)/shard_map/while/body/eval_jaxpr/all_gather | solution.py:16
  52.0 0.6 gather_fusion
  53.6 54.7 %while.35 = (s32[]{:T(128)}, f32[1,8,1024]{2,1,0:T(8,128)S(1)}, bf16[8,1024]{1,0:T(8,128)(2,1)S(1)}, s32[]{:T(128)}, f32[]{:T(128)}, /*index=5*/s32[1,8,3]{1,2,0...) while((s32[]{:T(128)}, f32[1,8,1024]{2,1,0:T(8,128)S(1)}, ...), condition=%wide.region_3.5_spmd.clone, body=%wide.region_2.4_spmd.clone.sunk | while | flops 8791282 | bytes 4167086 | solution.py:76
  53.6 1.4 %collective-permute-start.1 = (bf16[8,1024]{1,0:T(8,128)(2,1)S(1)}, bf16[8,1024]{1,0:T(8,128)(2,1)S(1)}, u32[]{:S(2)}, u32[]{:S(2)}) collective-permute-start(bf16[8,1024]{1,0:T(8,128)(2,1)S(1)} %select_convert_fusion.2), channel_id=1, source_target_pairs={{4,0},{8,4},{12,8},{16,12},{20,16},{24,20},{28,24},{5,1},{9,5},{13... | collective-permute-start | bytes 49160 | tf_op jit(solution)/shard_map/while/body/eval_jaxpr/ppermute | solution.py:12
  55.3 5.2 %collective-permute-done.1 = bf16[8,1024]{1,0:T(8,128)(2,1)S(1)} collective-permute-done((bf16[8,1024]{1,0:T(8,128)(2,1)S(1)}, bf16[8,1024]{1,0:T(8,128)(2,1)S(1)}, u32[]{:S(2)}, u32[]{:S(2)}) %collective-permute-start.1) | collective-permute-done | bytes 16416 | tf_op jit(solution)/shard_map/while/body/eval_jaxpr/ppermute | solution.py:12
  60.6 5.2 %all_gather.21 = bf16[8,4096]{1,0:T(8,128)(2,1)S(1)} all-gather(bf16[8,1024]{1,0:T(8,128)(2,1)S(1)} %multiply_convert_fusion.2), channel_id=1, replica_groups=mesh['sweep'=8,'tile'=4] {'tile'}, dimensions={1}, use_global_device_ids=true | all-gather | bytes 81920 | tf_op jit(solution)/shard_map/while/body/eval_jaxpr/all_gather | solution.py:16
  65.8 0.6 gather_fusion.1
  67.4 1.4 %collective-permute-start.1 = (bf16[8,1024]{1,0:T(8,128)(2,1)S(1)}, bf16[8,1024]{1,0:T(8,128)(2,1)S(1)}, u32[]{:S(2)}, u32[]{:S(2)}) collective-permute-start(bf16[8,1024]{1,0:T(8,128)(2,1)S(1)} %select_convert_fusion.2), channel_id=1, source_target_pairs={{4,0},{8,4},{12,8},{16,12},{20,16},{24,20},{28,24},{5,1},{9,5},{13... | collective-permute-start | bytes 49160 | tf_op jit(solution)/shard_map/while/body/eval_jaxpr/ppermute | solution.py:12
  69.2 5.2 %collective-permute-done.1 = bf16[8,1024]{1,0:T(8,128)(2,1)S(1)} collective-permute-done((bf16[8,1024]{1,0:T(8,128)(2,1)S(1)}, bf16[8,1024]{1,0:T(8,128)(2,1)S(1)}, u32[]{:S(2)}, u32[]{:S(2)}) %collective-permute-start.1) | collective-permute-done | bytes 16416 | tf_op jit(solution)/shard_map/while/body/eval_jaxpr/ppermute | solution.py:12
  74.4 5.2 %all_gather.21 = bf16[8,4096]{1,0:T(8,128)(2,1)S(1)} all-gather(bf16[8,1024]{1,0:T(8,128)(2,1)S(1)} %multiply_convert_fusion.2), channel_id=1, replica_groups=mesh['sweep'=8,'tile'=4] {'tile'}, dimensions={1}, use_global_device_ids=true | all-gather | bytes 81920 | tf_op jit(solution)/shard_map/while/body/eval_jaxpr/all_gather | solution.py:16
  81.3 1.4 %collective-permute-start.1 = (bf16[8,1024]{1,0:T(8,128)(2,1)S(1)}, bf16[8,1024]{1,0:T(8,128)(2,1)S(1)}, u32[]{:S(2)}, u32[]{:S(2)}) collective-permute-start(bf16[8,1024]{1,0:T(8,128)(2,1)S(1)} %select_convert_fusion.2), channel_id=1, source_target_pairs={{4,0},{8,4},{12,8},{16,12},{20,16},{24,20},{28,24},{5,1},{9,5},{13... | collective-permute-start | bytes 49160 | tf_op jit(solution)/shard_map/while/body/eval_jaxpr/ppermute | solution.py:12
  83.0 4.9 %collective-permute-done.1 = bf16[8,1024]{1,0:T(8,128)(2,1)S(1)} collective-permute-done((bf16[8,1024]{1,0:T(8,128)(2,1)S(1)}, bf16[8,1024]{1,0:T(8,128)(2,1)S(1)}, u32[]{:S(2)}, u32[]{:S(2)}) %collective-permute-start.1) | collective-permute-done | bytes 16416 | tf_op jit(solution)/shard_map/while/body/eval_jaxpr/ppermute | solution.py:12
  87.9 5.2 %all_gather.21 = bf16[8,4096]{1,0:T(8,128)(2,1)S(1)} all-gather(bf16[8,1024]{1,0:T(8,128)(2,1)S(1)} %multiply_convert_fusion.2), channel_id=1, replica_groups=mesh['sweep'=8,'tile'=4] {'tile'}, dimensions={1}, use_global_device_ids=true | all-gather | bytes 81920 | tf_op jit(solution)/shard_map/while/body/eval_jaxpr/all_gather | solution.py:16
  94.8 1.4 %collective-permute-start.1 = (bf16[8,1024]{1,0:T(8,128)(2,1)S(1)}, bf16[8,1024]{1,0:T(8,128)(2,1)S(1)}, u32[]{:S(2)}, u32[]{:S(2)}) collective-permute-start(bf16[8,1024]{1,0:T(8,128)(2,1)S(1)} %select_convert_fusion.2), channel_id=1, source_target_pairs={{4,0},{8,4},{12,8},{16,12},{20,16},{24,20},{28,24},{5,1},{9,5},{13... | collective-permute-start | bytes 49160 | tf_op jit(solution)/shard_map/while/body/eval_jaxpr/ppermute | solution.py:12
  96.5 4.9 %collective-permute-done.1 = bf16[8,1024]{1,0:T(8,128)(2,1)S(1)} collective-permute-done((bf16[8,1024]{1,0:T(8,128)(2,1)S(1)}, bf16[8,1024]{1,0:T(8,128)(2,1)S(1)}, u32[]{:S(2)}, u32[]{:S(2)}) %collective-permute-start.1) | collective-permute-done | bytes 16416 | tf_op jit(solution)/shard_map/while/body/eval_jaxpr/ppermute | solution.py:12
  101.5 5.2 %all_gather.21 = bf16[8,4096]{1,0:T(8,128)(2,1)S(1)} all-gather(bf16[8,1024]{1,0:T(8,128)(2,1)S(1)} %multiply_convert_fusion.2), channel_id=1, replica_groups=mesh['sweep'=8,'tile'=4] {'tile'}, dimensions={1}, use_global_device_ids=true | all-gather | bytes 81920 | tf_op jit(solution)/shard_map/while/body/eval_jaxpr/all_gather | solution.py:16
  108.3 0.6 copy-done.2
  (137 shorter events, 12.6 us)
Async XLA Ops:
  0.0 0.7 copy-start.4
  0.0 0.8 copy-start.3
  0.8 12.6 %copy-start = (bf16[1,8,4,64,128]{4,3,2,1,0:T(8,128)(2,1)S(1)}, bf16[1,8,4,64,128]{4,3,2,1,0:T(8,128)(2,1)}, u32[]{:S(2)}) copy-start(bf16[1,8,4,64,128]{4,3,2,1,0:T(8,128)(2,1)} %get-tuple-element.615) | copy-start | bytes 1572868 | tf_op jit(solution)/shard_map/while
  0.8 6.6 %collective-permute-start = (f32[8,1024]{1,0:T(8,128)S(1)}, f32[8,1024]{1,0:T(8,128)S(1)}, u32[]{:S(2)}, u32[]{:S(2)}) collective-permute-start(f32[8,1024]{1,0:T(8,128)S(1)} %get-tuple-element.598), channel_id=1, source_target_pairs={{0,4},{4,8},{8,12},{12,16},{16,20},{20,24},{24,28},{1,5},{5,9},{9,... | collective-permute-start | bytes 98312 | tf_op jit(solution)/shard_map/while/body/eval_jaxpr/ppermute | solution.py:12
  14.2 12.0 %copy-start = (bf16[1,8,4,64,128]{4,3,2,1,0:T(8,128)(2,1)S(1)}, bf16[1,8,4,64,128]{4,3,2,1,0:T(8,128)(2,1)}, u32[]{:S(2)}) copy-start(bf16[1,8,4,64,128]{4,3,2,1,0:T(8,128)(2,1)} %get-tuple-element.615) | copy-start | bytes 1572868 | tf_op jit(solution)/shard_map/while
  14.2 6.0 %collective-permute-start = (f32[8,1024]{1,0:T(8,128)S(1)}, f32[8,1024]{1,0:T(8,128)S(1)}, u32[]{:S(2)}, u32[]{:S(2)}) collective-permute-start(f32[8,1024]{1,0:T(8,128)S(1)} %get-tuple-element.598), channel_id=1, source_target_pairs={{0,4},{4,8},{8,12},{12,16},{16,20},{20,24},{24,28},{1,5},{5,9},{9,... | collective-permute-start | bytes 98312 | tf_op jit(solution)/shard_map/while/body/eval_jaxpr/ppermute | solution.py:12
  27.0 12.1 %copy-start = (bf16[1,8,4,64,128]{4,3,2,1,0:T(8,128)(2,1)S(1)}, bf16[1,8,4,64,128]{4,3,2,1,0:T(8,128)(2,1)}, u32[]{:S(2)}) copy-start(bf16[1,8,4,64,128]{4,3,2,1,0:T(8,128)(2,1)} %get-tuple-element.615) | copy-start | bytes 1572868 | tf_op jit(solution)/shard_map/while
  27.0 6.0 %collective-permute-start = (f32[8,1024]{1,0:T(8,128)S(1)}, f32[8,1024]{1,0:T(8,128)S(1)}, u32[]{:S(2)}, u32[]{:S(2)}) collective-permute-start(f32[8,1024]{1,0:T(8,128)S(1)} %get-tuple-element.598), channel_id=1, source_target_pairs={{0,4},{4,8},{8,12},{12,16},{16,20},{20,24},{24,28},{1,5},{5,9},{9,... | collective-permute-start | bytes 98312 | tf_op jit(solution)/shard_map/while/body/eval_jaxpr/ppermute | solution.py:12
  39.9 12.9 %copy-start = (bf16[1,8,4,64,128]{4,3,2,1,0:T(8,128)(2,1)S(1)}, bf16[1,8,4,64,128]{4,3,2,1,0:T(8,128)(2,1)}, u32[]{:S(2)}) copy-start(bf16[1,8,4,64,128]{4,3,2,1,0:T(8,128)(2,1)} %get-tuple-element.615) | copy-start | bytes 1572868 | tf_op jit(solution)/shard_map/while
  39.9 6.9 %collective-permute-start = (f32[8,1024]{1,0:T(8,128)S(1)}, f32[8,1024]{1,0:T(8,128)S(1)}, u32[]{:S(2)}, u32[]{:S(2)}) collective-permute-start(f32[8,1024]{1,0:T(8,128)S(1)} %get-tuple-element.598), channel_id=1, source_target_pairs={{0,4},{4,8},{8,12},{12,16},{16,20},{20,24},{24,28},{1,5},{5,9},{9,... | collective-permute-start | bytes 98312 | tf_op jit(solution)/shard_map/while/body/eval_jaxpr/ppermute | solution.py:12
  53.6 13.0 %copy-start.1 = (bf16[1,8,4,64,128]{4,3,2,1,0:T(8,128)(2,1)S(1)}, bf16[1,8,4,64,128]{4,3,2,1,0:T(8,128)(2,1)}, u32[]{:S(2)}) copy-start(bf16[1,8,4,64,128]{4,3,2,1,0:T(8,128)(2,1)} %get-tuple-element.650) | copy-start | bytes 1572868 | tf_op jit(solution)/shard_map/while
  53.6 7.0 %collective-permute-start.1 = (bf16[8,1024]{1,0:T(8,128)(2,1)S(1)}, bf16[8,1024]{1,0:T(8,128)(2,1)S(1)}, u32[]{:S(2)}, u32[]{:S(2)}) collective-permute-start(bf16[8,1024]{1,0:T(8,128)(2,1)S(1)} %select_convert_fusion.2), channel_id=1, source_target_pairs={{4,0},{8,4},{12,8},{16,12},{20,16},{24,20},{28,24},{5,1},{9,5},{13... | collective-permute-start | bytes 49160 | tf_op jit(solution)/shard_map/while/body/eval_jaxpr/ppermute | solution.py:12
  67.4 13.0 %copy-start.1 = (bf16[1,8,4,64,128]{4,3,2,1,0:T(8,128)(2,1)S(1)}, bf16[1,8,4,64,128]{4,3,2,1,0:T(8,128)(2,1)}, u32[]{:S(2)}) copy-start(bf16[1,8,4,64,128]{4,3,2,1,0:T(8,128)(2,1)} %get-tuple-element.650) | copy-start | bytes 1572868 | tf_op jit(solution)/shard_map/while
  67.4 7.0 %collective-permute-start.1 = (bf16[8,1024]{1,0:T(8,128)(2,1)S(1)}, bf16[8,1024]{1,0:T(8,128)(2,1)S(1)}, u32[]{:S(2)}, u32[]{:S(2)}) collective-permute-start(bf16[8,1024]{1,0:T(8,128)(2,1)S(1)} %select_convert_fusion.2), channel_id=1, source_target_pairs={{4,0},{8,4},{12,8},{16,12},{20,16},{24,20},{28,24},{5,1},{9,5},{13... | collective-permute-start | bytes 49160 | tf_op jit(solution)/shard_map/while/body/eval_jaxpr/ppermute | solution.py:12
  81.2 12.7 %copy-start.1 = (bf16[1,8,4,64,128]{4,3,2,1,0:T(8,128)(2,1)S(1)}, bf16[1,8,4,64,128]{4,3,2,1,0:T(8,128)(2,1)}, u32[]{:S(2)}) copy-start(bf16[1,8,4,64,128]{4,3,2,1,0:T(8,128)(2,1)} %get-tuple-element.650) | copy-start | bytes 1572868 | tf_op jit(solution)/shard_map/while
  81.3 6.7 %collective-permute-start.1 = (bf16[8,1024]{1,0:T(8,128)(2,1)S(1)}, bf16[8,1024]{1,0:T(8,128)(2,1)S(1)}, u32[]{:S(2)}, u32[]{:S(2)}) collective-permute-start(bf16[8,1024]{1,0:T(8,128)(2,1)S(1)} %select_convert_fusion.2), channel_id=1, source_target_pairs={{4,0},{8,4},{12,8},{16,12},{20,16},{24,20},{28,24},{5,1},{9,5},{13... | collective-permute-start | bytes 49160 | tf_op jit(solution)/shard_map/while/body/eval_jaxpr/ppermute | solution.py:12
  94.8 12.7 %copy-start.1 = (bf16[1,8,4,64,128]{4,3,2,1,0:T(8,128)(2,1)S(1)}, bf16[1,8,4,64,128]{4,3,2,1,0:T(8,128)(2,1)}, u32[]{:S(2)}) copy-start(bf16[1,8,4,64,128]{4,3,2,1,0:T(8,128)(2,1)} %get-tuple-element.650) | copy-start | bytes 1572868 | tf_op jit(solution)/shard_map/while
  94.8 6.7 %collective-permute-start.1 = (bf16[8,1024]{1,0:T(8,128)(2,1)S(1)}, bf16[8,1024]{1,0:T(8,128)(2,1)S(1)}, u32[]{:S(2)}, u32[]{:S(2)}) collective-permute-start(bf16[8,1024]{1,0:T(8,128)(2,1)S(1)} %select_convert_fusion.2), channel_id=1, source_target_pairs={{4,0},{8,4},{12,8},{16,12},{20,16},{24,20},{28,24},{5,1},{9,5},{13... | collective-permute-start | bytes 49160 | tf_op jit(solution)/shard_map/while/body/eval_jaxpr/ppermute | solution.py:12
  108.3 0.6 copy-start.2
where the time goes:
time: 110 us; the launch traced here: 109 us
  blocking collectives  41.8 us (38%)
  waiting for transfers between devices  25.4 us (23%)
  starting transfers between devices  24.8 us (23%)
  local copies, waits for them, and re-layouts  8.23 us (7%)
  matrix products  4.73 us (4%)
  other arithmetic  3.34 us (3%)
    all_gather x8, blocking collectives, layer_apply(): gathered = lax.all_gather(vector, 'tile', axis=1, tiled=True)  41.8 us
    ppermute x8, waiting for transfers between devices, from_behind(): return lax.ppermute(block, axis, route)  25.4 us
    ppermute x8, starting transfers between devices, from_behind(): return lax.ppermute(block, axis, route)  24.8 us
    gather x8, local copies, waits for them, and re-layouts, layer_apply(): picked = jnp.take(tiles, column_ids, axis=1)  4.72 us
    dot_general x8, matrix products, layer_apply(): jnp.einsum('rbkc,bkoc->rbo', imag_in, layer_blocks, preferred_element_typ...  2.48 us
    dot_general x8, matrix products, layer_apply(): jnp.einsum('rbkc,bkoc->rbo', real_in, layer_blocks, preferred_element_typ...  2.25 us
  transfers between devices with their start and end apart: 8, of which 8 were waited for; matrix products, arithmetic and copies ran while one was open for 2% of the time, Pallas kernels for 0%

commit v1 on v0

v1 whole, which is shorter than its diff:
```python
import functools

import jax
import jax.numpy as jnp
from jax import lax
from jax.experimental import pallas as pl
from jax.experimental.pallas import tpu as pltpu
from jax.sharding import PartitionSpec as P

SEG = 4
AXES = ("sweep", "tile")


def swap_route(pairs, sweeps, tiles, flip):
    route = []
    for layer in range(sweeps):
        other = pairs.get(layer, layer)
        mask = flip if other != layer else (flip or 1)
        route += [(layer * tiles + t, other * tiles + (t ^ mask)) for t in range(tiles)]
    return route


def apply_kernel(pieces, with_src, stage, info, *refs):
    recs, refs = refs[:pieces], refs[pieces:]
    if with_src:
        srcs, refs = refs[: with_src], refs[with_src:]
    own_blocks, pair_blocks, state_in, state_out, msg_out, vec = refs
    nb = own_blocks.shape[0]
    width = own_blocks.shape[-1]
    half = width // 2
    lane = lax.broadcasted_iota(jnp.int32, (1, 1, width), 2)
    sign = jnp.where(lane < half, 1.0, -1.0).astype(jnp.float32)
    at = 0
    for rec in recs:
        count = rec.shape[0]
        value = rec[...].astype(jnp.float32)
        if with_src:
            src = jnp.concatenate([s[...] for s in srcs[at // nb : (at + count) // nb]], axis=0)
            value = src if stage == 0 else value + src
        value = value.astype(jnp.bfloat16).astype(jnp.float32)
        real_in = value * sign
        imag_in = pltpu.roll(value, half, axis=2)
        vec[pl.ds(at, count)] = jnp.concatenate([real_in, imag_in], axis=1).astype(jnp.bfloat16)
        at += count
    rows = 2 * nb
    active = info[rows * 4 + stage] != 0
    for row in range(rows):
        source = own_blocks if row < nb else pair_blocks
        mats = jnp.concatenate([source[row % nb, j] for j in range(4)], axis=1)
        inputs = jnp.concatenate([vec[info[row * 4 + j]] for j in range(4)], axis=1)
        out = lax.dot_general(
            inputs, mats, (((1,), (1,)), ((), ())), preferred_element_type=jnp.float32
        )
        rhs = out.shape[0] // 2
        result = jnp.concatenate([out[:rhs], out[rhs:]], axis=1)
        state = jnp.where(active, state_in[row] + result, state_in[row])
        state_out[row] = state
        msg = result if stage < SEG - 1 else state
        msg_out[row] = msg.astype(jnp.bfloat16)


def layer_apply(stage, info, recs, srcs, own_blocks, pair_blocks, state):
    nb = own_blocks.shape[0]
    total = sum(r.shape[0] for r in recs)
    rhs, width = recs[0].shape[1:]
    vmem = pl.BlockSpec(memory_space=pltpu.VMEM)
    args = [*recs, *srcs, own_blocks, pair_blocks, state]
    return pl.pallas_call(
        functools.partial(apply_kernel, len(recs), len(srcs), stage),
        in_specs=[pl.BlockSpec(memory_space=pltpu.SMEM)] + [vmem] * len(args),
        out_specs=[vmem, vmem],
        out_shape=[
            jax.ShapeDtypeStruct((2 * nb, rhs, width), jnp.float32),
            jax.ShapeDtypeStruct((2 * nb, rhs, width), jnp.bfloat16),
        ],
        scratch_shapes=[pltpu.VMEM((total, 2 * rhs, width), jnp.bfloat16)],
        name=f"apply_{stage}",
    )(info, *args)


def per_device(sources, blocks, pattern):
    sweeps, tiles = lax.axis_size("sweep"), lax.axis_size("tile")
    sweep, tile = lax.axis_index("sweep"), lax.axis_index("tile")
    own_blocks, own_pattern = blocks[0], pattern[0]
    nb, width = own_blocks.shape[0], own_blocks.shape[-1]
    rhs = sources.shape[1]

    flat = {layer: layer ^ 1 for layer in range(sweeps)}
    odd = {layer: ((layer + 1) ^ 1) - 1 for layer in range(1, sweeps - 1)}
    same = {}

    def exchange(value, pairs, flip):
        return lax.ppermute(value, AXES, swap_route(pairs, sweeps, tiles, flip))

    def own_swap(value, flip):
        return lax.ppermute(value, "tile", [(t, t ^ flip) for t in range(tiles)])

    src_own = sources[0].reshape(rhs, nb, width).transpose(1, 0, 2)
    srcs = [src_own] + [own_swap(src_own, flip) for flip in range(1, tiles)]
    pair_blocks = own_swap(own_blocks, 1)
    pair_pattern = own_swap(own_pattern, 1)

    local = jnp.arange(nb, dtype=jnp.int32)
    columns = jnp.concatenate(
        [
            jnp.concatenate([(tile ^ flip) * nb + local[:, None], pat], axis=1)
            for flip, pat in ((0, own_pattern), (1, pair_pattern))
        ],
        axis=0,
    )
    slots = ((columns // nb) ^ tile) * nb + columns % nb
    first = jnp.maximum(((sweep + SEG // 2) // SEG) * SEG - SEG // 2, 0)
    place = sweep - first
    last = ((sweep + 1) % SEG == SEG // 2) | (sweep == sweeps - 1)
    flags = [place == stage for stage in range(SEG)]
    flags += [(place == SEG - 2 - step) & ~last for step in range(SEG - 1)]
    info = jnp.concatenate([slots.reshape(-1), jnp.stack(flags).astype(jnp.int32)])

    state = jnp.zeros((2 * nb, rhs, width), jnp.float32)
    stage_pairs = [flat, odd, flat, flat, odd, flat]
    recs = srcs
    for stage in range(2 * SEG - 1):
        state, msg = layer_apply(
            stage, info, recs, srcs if stage < SEG else [], own_blocks, pair_blocks, state
        )
        if stage < 2 * SEG - 2:
            recs = [exchange(msg, stage_pairs[stage], flip) for flip in range(0, tiles, 2)]
    return state[:nb].transpose(1, 0, 2).reshape(1, rhs, nb * width)


def solution(mesh):
    return jax.shard_map(
        per_device,
        mesh=mesh,
        in_specs=(
            P("sweep", None, "tile"),
            P("sweep", "tile", None, None, None),
            P("sweep", "tile", None),
        ),
        out_specs=P("sweep", None, "tile"),
        check_vma=False,
    )
```

time: 110 us -> 67.7 us (0.62)
  blocking collectives: 41.8 us -> 0 us
  Pallas kernels: 0 us -> 17.2 us
  matrix products: 4.73 us -> 0 us
  starting transfers between devices: 24.8 us -> 20.3 us
  waiting for transfers between devices: 25.4 us -> 22.8 us
  other arithmetic: 3.34 us -> 0.75 us
  local copies, waits for them, and re-layouts: 8.23 us -> 6.15 us
    all_gather x8 -> x0, blocking collectives: 41.8 us -> none  [layer_apply(): gathered = lax.all_gather(vector, 'tile', axis=1, tiled=True)]
    pallas_call x0 -> x7, Pallas kernels: none -> 17.2 us  [layer_apply(): pl.pallas_call(functools.partial(apply_kernel, len(recs), len(srcs), stag...]
    dot_general x16 -> x0, matrix products: 4.73 us -> none  [the longest x8 2.48 us: layer_apply(): jnp.einsum('rbkc,bkoc->rbo', imag_in, layer_blocks, preferred_element_typ...]
    gather x8 -> x0, local copies, waits for them, and re-layouts: 4.72 us -> none  [layer_apply(): picked = jnp.take(tiles, column_ids, axis=1)]
    ppermute x8 -> x17, starting transfers between devices: 24.8 us -> 20.3 us  [the longest x12 16.7 us: exchange(): return lax.ppermute(value, AXES, swap_route(pairs, sweeps, tiles, flip))]
    ppermute x8 -> x17, waiting for transfers between devices: 25.4 us -> 22.8 us  [the longest x12 20.9 us: exchange(): return lax.ppermute(value, AXES, swap_route(pairs, sweeps, tiles, flip))]
    unnamed x7 -> x35, local copies, waits for them, and re-layouts: 1.38 us -> 3.83 us
    select_n x16 -> x0, other arithmetic: 1.49 us -> none  [the longest x8 0.81 us: layer_apply(): picked = jnp.take(tiles, column_ids, axis=1)]
  transfers between devices with their start and end apart: 8 -> 17, of which waited for: 8 -> 12; matrix products, arithmetic and copies ran while one was open for 2% -> 2% of each run, Pallas kernels for 0% -> 0%
where the time goes in v1:
time: 67.7 us; the launch traced here: 67.3 us
  waiting for transfers between devices  22.8 us (34%)
  starting transfers between devices  20.3 us (30%)
  Pallas kernels  17.2 us (25%)
  local copies, waits for them, and re-layouts  6.15 us (9%)
  other arithmetic  0.75 us (1%)
    ppermute x12, waiting for transfers between devices, exchange(): return lax.ppermute(value, AXES, swap_route(pairs, sweeps, tiles, flip))  20.9 us
    pallas_call x7, Pallas kernels, layer_apply(): pl.pallas_call(functools.partial(apply_kernel, len(recs), len(srcs), stag...  17.2 us
    ppermute x12, starting transfers between devices, exchange(): return lax.ppermute(value, AXES, swap_route(pairs, sweeps, tiles, flip))  16.7 us
    unnamed x35, local copies, waits for them, and re-layouts  3.83 us
    ppermute x5, starting transfers between devices, own_swap(): return lax.ppermute(value, 'tile', [(t, t ^ flip) for t in range(tiles)])  3.6 us
    ppermute x5, waiting for transfers between devices, own_swap(): return lax.ppermute(value, 'tile', [(t, t ^ flip) for t in range(tiles)])  1.94 us
    reshape x1, local copies, waits for them, and re-layouts, per_device(): return state[:nb].transpose(1, 0, 2).reshape(1, rhs, nb * width)  1.37 us
  transfers between devices with their start and end apart: 17, of which 12 were waited for; matrix products, arithmetic and copies ran while one was open for 2% of the time, Pallas kernels for 0%

profile of v1, /device:TPU:0, one launch (start us, length us, event | category | flops | bytes accessed | tf_op | source)
XLA Modules:
  0.0 67.3 jit_solution(17380374859821810806)
XLA Ops:
  0.0 2.4 %collective-permute-start.3 = (f32[8,8,128]{2,1,0:T(8,128)}, f32[8,8,128]{2,1,0:T(8,128)S(1)}, u32[]{:S(2)}, u32[]{:S(2)}) collective-permute-start(f32[8,8,128]{2,1,0:T(8,128)} %bitcast.26), channel_id=1, source_target_pairs={{0,3},{1,2},{2,1},{3,0},{4,7},{5,6},{6,5},{7,4},{8,11},{9,10},{10,... | collective-permute-start | bytes 98312 | tf_op jit(solution)/shard_map/ppermute | solution.py:96
  2.4 0.6 collective-permute-start.2
  3.7 0.7 %collective-permute-done = s32[8,3]{0,1:T(4,128)S(1)} collective-permute-done((s32[8,3]{0,1:T(4,128)S(1)}, s32[8,3]{0,1:T(4,128)S(1)}, u32[]{:S(2)}, u32[]{:S(2)}) %collective-permute-start) | collective-permute-done | bytes 128 | tf_op jit(solution)/shard_map/ppermute | solution.py:96
  4.7 0.7 pad_add_fusion.info
  5.4 1.2 %collective-permute-done.2.refs_2_.refs_6_.refs_4_ = f32[8,8,128]{2,1,0:T(8,128)S(1)} collective-permute-done((f32[8,8,128]{2,1,0:T(8,128)}, f32[8,8,128]{2,1,0:T(8,128)S(1)}, u32[]{:S(2)}, u32[]{:S(2)}) %collective-permute-start.2) | collective-permute-done | bytes 32800 | tf_op jit(solution)/shard_map/ppermute | solution.py:96
  6.6 0.7 broadcast_in_dim.2.refs_10_
  7.4 2.5 %apply_0.1 = (f32[16,8,128]{2,1,0:T(8,128)}, bf16[16,8,128]{2,1,0:T(8,128)(2,1)}) custom-call(s32[71]{0:T(128)} %pad_add_fusion.info, f32[8,8,128]{2,1,0:T(8,128)} %bitcast.29, f32[8,8,128]{2,1,0:T(8,128)} %copy-done.3, f32[8,8,128]{2,1,0:T(8,128)} %copy-done.2, f32[8,8,128]{2,1,0:T(8,128)} %copy-done.1, f32[8,8,128]{2,1,0:T(8,128)} %bitcast.30, ...), custom_call_target="tpu_custom_call" | custom-call | tf_op jit(solution)/shard_map/apply_0/pallas_call | solution.py:68
  9.9 1.9 %collective-permute-start.6 = (bf16[16,8,128]{2,1,0:T(8,128)(2,1)}, bf16[16,8,128]{2,1,0:T(8,128)(2,1)S(1)}, u32[]{:S(2)}, u32[]{:S(2)}) collective-permute-start(bf16[16,8,128]{2,1,0:T(8,128)(2,1)} %get-tuple-element.18), channel_id=1, source_target_pairs={{0,6},{1,7},{2,4},{3,5},{4,2},{5,3},{6,0},{7,1},{8,14},{9,15},{10,... | collective-permute-start | bytes 98312 | tf_op jit(solution)/shard_map/ppermute | solution.py:93
  12.4 2.7 %collective-permute-done.6.refs_1_ = bf16[16,8,128]{2,1,0:T(8,128)(2,1)S(1)} collective-permute-done((bf16[16,8,128]{2,1,0:T(8,128)(2,1)}, bf16[16,8,128]{2,1,0:T(8,128)(2,1)S(1)}, u32[]{:S(2)}, u32[]{:S(2)}) %collective-permute-start.6) | collective-permute-done | bytes 32800 | tf_op jit(solution)/shard_map/ppermute | solution.py:93
  15.1 0.9 %collective-permute-done.5.refs_0_ = bf16[16,8,128]{2,1,0:T(8,128)(2,1)S(1)} collective-permute-done((bf16[16,8,128]{2,1,0:T(8,128)(2,1)}, bf16[16,8,128]{2,1,0:T(8,128)(2,1)S(1)}, u32[]{:S(2)}, u32[]{:S(2)}) %collective-permute-start.5) | collective-permute-done | bytes 32800 | tf_op jit(solution)/shard_map/ppermute | solution.py:93
  16.0 0.6 copy-done.12
  16.6 2.5 %apply_1.1 = (f32[16,8,128]{2,1,0:T(8,128)}, bf16[16,8,128]{2,1,0:T(8,128)(2,1)}) custom-call(s32[71]{0:T(128)} %pad_add_fusion.info, bf16[16,8,128]{2,1,0:T(8,128)(2,1)} %copy-done.12, bf16[16,8,128]{2,1,0:T(8,128)(2,1)} %copy-done.6, f32[8,8,128]{2,1,0:T(8,128)} %bitcast.31, f32[8,8,128]{2,1,0:T(8,128)} %copy-done.3, f32[8,8,128]{2,1,0:T(8,128)} %copy-done.2, ...), custom_call_target="tpu_custom_call" | custom-call | tf_op jit(solution)/shard_map/apply_1/pallas_call | solution.py:68
  19.1 1.0 %collective-permute-start.8 = (bf16[16,8,128]{2,1,0:T(8,128)(2,1)}, bf16[16,8,128]{2,1,0:T(8,128)(2,1)S(1)}, u32[]{:S(2)}, u32[]{:S(2)}) collective-permute-start(bf16[16,8,128]{2,1,0:T(8,128)(2,1)} %get-tuple-element.20), channel_id=1, source_target_pairs={{0,2},{1,3},{2,0},{3,1},{4,10},{5,11},{6,8},{7,9},{8,6},{9,7},{10,... | collective-permute-start | bytes 98312 | tf_op jit(solution)/shard_map/ppermute | solution.py:93
  20.1 3.1 %collective-permute-done.8.refs_1_ = bf16[16,8,128]{2,1,0:T(8,128)(2,1)S(1)} collective-permute-done((bf16[16,8,128]{2,1,0:T(8,128)(2,1)}, bf16[16,8,128]{2,1,0:T(8,128)(2,1)S(1)}, u32[]{:S(2)}, u32[]{:S(2)}) %collective-permute-start.8) | collective-permute-done | bytes 32800 | tf_op jit(solution)/shard_map/ppermute | solution.py:93
  23.8 2.5 %apply_2.1 = (f32[16,8,128]{2,1,0:T(8,128)}, bf16[16,8,128]{2,1,0:T(8,128)(2,1)}) custom-call(s32[71]{0:T(128)} %pad_add_fusion.info, bf16[16,8,128]{2,1,0:T(8,128)(2,1)} %copy-done.13, bf16[16,8,128]{2,1,0:T(8,128)(2,1)} %copy-done.7, f32[8,8,128]{2,1,0:T(8,128)} %bitcast.32, f32[8,8,128]{2,1,0:T(8,128)} %copy-done.3, f32[8,8,128]{2,1,0:T(8,128)} %copy-done.2, ...), custom_call_target="tpu_custom_call" | custom-call | tf_op jit(solution)/shard_map/apply_2/pallas_call | solution.py:68
  26.3 4.8 %collective-permute-start.10 = (bf16[16,8,128]{2,1,0:T(8,128)(2,1)}, bf16[16,8,128]{2,1,0:T(8,128)(2,1)S(1)}, u32[]{:S(2)}, u32[]{:S(2)}) collective-permute-start(bf16[16,8,128]{2,1,0:T(8,128)(2,1)} %get-tuple-element.22), channel_id=1, source_target_pairs={{0,6},{1,7},{2,4},{3,5},{4,2},{5,3},{6,0},{7,1},{8,14},{9,15},{10,... | collective-permute-start | bytes 98312 | tf_op jit(solution)/shard_map/ppermute | solution.py:93
  31.2 2.1 %collective-permute-done.10.refs_1_ = bf16[16,8,128]{2,1,0:T(8,128)(2,1)S(1)} collective-permute-done((bf16[16,8,128]{2,1,0:T(8,128)(2,1)}, bf16[16,8,128]{2,1,0:T(8,128)(2,1)S(1)}, u32[]{:S(2)}, u32[]{:S(2)}) %collective-permute-start.10) | collective-permute-done | bytes 32800 | tf_op jit(solution)/shard_map/ppermute | solution.py:93
  33.3 2.0 %collective-permute-done.9.refs_0_ = bf16[16,8,128]{2,1,0:T(8,128)(2,1)S(1)} collective-permute-done((bf16[16,8,128]{2,1,0:T(8,128)(2,1)}, bf16[16,8,128]{2,1,0:T(8,128)(2,1)S(1)}, u32[]{:S(2)}, u32[]{:S(2)}) %collective-permute-start.9) | collective-permute-done | bytes 32800 | tf_op jit(solution)/shard_map/ppermute | solution.py:93
  35.9 2.5 %apply_3.1 = (f32[16,8,128]{2,1,0:T(8,128)}, bf16[16,8,128]{2,1,0:T(8,128)(2,1)}) custom-call(s32[71]{0:T(128)} %pad_add_fusion.info, bf16[16,8,128]{2,1,0:T(8,128)(2,1)} %copy-done.8, bf16[16,8,128]{2,1,0:T(8,128)(2,1)} %copy-done.4, f32[8,8,128]{2,1,0:T(8,128)} %bitcast.33, f32[8,8,128]{2,1,0:T(8,128)} %copy-done.3, f32[8,8,128]{2,1,0:T(8,128)} %copy-done.2, ...), custom_call_target="tpu_custom_call" | custom-call | tf_op jit(solution)/shard_map/apply_3/pallas_call | solution.py:68
  38.4 0.9 %collective-permute-start.12 = (bf16[16,8,128]{2,1,0:T(8,128)(2,1)}, bf16[16,8,128]{2,1,0:T(8,128)(2,1)S(1)}, u32[]{:S(2)}, u32[]{:S(2)}) collective-permute-start(bf16[16,8,128]{2,1,0:T(8,128)(2,1)} %get-tuple-element.24), channel_id=1, source_target_pairs={{0,6},{1,7},{2,4},{3,5},{4,2},{5,3},{6,0},{7,1},{8,14},{9,15},{10,... | collective-permute-start | bytes 98312 | tf_op jit(solution)/shard_map/ppermute | solution.py:93
  39.3 1.6 %collective-permute-start.11 = (bf16[16,8,128]{2,1,0:T(8,128)(2,1)}, bf16[16,8,128]{2,1,0:T(8,128)(2,1)S(1)}, u32[]{:S(2)}, u32[]{:S(2)}) collective-permute-start(bf16[16,8,128]{2,1,0:T(8,128)(2,1)} %get-tuple-element.24), channel_id=1, source_target_pairs={{0,4},{1,5},{2,6},{3,7},{4,0},{5,1},{6,2},{7,3},{8,12},{9,13},{10,... | collective-permute-start | bytes 98312 | tf_op jit(solution)/shard_map/ppermute | solution.py:93
  40.9 2.6 %collective-permute-done.12.refs_1_ = bf16[16,8,128]{2,1,0:T(8,128)(2,1)S(1)} collective-permute-done((bf16[16,8,128]{2,1,0:T(8,128)(2,1)}, bf16[16,8,128]{2,1,0:T(8,128)(2,1)S(1)}, u32[]{:S(2)}, u32[]{:S(2)}) %collective-permute-start.12) | collective-permute-done | bytes 32800 | tf_op jit(solution)/shard_map/ppermute | solution.py:93
  44.4 2.4 %apply_4.1 = (f32[16,8,128]{2,1,0:T(8,128)}, bf16[16,8,128]{2,1,0:T(8,128)(2,1)}) custom-call(s32[71]{0:T(128)} %pad_add_fusion.info, bf16[16,8,128]{2,1,0:T(8,128)(2,1)} %copy-done.14, bf16[16,8,128]{2,1,0:T(8,128)(2,1)} %copy-done.9, bf16[8,4,64,128]{3,2,1,0:T(8,128)(2,1)} %bitcast.23, bf16[8,4,64,128]{3,2,1,0:T(8,128)(2,1)} %copy-done, ...), custom_call_target="tpu_custom_call" | custom-call | tf_op jit(solution)/shard_map/apply_4/pallas_call | solution.py:68
  46.8 1.0 %collective-permute-start.14 = (bf16[16,8,128]{2,1,0:T(8,128)(2,1)}, bf16[16,8,128]{2,1,0:T(8,128)(2,1)S(1)}, u32[]{:S(2)}, u32[]{:S(2)}) collective-permute-start(bf16[16,8,128]{2,1,0:T(8,128)(2,1)} %get-tuple-element.26), channel_id=1, source_target_pairs={{0,2},{1,3},{2,0},{3,1},{4,10},{5,11},{6,8},{7,9},{8,6},{9,7},{10,... | collective-permute-start | bytes 98312 | tf_op jit(solution)/shard_map/ppermute | solution.py:93
  47.8 3.1 %collective-permute-done.14.refs_1_ = bf16[16,8,128]{2,1,0:T(8,128)(2,1)S(1)} collective-permute-done((bf16[16,8,128]{2,1,0:T(8,128)(2,1)}, bf16[16,8,128]{2,1,0:T(8,128)(2,1)S(1)}, u32[]{:S(2)}, u32[]{:S(2)}) %collective-permute-start.14) | collective-permute-done | bytes 32800 | tf_op jit(solution)/shard_map/ppermute | solution.py:93
  51.5 2.4 %apply_5.1 = (f32[16,8,128]{2,1,0:T(8,128)}, bf16[16,8,128]{2,1,0:T(8,128)(2,1)}) custom-call(s32[71]{0:T(128)} %pad_add_fusion.info, bf16[16,8,128]{2,1,0:T(8,128)(2,1)} %copy-done.15, bf16[16,8,128]{2,1,0:T(8,128)(2,1)} %copy-done.10, bf16[8,4,64,128]{3,2,1,0:T(8,128)(2,1)} %bitcast.24, bf16[8,4,64,128]{3,2,1,0:T(8,128)(2,1)} %copy-done, ...), custom_call_target="tpu_custom_call" | custom-call | tf_op jit(solution)/shard_map/apply_5/pallas_call | solution.py:68
  54.0 4.8 %collective-permute-start.16 = (bf16[16,8,128]{2,1,0:T(8,128)(2,1)}, bf16[16,8,128]{2,1,0:T(8,128)(2,1)S(1)}, u32[]{:S(2)}, u32[]{:S(2)}) collective-permute-start(bf16[16,8,128]{2,1,0:T(8,128)(2,1)} %get-tuple-element.28), channel_id=1, source_target_pairs={{0,6},{1,7},{2,4},{3,5},{4,2},{5,3},{6,0},{7,1},{8,14},{9,15},{10,... | collective-permute-start | bytes 98312 | tf_op jit(solution)/shard_map/ppermute | solution.py:93
  58.8 2.1 %collective-permute-done.16.refs_1_ = bf16[16,8,128]{2,1,0:T(8,128)(2,1)S(1)} collective-permute-done((bf16[16,8,128]{2,1,0:T(8,128)(2,1)}, bf16[16,8,128]{2,1,0:T(8,128)(2,1)S(1)}, u32[]{:S(2)}, u32[]{:S(2)}) %collective-permute-start.16) | collective-permute-done | bytes 32800 | tf_op jit(solution)/shard_map/ppermute | solution.py:93
  60.9 2.0 %collective-permute-done.15.refs_0_ = bf16[16,8,128]{2,1,0:T(8,128)(2,1)S(1)} collective-permute-done((bf16[16,8,128]{2,1,0:T(8,128)(2,1)}, bf16[16,8,128]{2,1,0:T(8,128)(2,1)S(1)}, u32[]{:S(2)}, u32[]{:S(2)}) %collective-permute-start.15) | collective-permute-done | bytes 32800 | tf_op jit(solution)/shard_map/ppermute | solution.py:93
  62.9 0.6 copy-done.11
  63.5 2.4 %apply_6.1 = (f32[16,8,128]{2,1,0:T(8,128)}, bf16[16,8,128]{2,1,0:T(8,128)(2,1)}) custom-call(s32[71]{0:T(128)} %pad_add_fusion.info, bf16[16,8,128]{2,1,0:T(8,128)(2,1)} %copy-done.11, bf16[16,8,128]{2,1,0:T(8,128)(2,1)} %copy-done.5, bf16[8,4,64,128]{3,2,1,0:T(8,128)(2,1)} %bitcast.25, bf16[8,4,64,128]{3,2,1,0:T(8,128)(2,1)} %copy-done, ...), custom_call_target="tpu_custom_call" | custom-call | tf_op jit(solution)/shard_map/apply_6/pallas_call | solution.py:68
  65.9 1.4 %slice_bitcast_fusion = f32[1,8,1024]{2,1,0:T(8,128)} fusion(f32[16,8,128]{2,1,0:T(8,128)} %get-tuple-element.30), kind=kLoop, calls=%fused_computation | loop fusion | bytes 65536 | tf_op jit(solution)/shard_map/reshape | solution.py:128
  (54 shorter events, 4.4 us)
Async XLA Ops:
  0.0 3.1 %copy-start.16 = (s32[1,8,3]{1,0,2:T(1,128)S(1)}, s32[1,8,3]{1,0,2:T(1,128)}, u32[]{:S(2)}) copy-start(s32[1,8,3]{1,0,2:T(1,128)} %param.5) | copy-start | bytes 292
  0.0 5.4 %collective-permute-start.3 = (f32[8,8,128]{2,1,0:T(8,128)}, f32[8,8,128]{2,1,0:T(8,128)S(1)}, u32[]{:S(2)}, u32[]{:S(2)}) collective-permute-start(f32[8,8,128]{2,1,0:T(8,128)} %bitcast.26), channel_id=1, source_target_pairs={{0,3},{1,2},{2,1},{3,0},{4,7},{5,6},{6,5},{7,4},{8,11},{9,10},{10,... | collective-permute-start | bytes 98312 | tf_op jit(solution)/shard_map/ppermute | solution.py:96
  2.4 4.2 %collective-permute-start.2 = (f32[8,8,128]{2,1,0:T(8,128)}, f32[8,8,128]{2,1,0:T(8,128)S(1)}, u32[]{:S(2)}, u32[]{:S(2)}) collective-permute-start(f32[8,8,128]{2,1,0:T(8,128)} %bitcast.27), channel_id=1, source_target_pairs={{0,2},{1,3},{2,0},{3,1},{4,6},{5,7},{6,4},{7,5},{8,10},{9,11},{10,... | collective-permute-start | bytes 98312 | tf_op jit(solution)/shard_map/ppermute | solution.py:96
  3.0 3.6 %collective-permute-start.1 = (f32[8,8,128]{2,1,0:T(8,128)}, f32[8,8,128]{2,1,0:T(8,128)S(1)}, u32[]{:S(2)}, u32[]{:S(2)}) collective-permute-start(f32[8,8,128]{2,1,0:T(8,128)} %bitcast.28), channel_id=1, source_target_pairs={{0,1},{1,0},{2,3},{3,2},{4,5},{5,4},{6,7},{7,6},{8,9},{9,8},{10,11... | collective-permute-start | bytes 98312 | tf_op jit(solution)/shard_map/ppermute | solution.py:96
  3.1 1.4 %collective-permute-start = (s32[8,3]{0,1:T(4,128)S(1)}, s32[8,3]{0,1:T(4,128)S(1)}, u32[]{:S(2)}, u32[]{:S(2)}) collective-permute-start(s32[8,3]{0,1:T(4,128)S(1)} %bitcast.34), channel_id=1, source_target_pairs={{0,1},{1,0},{2,3},{3,2},{4,5},{5,4},{6,7},{7,6},{8,9},{9,8},{10,11... | collective-permute-start | bytes 296 | tf_op jit(solution)/shard_map/ppermute | solution.py:96
  3.5 3.1 %collective-permute-start.4 = (bf16[8,4,64,128]{3,2,1,0:T(8,128)(2,1)}, bf16[8,4,64,128]{3,2,1,0:T(8,128)(2,1)S(1)}, u32[]{:S(2)}, u32[]{:S(2)}) collective-permute-start(bf16[8,4,64,128]{3,2,1,0:T(8,128)(2,1)} %bitcast.18), channel_id=1, source_target_pairs={{0,1},{1,0},{2,3},{3,2},{4,5},{5,4},{6,7},{7,6},{8,9},{9,8},{10,11... | collective-permute-start | bytes 1572872 | tf_op jit(solution)/shard_map/ppermute | solution.py:96
  5.4 1.9 %copy-start.1 = (f32[8,8,128]{2,1,0:T(8,128)}, f32[8,8,128]{2,1,0:T(8,128)S(1)}, u32[]{:S(2)}) copy-start(f32[8,8,128]{2,1,0:T(8,128)S(1)} %collective-permute-done.3.refs_3_.refs_7_.refs_5_) | copy-start | bytes 98308
  6.6 0.7 %copy-start.2 = (f32[8,8,128]{2,1,0:T(8,128)}, f32[8,8,128]{2,1,0:T(8,128)S(1)}, u32[]{:S(2)}) copy-start(f32[8,8,128]{2,1,0:T(8,128)S(1)} %collective-permute-done.2.refs_2_.refs_6_.refs_4_) | copy-start | bytes 98308
  6.6 0.7 %copy-start.3 = (f32[8,8,128]{2,1,0:T(8,128)}, f32[8,8,128]{2,1,0:T(8,128)S(1)}, u32[]{:S(2)}) copy-start(f32[8,8,128]{2,1,0:T(8,128)S(1)} %collective-permute-done.1.refs_1_.refs_5_.refs_3_) | copy-start | bytes 98308
  6.6 0.8 %copy-start = (bf16[8,4,64,128]{3,2,1,0:T(8,128)(2,1)}, bf16[8,4,64,128]{3,2,1,0:T(8,128)(2,1)S(1)}, u32[]{:S(2)}) copy-start(bf16[8,4,64,128]{3,2,1,0:T(8,128)(2,1)S(1)} %collective-permute-done.4.refs_9_.refs_7_.refs_3_) | copy-start | bytes 1572868
  9.9 5.1 %collective-permute-start.6 = (bf16[16,8,128]{2,1,0:T(8,128)(2,1)}, bf16[16,8,128]{2,1,0:T(8,128)(2,1)S(1)}, u32[]{:S(2)}, u32[]{:S(2)}) collective-permute-start(bf16[16,8,128]{2,1,0:T(8,128)(2,1)} %get-tuple-element.18), channel_id=1, source_target_pairs={{0,6},{1,7},{2,4},{3,5},{4,2},{5,3},{6,0},{7,1},{8,14},{9,15},{10,... | collective-permute-start | bytes 98312 | tf_op jit(solution)/shard_map/ppermute | solution.py:93
  11.9 4.1 %collective-permute-start.5 = (bf16[16,8,128]{2,1,0:T(8,128)(2,1)}, bf16[16,8,128]{2,1,0:T(8,128)(2,1)S(1)}, u32[]{:S(2)}, u32[]{:S(2)}) collective-permute-start(bf16[16,8,128]{2,1,0:T(8,128)(2,1)} %get-tuple-element.18), channel_id=1, source_target_pairs={{0,4},{1,5},{2,6},{3,7},{4,0},{5,1},{6,2},{7,3},{8,12},{9,13},{10,... | collective-permute-start | bytes 98312 | tf_op jit(solution)/shard_map/ppermute | solution.py:93
  15.1 0.9 %copy-start.6 = (bf16[16,8,128]{2,1,0:T(8,128)(2,1)}, bf16[16,8,128]{2,1,0:T(8,128)(2,1)S(1)}, u32[]{:S(2)}) copy-start(bf16[16,8,128]{2,1,0:T(8,128)(2,1)S(1)} %collective-permute-done.6.refs_1_) | copy-start | bytes 98308
  16.0 0.6 copy-start.12
  19.1 4.1 %collective-permute-start.8 = (bf16[16,8,128]{2,1,0:T(8,128)(2,1)}, bf16[16,8,128]{2,1,0:T(8,128)(2,1)S(1)}, u32[]{:S(2)}, u32[]{:S(2)}) collective-permute-start(bf16[16,8,128]{2,1,0:T(8,128)(2,1)} %get-tuple-element.20), channel_id=1, source_target_pairs={{0,2},{1,3},{2,0},{3,1},{4,10},{5,11},{6,8},{7,9},{8,6},{9,7},{10,... | collective-permute-start | bytes 98312 | tf_op jit(solution)/shard_map/ppermute | solution.py:93
  20.1 3.1 %collective-permute-start.7 = (bf16[16,8,128]{2,1,0:T(8,128)(2,1)}, bf16[16,8,128]{2,1,0:T(8,128)(2,1)S(1)}, u32[]{:S(2)}, u32[]{:S(2)}) collective-permute-start(bf16[16,8,128]{2,1,0:T(8,128)(2,1)} %get-tuple-element.20), channel_id=1, source_target_pairs={{0,1},{1,0},{2,3},{3,2},{4,8},{5,9},{6,10},{7,11},{8,4},{9,5},{10,... | collective-permute-start | bytes 98312 | tf_op jit(solution)/shard_map/ppermute | solution.py:93
  23.2 0.6 copy-start.13
  26.3 6.9 %collective-permute-start.10 = (bf16[16,8,128]{2,1,0:T(8,128)(2,1)}, bf16[16,8,128]{2,1,0:T(8,128)(2,1)S(1)}, u32[]{:S(2)}, u32[]{:S(2)}) collective-permute-start(bf16[16,8,128]{2,1,0:T(8,128)(2,1)} %get-tuple-element.22), channel_id=1, source_target_pairs={{0,6},{1,7},{2,4},{3,5},{4,2},{5,3},{6,0},{7,1},{8,14},{9,15},{10,... | collective-permute-start | bytes 98312 | tf_op jit(solution)/shard_map/ppermute | solution.py:93
  31.2 4.1 %collective-permute-start.9 = (bf16[16,8,128]{2,1,0:T(8,128)(2,1)}, bf16[16,8,128]{2,1,0:T(8,128)(2,1)S(1)}, u32[]{:S(2)}, u32[]{:S(2)}) collective-permute-start(bf16[16,8,128]{2,1,0:T(8,128)(2,1)} %get-tuple-element.22), channel_id=1, source_target_pairs={{0,4},{1,5},{2,6},{3,7},{4,0},{5,1},{6,2},{7,3},{8,12},{9,13},{10,... | collective-permute-start | bytes 98312 | tf_op jit(solution)/shard_map/ppermute | solution.py:93
  33.3 2.0 %copy-start.4 = (bf16[16,8,128]{2,1,0:T(8,128)(2,1)}, bf16[16,8,128]{2,1,0:T(8,128)(2,1)S(1)}, u32[]{:S(2)}) copy-start(bf16[16,8,128]{2,1,0:T(8,128)(2,1)S(1)} %collective-permute-done.10.refs_1_) | copy-start | bytes 98308
  35.3 0.6 copy-start.8
  38.4 5.1 %collective-permute-start.12 = (bf16[16,8,128]{2,1,0:T(8,128)(2,1)}, bf16[16,8,128]{2,1,0:T(8,128)(2,1)S(1)}, u32[]{:S(2)}, u32[]{:S(2)}) collective-permute-start(bf16[16,8,128]{2,1,0:T(8,128)(2,1)} %get-tuple-element.24), channel_id=1, source_target_pairs={{0,6},{1,7},{2,4},{3,5},{4,2},{5,3},{6,0},{7,1},{8,14},{9,15},{10,... | collective-permute-start | bytes 98312 | tf_op jit(solution)/shard_map/ppermute | solution.py:93
  39.3 4.5 %collective-permute-start.11 = (bf16[16,8,128]{2,1,0:T(8,128)(2,1)}, bf16[16,8,128]{2,1,0:T(8,128)(2,1)S(1)}, u32[]{:S(2)}, u32[]{:S(2)}) collective-permute-start(bf16[16,8,128]{2,1,0:T(8,128)(2,1)} %get-tuple-element.24), channel_id=1, source_target_pairs={{0,4},{1,5},{2,6},{3,7},{4,0},{5,1},{6,2},{7,3},{8,12},{9,13},{10,... | collective-permute-start | bytes 98312 | tf_op jit(solution)/shard_map/ppermute | solution.py:93
  43.8 0.6 copy-start.14
  46.8 4.1 %collective-permute-start.14 = (bf16[16,8,128]{2,1,0:T(8,128)(2,1)}, bf16[16,8,128]{2,1,0:T(8,128)(2,1)S(1)}, u32[]{:S(2)}, u32[]{:S(2)}) collective-permute-start(bf16[16,8,128]{2,1,0:T(8,128)(2,1)} %get-tuple-element.26), channel_id=1, source_target_pairs={{0,2},{1,3},{2,0},{3,1},{4,10},{5,11},{6,8},{7,9},{8,6},{9,7},{10,... | collective-permute-start | bytes 98312 | tf_op jit(solution)/shard_map/ppermute | solution.py:93
  47.8 3.1 %collective-permute-start.13 = (bf16[16,8,128]{2,1,0:T(8,128)(2,1)}, bf16[16,8,128]{2,1,0:T(8,128)(2,1)S(1)}, u32[]{:S(2)}, u32[]{:S(2)}) collective-permute-start(bf16[16,8,128]{2,1,0:T(8,128)(2,1)} %get-tuple-element.26), channel_id=1, source_target_pairs={{0,1},{1,0},{2,3},{3,2},{4,8},{5,9},{6,10},{7,11},{8,4},{9,5},{10,... | collective-permute-start | bytes 98312 | tf_op jit(solution)/shard_map/ppermute | solution.py:93
  50.9 0.6 copy-start.10
  50.9 0.6 copy-start.15
  54.0 6.9 %collective-permute-start.16 = (bf16[16,8,128]{2,1,0:T(8,128)(2,1)}, bf16[16,8,128]{2,1,0:T(8,128)(2,1)S(1)}, u32[]{:S(2)}, u32[]{:S(2)}) collective-permute-start(bf16[16,8,128]{2,1,0:T(8,128)(2,1)} %get-tuple-element.28), channel_id=1, source_target_pairs={{0,6},{1,7},{2,4},{3,5},{4,2},{5,3},{6,0},{7,1},{8,14},{9,15},{10,... | collective-permute-start | bytes 98312 | tf_op jit(solution)/shard_map/ppermute | solution.py:93
  58.8 4.1 %collective-permute-start.15 = (bf16[16,8,128]{2,1,0:T(8,128)(2,1)}, bf16[16,8,128]{2,1,0:T(8,128)(2,1)S(1)}, u32[]{:S(2)}, u32[]{:S(2)}) collective-permute-start(bf16[16,8,128]{2,1,0:T(8,128)(2,1)} %get-tuple-element.28), channel_id=1, source_target_pairs={{0,4},{1,5},{2,6},{3,7},{4,0},{5,1},{6,2},{7,3},{8,12},{9,13},{10,... | collective-permute-start | bytes 98312 | tf_op jit(solution)/shard_map/ppermute | solution.py:93
  60.9 2.0 %copy-start.5 = (bf16[16,8,128]{2,1,0:T(8,128)(2,1)}, bf16[16,8,128]{2,1,0:T(8,128)(2,1)S(1)}, u32[]{:S(2)}) copy-start(bf16[16,8,128]{2,1,0:T(8,128)(2,1)S(1)} %collective-permute-done.16.refs_1_) | copy-start | bytes 98308
  62.9 0.6 copy-start.11
  (2 other events, 1.2 us)

commit v2 on v1

--- a/solution.py
+++ b/solution.py
@@ -24,7 +24,7 @@
     recs, refs = refs[:pieces], refs[pieces:]
     if with_src:
         srcs, refs = refs[: with_src], refs[with_src:]
-    own_blocks, pair_blocks, state_in, state_out, msg_out, vec = refs
+    own_blocks, pair_blocks, state_in, state_out, *msg_out, vec = refs
     nb = own_blocks.shape[0]
     width = own_blocks.shape[-1]
     half = width // 2
@@ -42,8 +42,8 @@
         imag_in = pltpu.roll(value, half, axis=2)
         vec[pl.ds(at, count)] = jnp.concatenate([real_in, imag_in], axis=1).astype(jnp.bfloat16)
         at += count
-    rows = 2 * nb
-    active = info[rows * 4 + stage] != 0
+    rows = 2 * nb if msg_out else nb
+    active = info[8 * nb + stage] != 0
     for row in range(rows):
         source = own_blocks if row < nb else pair_blocks
         mats = jnp.concatenate([source[row % nb, j] for j in range(4)], axis=1)
@@ -54,9 +54,12 @@
         rhs = out.shape[0] // 2
         result = jnp.concatenate([out[:rhs], out[rhs:]], axis=1)
         state = jnp.where(active, state_in[row] + result, state_in[row])
+        if not msg_out:
+            state_out[:, row * width : (row + 1) * width] = state
+            continue
         state_out[row] = state
         msg = result if stage < SEG - 1 else state
-        msg_out[row] = msg.astype(jnp.bfloat16)
+        msg_out[0][row] = msg.astype(jnp.bfloat16)
 
 
 def layer_apply(stage, info, recs, srcs, own_blocks, pair_blocks, state):
@@ -65,15 +68,19 @@
     rhs, width = recs[0].shape[1:]
     vmem = pl.BlockSpec(memory_space=pltpu.VMEM)
     args = [*recs, *srcs, own_blocks, pair_blocks, state]
+    out_shape = [
+        jax.ShapeDtypeStruct((2 * nb, rhs, width), jnp.float32),
+        jax.ShapeDtypeStruct((2 * nb, rhs, width), jnp.bfloat16),
+    ]
+    if stage == 2 * SEG - 2:
+        out_shape = [jax.ShapeDtypeStruct((rhs, nb * width), jnp.float32)]
     return pl.pallas_call(
         functools.partial(apply_kernel, len(recs), len(srcs), stage),
         in_specs=[pl.BlockSpec(memory_space=pltpu.SMEM)] + [vmem] * len(args),
-        out_specs=[vmem, vmem],
-        out_shape=[
-            jax.ShapeDtypeStruct((2 * nb, rhs, width), jnp.float32),
-            jax.ShapeDtypeStruct((2 * nb, rhs, width), jnp.bfloat16),
-        ],
+        out_specs=[vmem] * len(out_shape),
+        out_shape=out_shape,
         scratch_shapes=[pltpu.VMEM((total, 2 * rhs, width), jnp.bfloat16)],
+        compiler_params=pltpu.CompilerParams(vmem_limit_bytes=8 * 1024 * 1024),
         name=f"apply_{stage}",
     )(info, *args)
 
@@ -87,7 +94,6 @@
 
     flat = {layer: layer ^ 1 for layer in range(sweeps)}
     odd = {layer: ((layer + 1) ^ 1) - 1 for layer in range(1, sweeps - 1)}
-    same = {}
 
     def exchange(value, pairs, flip):
         return lax.ppermute(value, AXES, swap_route(pairs, sweeps, tiles, flip))
@@ -120,12 +126,12 @@
     stage_pairs = [flat, odd, flat, flat, odd, flat]
     recs = srcs
     for stage in range(2 * SEG - 1):
-        state, msg = layer_apply(
+        state, *msg = layer_apply(
             stage, info, recs, srcs if stage < SEG else [], own_blocks, pair_blocks, state
         )
-        if stage < 2 * SEG - 2:
-            recs = [exchange(msg, stage_pairs[stage], flip) for flip in range(0, tiles, 2)]
-    return state[:nb].transpose(1, 0, 2).reshape(1, rhs, nb * width)
+        if msg:
+            recs = [exchange(msg[0], stage_pairs[stage], flip) for flip in range(0, tiles, 2)]
+    return state[None]
 
 
 def solution(mesh):

time: 67.7 us -> 52.3 us (0.77)
  Pallas kernels: 17.2 us -> 7.75 us
  local copies, waits for them, and re-layouts: 6.15 us -> 1.33 us
    pallas_call x7, Pallas kernels: 17.2 us -> 7.75 us  [layer_apply(): pl.pallas_call(functools.partial(apply_kernel, len(recs), len(srcs), stag...]
    unnamed x35 -> x9, local copies, waits for them, and re-layouts: 3.83 us -> 1.05 us
    reshape x1 -> x0, local copies, waits for them, and re-layouts: 1.37 us -> none  [per_device(): return state[:nb].transpose(1, 0, 2).reshape(1, rhs, nb * width)]
    ppermute x12, waiting for transfers between devices: 20.9 us -> 19.6 us  [exchange(): return lax.ppermute(value, AXES, swap_route(pairs, sweeps, tiles, flip))]
  transfers between devices with their start and end apart: 17 -> 17, of which waited for: 12 -> 12; matrix products, arithmetic and copies ran while one was open for 2% -> 1% of each run, Pallas kernels for 0% -> 0%
where the time goes in v2:
time: 52.3 us; the launch traced here: 52.2 us
  waiting for transfers between devices  22.2 us (42%)
  starting transfers between devices  20.7 us (40%)
  Pallas kernels  7.75 us (15%)
  local copies, waits for them, and re-layouts  1.33 us (3%)
    ppermute x12, waiting for transfers between devices, exchange(): return lax.ppermute(value, AXES, swap_route(pairs, sweeps, tiles, flip))  19.6 us
    ppermute x12, starting transfers between devices, exchange(): return lax.ppermute(value, AXES, swap_route(pairs, sweeps, tiles, flip))  17.1 us
    pallas_call x7, Pallas kernels, layer_apply(): pl.pallas_call(functools.partial(apply_kernel, len(recs), len(srcs), stag...  7.75 us
    ppermute x5, starting transfers between devices, own_swap(): return lax.ppermute(value, 'tile', [(t, t ^ flip) for t in range(tiles)])  3.6 us
    ppermute x5, waiting for transfers between devices, own_swap(): return lax.ppermute(value, 'tile', [(t, t ^ flip) for t in range(tiles)])  2.52 us
    unnamed x9, local copies, waits for them, and re-layouts  1.05 us
  transfers between devices with their start and end apart: 17, of which 12 were waited for; matrix products, arithmetic and copies ran while one was open for 1% of the time, Pallas kernels for 0%

profile of v2, /device:TPU:0, one launch (start us, length us, event | category | flops | bytes accessed | tf_op | source)
XLA Modules:
  0.0 52.2 jit_solution(2098247692314491389)
XLA Ops:
  0.0 2.4 %collective-permute-start.3 = (f32[8,8,128]{2,1,0:T(8,128)}, f32[8,8,128]{2,1,0:T(8,128)S(1)}, u32[]{:S(2)}, u32[]{:S(2)}) collective-permute-start(f32[8,8,128]{2,1,0:T(8,128)} %bitcast.23), channel_id=1, source_target_pairs={{0,3},{1,2},{2,1},{3,0},{4,7},{5,6},{6,5},{7,4},{8,11},{9,10},{10,... | collective-permute-start | bytes 98312 | tf_op jit(solution)/shard_map/ppermute | solution.py:102
  2.4 0.6 %collective-permute-start.2 = (f32[8,8,128]{2,1,0:T(8,128)}, f32[8,8,128]{2,1,0:T(8,128)S(1)}, u32[]{:S(2)}, u32[]{:S(2)}) collective-permute-start(f32[8,8,128]{2,1,0:T(8,128)} %bitcast.24), channel_id=1, source_target_pairs={{0,2},{1,3},{2,0},{3,1},{4,6},{5,7},{6,4},{7,5},{8,10},{9,11},{10,... | collective-permute-start | bytes 98312 | tf_op jit(solution)/shard_map/ppermute | solution.py:102
  3.1 0.5 collective-permute-start
  3.6 0.1 stack.31
  3.7 0.7 %collective-permute-done = s32[8,3]{0,1:T(4,128)S(1)} collective-permute-done((s32[8,3]{0,1:T(4,128)S(1)}, s32[8,3]{0,1:T(4,128)S(1)}, u32[]{:S(2)}, u32[]{:S(2)}) %collective-permute-start) | collective-permute-done | bytes 128 | tf_op jit(solution)/shard_map/ppermute | solution.py:102
  4.8 1.8 %collective-permute-done.2.refs_2_.refs_6_.refs_4_ = f32[8,8,128]{2,1,0:T(8,128)S(1)} collective-permute-done((f32[8,8,128]{2,1,0:T(8,128)}, f32[8,8,128]{2,1,0:T(8,128)S(1)}, u32[]{:S(2)}, u32[]{:S(2)}) %collective-permute-start.2) | collective-permute-done | bytes 32800 | tf_op jit(solution)/shard_map/ppermute | solution.py:102
  6.6 1.0 %copy-done = bf16[1,8,4,64,128]{4,3,2,1,0:T(8,128)(2,1)S(1)} copy-done((bf16[1,8,4,64,128]{4,3,2,1,0:T(8,128)(2,1)S(1)}, bf16[1,8,4,64,128]{4,3,2,1,0:T(8,128)(2,1)}, u32[]{:S(2)}) %copy-start) | copy-done | bytes 524312
  7.7 1.0 %apply_0.1 = (f32[16,8,128]{2,1,0:T(8,128)S(1)}, bf16[16,8,128]{2,1,0:T(8,128)(2,1)S(1)}) custom-call(s32[71]{0:T(128)S(1)} %pad_add_fusion.info, f32[8,8,128]{2,1,0:T(8,128)S(1)} %bitcast.26, f32[8,8,128]{2,1,0:T(8,128)S(1)} %collective-permute-done.1.refs_1_.refs_5_.refs_3_, f32[8,8,128]{2,1,0:T(8,128)S(1)} %collective-permute-done.2.refs_2_.refs_6_.refs_4_, ...), custom_call_target="tpu_custom_call" | custom-call | tf_op jit(solution)/shard_map/apply_0/pallas_call | solution.py:77
  8.7 2.0 %collective-permute-start.6 = (bf16[16,8,128]{2,1,0:T(8,128)(2,1)S(1)}, bf16[16,8,128]{2,1,0:T(8,128)(2,1)S(1)}, u32[]{:S(2)}, u32[]{:S(2)}) collective-permute-start(bf16[16,8,128]{2,1,0:T(8,128)(2,1)S(1)} %get-tuple-element.17), channel_id=1, source_target_pairs={{0,6},{1,7},{2,4},{3,5},{4,2},{5,3},{6,0},{7,1},{8,14},{9,15},{10,... | collective-permute-start | bytes 98312 | tf_op jit(solution)/shard_map/ppermute | solution.py:99
  10.7 0.5 collective-permute-start.5
  11.2 2.5 %collective-permute-done.6.refs_1_ = bf16[16,8,128]{2,1,0:T(8,128)(2,1)S(1)} collective-permute-done((bf16[16,8,128]{2,1,0:T(8,128)(2,1)S(1)}, bf16[16,8,128]{2,1,0:T(8,128)(2,1)S(1)}, u32[]{:S(2)}, u32[]{:S(2)}) %collective-permute-start.6) | collective-permute-done | bytes 32800 | tf_op jit(solution)/shard_map/ppermute | solution.py:99
  13.7 0.9 %collective-permute-done.5.refs_0_ = bf16[16,8,128]{2,1,0:T(8,128)(2,1)S(1)} collective-permute-done((bf16[16,8,128]{2,1,0:T(8,128)(2,1)S(1)}, bf16[16,8,128]{2,1,0:T(8,128)(2,1)S(1)}, u32[]{:S(2)}, u32[]{:S(2)}) %collective-permute-start.5) | collective-permute-done | bytes 32800 | tf_op jit(solution)/shard_map/ppermute | solution.py:99
  14.6 1.0 %apply_1.1 = (f32[16,8,128]{2,1,0:T(8,128)S(1)}, bf16[16,8,128]{2,1,0:T(8,128)(2,1)S(1)}) custom-call(s32[71]{0:T(128)S(1)} %pad_add_fusion.info, bf16[16,8,128]{2,1,0:T(8,128)(2,1)S(1)} %collective-permute-done.5.refs_0_, bf16[16,8,128]{2,1,0:T(8,128)(2,1)S(1)} %collective-permute-done.6.refs_1_, f32[8,8,128]{2,1,0:T(8,128)S(1)} %bitcast.28, ...), custom_call_target="tpu_custom_call" | custom-call | tf_op jit(solution)/shard_map/apply_1/pallas_call | solution.py:77
  15.6 1.1 %collective-permute-start.8 = (bf16[16,8,128]{2,1,0:T(8,128)(2,1)S(1)}, bf16[16,8,128]{2,1,0:T(8,128)(2,1)S(1)}, u32[]{:S(2)}, u32[]{:S(2)}) collective-permute-start(bf16[16,8,128]{2,1,0:T(8,128)(2,1)S(1)} %get-tuple-element.19), channel_id=1, source_target_pairs={{0,2},{1,3},{2,0},{3,1},{4,10},{5,11},{6,8},{7,9},{8,6},{9,7},{10,... | collective-permute-start | bytes 98312 | tf_op jit(solution)/shard_map/ppermute | solution.py:99
  16.7 2.9 %collective-permute-done.8.refs_1_ = bf16[16,8,128]{2,1,0:T(8,128)(2,1)S(1)} collective-permute-done((bf16[16,8,128]{2,1,0:T(8,128)(2,1)S(1)}, bf16[16,8,128]{2,1,0:T(8,128)(2,1)S(1)}, u32[]{:S(2)}, u32[]{:S(2)}) %collective-permute-start.8) | collective-permute-done | bytes 32800 | tf_op jit(solution)/shard_map/ppermute | solution.py:99
  19.6 1.0 %apply_2.1 = (f32[16,8,128]{2,1,0:T(8,128)S(1)}, bf16[16,8,128]{2,1,0:T(8,128)(2,1)S(1)}) custom-call(s32[71]{0:T(128)S(1)} %pad_add_fusion.info, bf16[16,8,128]{2,1,0:T(8,128)(2,1)S(1)} %collective-permute-done.7.refs_0_, bf16[16,8,128]{2,1,0:T(8,128)(2,1)S(1)} %collective-permute-done.8.refs_1_, f32[8,8,128]{2,1,0:T(8,128)S(1)} %bitcast.29, ...), custom_call_target="tpu_custom_call" | custom-call | tf_op jit(solution)/shard_map/apply_2/pallas_call | solution.py:77
  20.6 4.9 %collective-permute-start.10 = (bf16[16,8,128]{2,1,0:T(8,128)(2,1)S(1)}, bf16[16,8,128]{2,1,0:T(8,128)(2,1)S(1)}, u32[]{:S(2)}, u32[]{:S(2)}) collective-permute-start(bf16[16,8,128]{2,1,0:T(8,128)(2,1)S(1)} %get-tuple-element.21), channel_id=1, source_target_pairs={{0,6},{1,7},{2,4},{3,5},{4,2},{5,3},{6,0},{7,1},{8,14},{9,15},{10,... | collective-permute-start | bytes 98312 | tf_op jit(solution)/shard_map/ppermute | solution.py:99
  25.5 1.9 %collective-permute-done.10.refs_1_ = bf16[16,8,128]{2,1,0:T(8,128)(2,1)S(1)} collective-permute-done((bf16[16,8,128]{2,1,0:T(8,128)(2,1)S(1)}, bf16[16,8,128]{2,1,0:T(8,128)(2,1)S(1)}, u32[]{:S(2)}, u32[]{:S(2)}) %collective-permute-start.10) | collective-permute-done | bytes 32800 | tf_op jit(solution)/shard_map/ppermute | solution.py:99
  27.4 2.0 %collective-permute-done.9.refs_0_ = bf16[16,8,128]{2,1,0:T(8,128)(2,1)S(1)} collective-permute-done((bf16[16,8,128]{2,1,0:T(8,128)(2,1)S(1)}, bf16[16,8,128]{2,1,0:T(8,128)(2,1)S(1)}, u32[]{:S(2)}, u32[]{:S(2)}) %collective-permute-start.9) | collective-permute-done | bytes 32800 | tf_op jit(solution)/shard_map/ppermute | solution.py:99
  29.5 1.0 %apply_3.1 = (f32[16,8,128]{2,1,0:T(8,128)S(1)}, bf16[16,8,128]{2,1,0:T(8,128)(2,1)S(1)}) custom-call(s32[71]{0:T(128)S(1)} %pad_add_fusion.info, bf16[16,8,128]{2,1,0:T(8,128)(2,1)S(1)} %collective-permute-done.9.refs_0_, bf16[16,8,128]{2,1,0:T(8,128)(2,1)S(1)} %collective-permute-done.10.refs_1_, f32[8,8,128]{2,1,0:T(8,128)S(1)} %bitcast.30, ...), custom_call_target="tpu_custom_call" | custom-call | tf_op jit(solution)/shard_map/apply_3/pallas_call | solution.py:77
  30.5 1.0 %collective-permute-start.12 = (bf16[16,8,128]{2,1,0:T(8,128)(2,1)S(1)}, bf16[16,8,128]{2,1,0:T(8,128)(2,1)S(1)}, u32[]{:S(2)}, u32[]{:S(2)}) collective-permute-start(bf16[16,8,128]{2,1,0:T(8,128)(2,1)S(1)} %get-tuple-element.23), channel_id=1, source_target_pairs={{0,6},{1,7},{2,4},{3,5},{4,2},{5,3},{6,0},{7,1},{8,14},{9,15},{10,... | collective-permute-start | bytes 98312 | tf_op jit(solution)/shard_map/ppermute | solution.py:99
  31.5 1.6 %collective-permute-start.11 = (bf16[16,8,128]{2,1,0:T(8,128)(2,1)S(1)}, bf16[16,8,128]{2,1,0:T(8,128)(2,1)S(1)}, u32[]{:S(2)}, u32[]{:S(2)}) collective-permute-start(bf16[16,8,128]{2,1,0:T(8,128)(2,1)S(1)} %get-tuple-element.23), channel_id=1, source_target_pairs={{0,4},{1,5},{2,6},{3,7},{4,0},{5,1},{6,2},{7,3},{8,12},{9,13},{10,... | collective-permute-start | bytes 98312 | tf_op jit(solution)/shard_map/ppermute | solution.py:99
  33.1 2.3 %collective-permute-done.12.refs_1_ = bf16[16,8,128]{2,1,0:T(8,128)(2,1)S(1)} collective-permute-done((bf16[16,8,128]{2,1,0:T(8,128)(2,1)S(1)}, bf16[16,8,128]{2,1,0:T(8,128)(2,1)S(1)}, u32[]{:S(2)}, u32[]{:S(2)}) %collective-permute-start.12) | collective-permute-done | bytes 32800 | tf_op jit(solution)/shard_map/ppermute | solution.py:99
  35.4 0.3 collective-permute-done.11.refs_0_
  35.8 1.0 %apply_4.1 = (f32[16,8,128]{2,1,0:T(8,128)S(1)}, bf16[16,8,128]{2,1,0:T(8,128)(2,1)S(1)}) custom-call(s32[71]{0:T(128)S(1)} %pad_add_fusion.info, bf16[16,8,128]{2,1,0:T(8,128)(2,1)S(1)} %collective-permute-done.11.refs_0_, bf16[16,8,128]{2,1,0:T(8,128)(2,1)S(1)} %collective-permute-done.12.refs_1_, bf16[8,4,64,128]{3,2,1,0:T(8,128)(2,1)S(1)} %bitcast.20, ...), custom_call_target="tpu_custom_call" | custom-call | tf_op jit(solution)/shard_map/apply_4/pallas_call | solution.py:77
  36.8 1.1 %collective-permute-start.14 = (bf16[16,8,128]{2,1,0:T(8,128)(2,1)S(1)}, bf16[16,8,128]{2,1,0:T(8,128)(2,1)S(1)}, u32[]{:S(2)}, u32[]{:S(2)}) collective-permute-start(bf16[16,8,128]{2,1,0:T(8,128)(2,1)S(1)} %get-tuple-element.25), channel_id=1, source_target_pairs={{0,2},{1,3},{2,0},{3,1},{4,10},{5,11},{6,8},{7,9},{8,6},{9,7},{10,... | collective-permute-start | bytes 98312 | tf_op jit(solution)/shard_map/ppermute | solution.py:99
  37.9 2.9 %collective-permute-done.14.refs_1_ = bf16[16,8,128]{2,1,0:T(8,128)(2,1)S(1)} collective-permute-done((bf16[16,8,128]{2,1,0:T(8,128)(2,1)S(1)}, bf16[16,8,128]{2,1,0:T(8,128)(2,1)S(1)}, u32[]{:S(2)}, u32[]{:S(2)}) %collective-permute-start.14) | collective-permute-done | bytes 32800 | tf_op jit(solution)/shard_map/ppermute | solution.py:99
  40.8 1.0 %apply_5.1 = (f32[16,8,128]{2,1,0:T(8,128)S(1)}, bf16[16,8,128]{2,1,0:T(8,128)(2,1)S(1)}) custom-call(s32[71]{0:T(128)S(1)} %pad_add_fusion.info, bf16[16,8,128]{2,1,0:T(8,128)(2,1)S(1)} %collective-permute-done.13.refs_0_, bf16[16,8,128]{2,1,0:T(8,128)(2,1)S(1)} %collective-permute-done.14.refs_1_, bf16[8,4,64,128]{3,2,1,0:T(8,128)(2,1)S(1)} %bitcast.21, ...), custom_call_target="tpu_custom_call" | custom-call | tf_op jit(solution)/shard_map/apply_5/pallas_call | solution.py:77
  41.8 4.9 %collective-permute-start.16 = (bf16[16,8,128]{2,1,0:T(8,128)(2,1)S(1)}, bf16[16,8,128]{2,1,0:T(8,128)(2,1)S(1)}, u32[]{:S(2)}, u32[]{:S(2)}) collective-permute-start(bf16[16,8,128]{2,1,0:T(8,128)(2,1)S(1)} %get-tuple-element.27), channel_id=1, source_target_pairs={{0,6},{1,7},{2,4},{3,5},{4,2},{5,3},{6,0},{7,1},{8,14},{9,15},{10,... | collective-permute-start | bytes 98312 | tf_op jit(solution)/shard_map/ppermute | solution.py:99
  46.7 1.9 %collective-permute-done.16.refs_1_ = bf16[16,8,128]{2,1,0:T(8,128)(2,1)S(1)} collective-permute-done((bf16[16,8,128]{2,1,0:T(8,128)(2,1)S(1)}, bf16[16,8,128]{2,1,0:T(8,128)(2,1)S(1)}, u32[]{:S(2)}, u32[]{:S(2)}) %collective-permute-start.16) | collective-permute-done | bytes 32800 | tf_op jit(solution)/shard_map/ppermute | solution.py:99
  48.6 2.0 %collective-permute-done.15.refs_0_ = bf16[16,8,128]{2,1,0:T(8,128)(2,1)S(1)} collective-permute-done((bf16[16,8,128]{2,1,0:T(8,128)(2,1)S(1)}, bf16[16,8,128]{2,1,0:T(8,128)(2,1)S(1)}, u32[]{:S(2)}, u32[]{:S(2)}) %collective-permute-start.15) | collective-permute-done | bytes 32800 | tf_op jit(solution)/shard_map/ppermute | solution.py:99
  50.6 1.6 %apply_6.1 = f32[8,1024]{1,0:T(8,128)} custom-call(s32[71]{0:T(128)S(1)} %pad_add_fusion.info, bf16[16,8,128]{2,1,0:T(8,128)(2,1)S(1)} %collective-permute-done.15.refs_0_, bf16[16,8,128]{2,1,0:T(8,128)(2,1)S(1)} %collective-permute-done.16.refs_1_, bf16[8,4,64,128]{3,2,1,0:T(8,128)(2,1)S(1)} %bitcast.22, ...), custom_call_target="tpu_custom_call" | custom-call | tf_op jit(solution)/shard_map/apply_6/pallas_call | solution.py:77
  (27 shorter events, 0.5 us)
Async XLA Ops:
  0.0 3.1 %copy-start.3 = (s32[1,8,3]{1,0,2:T(1,128)S(1)}, s32[1,8,3]{1,0,2:T(1,128)}, u32[]{:S(2)}) copy-start(s32[1,8,3]{1,0,2:T(1,128)} %param.5) | copy-start | bytes 292
  0.0 4.8 %collective-permute-start.3 = (f32[8,8,128]{2,1,0:T(8,128)}, f32[8,8,128]{2,1,0:T(8,128)S(1)}, u32[]{:S(2)}, u32[]{:S(2)}) collective-permute-start(f32[8,8,128]{2,1,0:T(8,128)} %bitcast.23), channel_id=1, source_target_pairs={{0,3},{1,2},{2,1},{3,0},{4,7},{5,6},{6,5},{7,4},{8,11},{9,10},{10,... | collective-permute-start | bytes 98312 | tf_op jit(solution)/shard_map/ppermute | solution.py:102
  2.4 4.2 %collective-permute-start.2 = (f32[8,8,128]{2,1,0:T(8,128)}, f32[8,8,128]{2,1,0:T(8,128)S(1)}, u32[]{:S(2)}, u32[]{:S(2)}) collective-permute-start(f32[8,8,128]{2,1,0:T(8,128)} %bitcast.24), channel_id=1, source_target_pairs={{0,2},{1,3},{2,0},{3,1},{4,6},{5,7},{6,4},{7,5},{8,10},{9,11},{10,... | collective-permute-start | bytes 98312 | tf_op jit(solution)/shard_map/ppermute | solution.py:102
  3.0 3.6 %collective-permute-start.1 = (f32[8,8,128]{2,1,0:T(8,128)}, f32[8,8,128]{2,1,0:T(8,128)S(1)}, u32[]{:S(2)}, u32[]{:S(2)}) collective-permute-start(f32[8,8,128]{2,1,0:T(8,128)} %bitcast.25), channel_id=1, source_target_pairs={{0,1},{1,0},{2,3},{3,2},{4,5},{5,4},{6,7},{7,6},{8,9},{9,8},{10,11... | collective-permute-start | bytes 98312 | tf_op jit(solution)/shard_map/ppermute | solution.py:102
  3.1 1.4 %collective-permute-start = (s32[8,3]{0,1:T(4,128)S(1)}, s32[8,3]{0,1:T(4,128)S(1)}, u32[]{:S(2)}, u32[]{:S(2)}) collective-permute-start(s32[8,3]{0,1:T(4,128)S(1)} %bitcast.31), channel_id=1, source_target_pairs={{0,1},{1,0},{2,3},{3,2},{4,5},{5,4},{6,7},{7,6},{8,9},{9,8},{10,11... | collective-permute-start | bytes 296 | tf_op jit(solution)/shard_map/ppermute | solution.py:102
  3.5 3.0 %collective-permute-start.4 = (bf16[8,4,64,128]{3,2,1,0:T(8,128)(2,1)}, bf16[8,4,64,128]{3,2,1,0:T(8,128)(2,1)S(1)}, u32[]{:S(2)}, u32[]{:S(2)}) collective-permute-start(bf16[8,4,64,128]{3,2,1,0:T(8,128)(2,1)} %bitcast.15), channel_id=1, source_target_pairs={{0,1},{1,0},{2,3},{3,2},{4,5},{5,4},{6,7},{7,6},{8,9},{9,8},{10,11... | collective-permute-start | bytes 1572872 | tf_op jit(solution)/shard_map/ppermute | solution.py:102
  4.8 1.8 %copy-start.2 = (f32[1,8,1024]{2,1,0:T(8,128)S(1)}, f32[1,8,1024]{2,1,0:T(8,128)}, u32[]{:S(2)}) copy-start(f32[1,8,1024]{2,1,0:T(8,128)} %param.3) | copy-start | bytes 98308
  6.6 1.0 %copy-start = (bf16[1,8,4,64,128]{4,3,2,1,0:T(8,128)(2,1)S(1)}, bf16[1,8,4,64,128]{4,3,2,1,0:T(8,128)(2,1)}, u32[]{:S(2)}) copy-start(bf16[1,8,4,64,128]{4,3,2,1,0:T(8,128)(2,1)} %param.4) | copy-start | bytes 1572868
  8.7 5.0 %collective-permute-start.6 = (bf16[16,8,128]{2,1,0:T(8,128)(2,1)S(1)}, bf16[16,8,128]{2,1,0:T(8,128)(2,1)S(1)}, u32[]{:S(2)}, u32[]{:S(2)}) collective-permute-start(bf16[16,8,128]{2,1,0:T(8,128)(2,1)S(1)} %get-tuple-element.17), channel_id=1, source_target_pairs={{0,6},{1,7},{2,4},{3,5},{4,2},{5,3},{6,0},{7,1},{8,14},{9,15},{10,... | collective-permute-start | bytes 98312 | tf_op jit(solution)/shard_map/ppermute | solution.py:99
  10.7 3.9 %collective-permute-start.5 = (bf16[16,8,128]{2,1,0:T(8,128)(2,1)S(1)}, bf16[16,8,128]{2,1,0:T(8,128)(2,1)S(1)}, u32[]{:S(2)}, u32[]{:S(2)}) collective-permute-start(bf16[16,8,128]{2,1,0:T(8,128)(2,1)S(1)} %get-tuple-element.17), channel_id=1, source_target_pairs={{0,4},{1,5},{2,6},{3,7},{4,0},{5,1},{6,2},{7,3},{8,12},{9,13},{10,... | collective-permute-start | bytes 98312 | tf_op jit(solution)/shard_map/ppermute | solution.py:99
  15.6 4.0 %collective-permute-start.8 = (bf16[16,8,128]{2,1,0:T(8,128)(2,1)S(1)}, bf16[16,8,128]{2,1,0:T(8,128)(2,1)S(1)}, u32[]{:S(2)}, u32[]{:S(2)}) collective-permute-start(bf16[16,8,128]{2,1,0:T(8,128)(2,1)S(1)} %get-tuple-element.19), channel_id=1, source_target_pairs={{0,2},{1,3},{2,0},{3,1},{4,10},{5,11},{6,8},{7,9},{8,6},{9,7},{10,... | collective-permute-start | bytes 98312 | tf_op jit(solution)/shard_map/ppermute | solution.py:99
  16.7 2.9 %collective-permute-start.7 = (bf16[16,8,128]{2,1,0:T(8,128)(2,1)S(1)}, bf16[16,8,128]{2,1,0:T(8,128)(2,1)S(1)}, u32[]{:S(2)}, u32[]{:S(2)}) collective-permute-start(bf16[16,8,128]{2,1,0:T(8,128)(2,1)S(1)} %get-tuple-element.19), channel_id=1, source_target_pairs={{0,1},{1,0},{2,3},{3,2},{4,8},{5,9},{6,10},{7,11},{8,4},{9,5},{10,... | collective-permute-start | bytes 98312 | tf_op jit(solution)/shard_map/ppermute | solution.py:99
  20.6 6.8 %collective-permute-start.10 = (bf16[16,8,128]{2,1,0:T(8,128)(2,1)S(1)}, bf16[16,8,128]{2,1,0:T(8,128)(2,1)S(1)}, u32[]{:S(2)}, u32[]{:S(2)}) collective-permute-start(bf16[16,8,128]{2,1,0:T(8,128)(2,1)S(1)} %get-tuple-element.21), channel_id=1, source_target_pairs={{0,6},{1,7},{2,4},{3,5},{4,2},{5,3},{6,0},{7,1},{8,14},{9,15},{10,... | collective-permute-start | bytes 98312 | tf_op jit(solution)/shard_map/ppermute | solution.py:99
  25.5 3.9 %collective-permute-start.9 = (bf16[16,8,128]{2,1,0:T(8,128)(2,1)S(1)}, bf16[16,8,128]{2,1,0:T(8,128)(2,1)S(1)}, u32[]{:S(2)}, u32[]{:S(2)}) collective-permute-start(bf16[16,8,128]{2,1,0:T(8,128)(2,1)S(1)} %get-tuple-element.21), channel_id=1, source_target_pairs={{0,4},{1,5},{2,6},{3,7},{4,0},{5,1},{6,2},{7,3},{8,12},{9,13},{10,... | collective-permute-start | bytes 98312 | tf_op jit(solution)/shard_map/ppermute | solution.py:99
  29.5 6.3 %copy-start.1 = (bf16[1,8,4,64,128]{4,3,2,1,0:T(8,128)(2,1)S(1)}, bf16[1,8,4,64,128]{4,3,2,1,0:T(8,128)(2,1)}, u32[]{:S(2)}) copy-start(bf16[1,8,4,64,128]{4,3,2,1,0:T(8,128)(2,1)} %param.4) | copy-start | bytes 1572868
  30.5 4.9 %collective-permute-start.12 = (bf16[16,8,128]{2,1,0:T(8,128)(2,1)S(1)}, bf16[16,8,128]{2,1,0:T(8,128)(2,1)S(1)}, u32[]{:S(2)}, u32[]{:S(2)}) collective-permute-start(bf16[16,8,128]{2,1,0:T(8,128)(2,1)S(1)} %get-tuple-element.23), channel_id=1, source_target_pairs={{0,6},{1,7},{2,4},{3,5},{4,2},{5,3},{6,0},{7,1},{8,14},{9,15},{10,... | collective-permute-start | bytes 98312 | tf_op jit(solution)/shard_map/ppermute | solution.py:99
  31.5 4.3 %collective-permute-start.11 = (bf16[16,8,128]{2,1,0:T(8,128)(2,1)S(1)}, bf16[16,8,128]{2,1,0:T(8,128)(2,1)S(1)}, u32[]{:S(2)}, u32[]{:S(2)}) collective-permute-start(bf16[16,8,128]{2,1,0:T(8,128)(2,1)S(1)} %get-tuple-element.23), channel_id=1, source_target_pairs={{0,4},{1,5},{2,6},{3,7},{4,0},{5,1},{6,2},{7,3},{8,12},{9,13},{10,... | collective-permute-start | bytes 98312 | tf_op jit(solution)/shard_map/ppermute | solution.py:99
  36.8 4.0 %collective-permute-start.14 = (bf16[16,8,128]{2,1,0:T(8,128)(2,1)S(1)}, bf16[16,8,128]{2,1,0:T(8,128)(2,1)S(1)}, u32[]{:S(2)}, u32[]{:S(2)}) collective-permute-start(bf16[16,8,128]{2,1,0:T(8,128)(2,1)S(1)} %get-tuple-element.25), channel_id=1, source_target_pairs={{0,2},{1,3},{2,0},{3,1},{4,10},{5,11},{6,8},{7,9},{8,6},{9,7},{10,... | collective-permute-start | bytes 98312 | tf_op jit(solution)/shard_map/ppermute | solution.py:99
  37.9 2.9 %collective-permute-start.13 = (bf16[16,8,128]{2,1,0:T(8,128)(2,1)S(1)}, bf16[16,8,128]{2,1,0:T(8,128)(2,1)S(1)}, u32[]{:S(2)}, u32[]{:S(2)}) collective-permute-start(bf16[16,8,128]{2,1,0:T(8,128)(2,1)S(1)} %get-tuple-element.25), channel_id=1, source_target_pairs={{0,1},{1,0},{2,3},{3,2},{4,8},{5,9},{6,10},{7,11},{8,4},{9,5},{10,... | collective-permute-start | bytes 98312 | tf_op jit(solution)/shard_map/ppermute | solution.py:99
  41.8 6.8 %collective-permute-start.16 = (bf16[16,8,128]{2,1,0:T(8,128)(2,1)S(1)}, bf16[16,8,128]{2,1,0:T(8,128)(2,1)S(1)}, u32[]{:S(2)}, u32[]{:S(2)}) collective-permute-start(bf16[16,8,128]{2,1,0:T(8,128)(2,1)S(1)} %get-tuple-element.27), channel_id=1, source_target_pairs={{0,6},{1,7},{2,4},{3,5},{4,2},{5,3},{6,0},{7,1},{8,14},{9,15},{10,... | collective-permute-start | bytes 98312 | tf_op jit(solution)/shard_map/ppermute | solution.py:99
  46.7 3.9 %collective-permute-start.15 = (bf16[16,8,128]{2,1,0:T(8,128)(2,1)S(1)}, bf16[16,8,128]{2,1,0:T(8,128)(2,1)S(1)}, u32[]{:S(2)}, u32[]{:S(2)}) collective-permute-start(bf16[16,8,128]{2,1,0:T(8,128)(2,1)S(1)} %get-tuple-element.27), channel_id=1, source_target_pairs={{0,4},{1,5},{2,6},{3,7},{4,0},{5,1},{6,2},{7,3},{8,12},{9,13},{10,... | collective-permute-start | bytes 98312 | tf_op jit(solution)/shard_map/ppermute | solution.py:99

commit v3 on v0

v3 whole, which is shorter than its diff:
```python
import functools

import jax
import jax.numpy as jnp
from jax import lax
from jax.experimental import pallas as pl
from jax.experimental.pallas import tpu as pltpu
from jax.sharding import PartitionSpec as P


SEG = 4
AXES = ("sweep", "tile")
VMEM = pl.BlockSpec(memory_space=pltpu.VMEM)
SMEM = pl.BlockSpec(memory_space=pltpu.SMEM)


def place_of(sweep):
    turn = lax.rem(sweep + SEG // 2, SEG)
    return jnp.where(sweep < SEG // 2, sweep, turn)


def apply_kernel(stage, plan, *refs):
    rec_flips, add_src, row_flips, block_rows, n_states, has_msg, keep_src = plan
    refs = list(refs)
    take = lambda n: [refs.pop(0) for _ in range(n)]
    (patterns,), recs, srcs = take(1), take(len(rec_flips)), take(int(add_src))
    blocks, states = take(len(block_rows)), take(n_states)
    state_out = refs.pop(0)
    msg_out = refs.pop(0) if has_msg else None
    src_out = refs.pop(0) if keep_src else None
    (vec,) = refs
    width = blocks[0].shape[-1]
    half = width // 2
    off, nb = patterns.shape[0] // 3, patterns.shape[1]
    base = lax.axis_index("tile") * nb
    place = place_of(lax.axis_index("sweep"))
    lane = lax.broadcasted_iota(jnp.int32, (1, 1, width), 2)
    sign = jnp.where(lane < half, 1.0, -1.0).astype(jnp.float32)
    for rec, flips in zip(recs, rec_flips):
        for index, flip in enumerate(flips):
            value = rec[pl.ds(index * nb, nb)].astype(jnp.float32)
            slots = pl.ds(flip * nb, nb)
            if keep_src:
                src_out[slots] = value
            if add_src:
                value = value + srcs[0][slots]
            value = value.astype(jnp.bfloat16).astype(jnp.float32)
            imag_in = pltpu.roll(value, half, axis=2)
            pair = jnp.concatenate([value * sign, imag_in], axis=1)
            vec[slots] = pair.astype(jnp.bfloat16)
    row_refs = [(ref, at) for ref, count in zip(blocks, block_rows) for at in range(count)]
    for row, (ref, at) in enumerate(row_refs):
        group, local = divmod(row, nb)
        flip = row_flips[group]
        slots = [flip * nb + local]
        slots += [patterns[flip * off + j, local] ^ base for j in range(off)]
        mats = jnp.concatenate([ref[at, j] for j in range(off + 1)], axis=1)
        inputs = jnp.concatenate([vec[slot] for slot in slots], axis=1)
        out = lax.dot_general(
            inputs, mats, (((1,), (1,)), ((), ())), preferred_element_type=jnp.float32
        )
        rhs = out.shape[0] // 2
        result = jnp.concatenate([out[:rhs], out[rhs:]], axis=1)
        if stage == 4:
            result = states[group][local] + result
        if stage == 5:
            sweep = lax.axis_index("sweep")
            inner = (sweep >= SEG // 2) & (sweep < lax.axis_size("sweep") - SEG // 2)
            result = states[group][local] + jnp.where(inner, result, 0.0)
        if stage == 6:
            result = states[0][row] + result
            for other in (1, 2, 3):
                result = jnp.where(place == other, states[other][row], result)
            state_out[:, row * width : (row + 1) * width] = result
            continue
        if row < state_out.shape[0]:
            state_out[row] = result
        msg_out[row] = result.astype(jnp.bfloat16)


def layer_apply(stage, patterns, row_flips, recs, blocks, src=None, states=(), keep_src=False):
    arrays = [r for r, _ in recs]
    nb = patterns.shape[1]
    rhs, width = arrays[0].shape[1:]
    total = sum(r.shape[0] for r in arrays)
    rows = sum(b.shape[0] for b in blocks)
    has_msg = stage < 2 * SEG - 2
    if has_msg:
        kept = nb if stage < 3 else rows
        out_shape = [
            jax.ShapeDtypeStruct((kept, rhs, width), jnp.float32),
            jax.ShapeDtypeStruct((rows, rhs, width), jnp.bfloat16),
        ]
        if keep_src:
            out_shape.append(jax.ShapeDtypeStruct((total, rhs, width), jnp.float32))
    else:
        out_shape = [jax.ShapeDtypeStruct((rhs, rows * width), jnp.float32)]
    plan = (
        tuple(tuple(f) for _, f in recs),
        src is not None,
        tuple(row_flips),
        tuple(b.shape[0] for b in blocks),
        len(states),
        has_msg,
        keep_src,
    )
    args = [*arrays, *([] if src is None else [src]), *blocks, *states]
    return pl.pallas_call(
        functools.partial(apply_kernel, stage, plan),
        in_specs=[SMEM] + [VMEM] * len(args),
        out_specs=[VMEM] * len(out_shape),
        out_shape=out_shape,
        scratch_shapes=[pltpu.VMEM((total, 2 * rhs, width), jnp.bfloat16)],
        compiler_params=pltpu.CompilerParams(vmem_limit_bytes=8 * 1024 * 1024),
    )(patterns, *args)


def stage_in(blocks):
    def kernel(source, out, sem):
        copy = pltpu.make_async_copy(source, out, sem)
        copy.start()
        copy.wait()

    return pl.pallas_call(
        kernel,
        in_specs=[pl.BlockSpec(memory_space=pl.ANY)],
        out_specs=VMEM,
        out_shape=jax.ShapeDtypeStruct(blocks.shape, blocks.dtype),
        scratch_shapes=[pltpu.SemaphoreType.DMA(())],
        compiler_params=pltpu.CompilerParams(vmem_limit_bytes=4 * 1024 * 1024),
        name="stage_in",
    )(blocks)


def per_device(sources, blocks, pattern):
    sweeps, tiles = lax.axis_size("sweep"), lax.axis_size("tile")
    own_blocks, own_pattern = blocks[0], pattern[0].T
    nb, width = own_blocks.shape[0], own_blocks.shape[-1]
    rhs, hn = sources.shape[1], nb // 2
    layers = range(sweeps)

    def place(layer):
        return layer if layer < SEG // 2 else (layer + SEG // 2) % SEG

    def plane_late(layer):
        return (layer + SEG // 2) % SEG >= 2

    everyone = {layer: layer for layer in layers}
    early = {layer: layer for layer in layers if not plane_late(layer)}
    late = {layer: layer for layer in layers if plane_late(layer)}
    late_y = {layer: layer ^ 1 for layer in late}
    starts = {layer: layer for layer in layers if place(layer) < 2}
    start_y = {layer: layer ^ 1 for layer in layers if place(layer) < 2}
    across_y = {layer: layer ^ 1 for layer in layers}
    across_z = {
        layer: layer + (2 if not plane_late(layer) else -2)
        for layer in range(SEG // 2, sweeps - SEG // 2)
    }
    core_flips = [f for f in range(tiles) if not f & 2]
    even_flips = [f for f in range(tiles) if not f & 1]

    def swap(value, pairs, flip):
        route = []
        for layer in layers:
            mask = flip if layer in pairs else 1
            other = pairs.get(layer, layer)
            route += [(layer * tiles + t, other * tiles + (t ^ mask)) for t in range(tiles)]
        return lax.ppermute(value, AXES, route)

    def hop(msg, pairs, flips, other, own=False):
        recs = [(msg, (0, other))] if own else []
        for f in flips:
            if f or not own:
                recs.append((swap(msg, pairs, f), (f, f ^ other)))
        return recs

    src_own = sources[0].reshape(rhs, nb, width).transpose(1, 0, 2)
    src_pieces = [(src_own, (0,))]
    src_pieces += [(swap(src_own, everyone, f), (f,)) for f in range(1, tiles)]
    core_blocks = swap(own_blocks, everyone, 1)
    core_pattern = swap(own_pattern, everyone, 1)
    x_pattern = swap(own_pattern, everyone, 2)
    y_blocks = swap(own_blocks, late_y, 0)
    x_blocks = swap(own_blocks, late, 2)
    own = stage_in(own_blocks)

    patterns = jnp.concatenate([own_pattern, core_pattern, x_pattern], axis=0)
    core_rows = dict(patterns=patterns, row_flips=(0, 1))
    down_0, msg, src_all = layer_apply(
        0, recs=src_pieces, blocks=[own, core_blocks], keep_src=True, **core_rows
    )
    recs = hop(msg, start_y, even_flips, 1)

    y_patterns = swap(patterns, late_y, 0)
    src_other = swap(src_all, late_y, 0)
    diag_0 = swap(y_blocks[:hn], late, 2)
    diag_1 = swap(x_blocks[hn:], late_y, 0)

    down_1, msg = layer_apply(
        1, recs=recs, blocks=[own, core_blocks], src=src_all, **core_rows
    )
    recs = hop(msg, across_z, even_flips, 1)
    down_1_x = swap(down_1, starts, 2)
    x_late = swap(own_blocks, early, 2)

    y_core = swap(y_blocks, everyone, 1)
    down_2, msg = layer_apply(2, y_patterns, (0, 1), recs, [y_blocks, y_core], src=src_other)
    recs = hop(msg, late, even_flips, 1, own=True)
    down_2_x = swap(down_2, late, 2)
    own_rows = dict(patterns=patterns, row_flips=(0, 2))
    down_3, msg = layer_apply(
        3, recs=recs, blocks=[own, x_blocks], src=src_all, **own_rows
    )
    recs = hop(msg, everyone, core_flips, 2, own=True)
    up_2, msg = layer_apply(
        4, y_patterns, (0, 2), recs, [y_blocks, diag_0, diag_1], states=[down_2, down_2_x]
    )
    recs = hop(msg, across_z, core_flips, 2)
    up_2_own = swap(up_2[:nb], late_y, 0)
    up_1, msg = layer_apply(
        5, recs=recs, blocks=[own, x_late], states=[down_1, down_1_x], **own_rows
    )
    recs = hop(msg, across_y, core_flips, 2)
    (upper,) = layer_apply(
        6,
        patterns=patterns,
        row_flips=(0,),
        recs=recs,
        blocks=[own],
        states=[down_0, up_1, up_2_own, down_3],
    )
    return upper[None]


def solution(mesh):
    return jax.shard_map(
        per_device,
        mesh=mesh,
        in_specs=(
            P("sweep", None, "tile"),
            P("sweep", "tile", None, None, None),
            P("sweep", "tile", None),
        ),
        out_specs=P("sweep", None, "tile"),
        check_vma=False,
    )
```

time: 110 us -> 72.9 us (0.66)
  the two profiles are of different devices: /device:TPU:0 before, /device:TPU:9 now
where the time goes in v3:
time: 72.9 us; the launch traced here: 72.7 us
  waiting for transfers between devices  33 us (45%)
  starting transfers between devices  29.8 us (41%)
  Pallas kernels  8.73 us (12%)
  local copies, waits for them, and re-layouts  1.12 us (2%)
    ppermute x27, waiting for transfers between devices, swap(): return lax.ppermute(value, AXES, route)  33 us
    ppermute x27, starting transfers between devices, swap(): return lax.ppermute(value, AXES, route)  29.8 us
    pallas_call x7, Pallas kernels, layer_apply(): pl.pallas_call(functools.partial(apply_kernel, stage, plan), in_specs=[SM...  8.69 us
  transfers between devices with their start and end apart: 27, of which 16 were waited for; matrix products, arithmetic and copies ran while one was open for 0% of the time, Pallas kernels for 10%

profile of v3, /device:TPU:9, one launch (start us, length us, event | category | flops | bytes accessed | tf_op | source)
XLA Modules:
  0.0 72.7 jit_solution(9207400936582141111)
XLA Ops:
  1.2 1.2 %collective-permute-done.12.refs_4_.refs_3_ = bf16[8,4,64,128]{3,2,1,0:T(8,128)(2,1)S(1)} collective-permute-done((bf16[8,4,64,128]{3,2,1,0:T(8,128)(2,1)}, bf16[8,4,64,128]{3,2,1,0:T(8,128)(2,1)S(1)}, u32[]{:S(2)}, u32[]{:S(2)}) %collective-permute-start.12) | collective-permute-done | bytes 524320 | tf_op jit(solution)/shard_map/ppermute | solution.py:168
  2.8 1.2 %collective-permute-start.22 = (bf16[8,4,64,128]{3,2,1,0:T(8,128)(2,1)}, bf16[8,4,64,128]{3,2,1,0:T(8,128)(2,1)S(1)}, u32[]{:S(2)}, u32[]{:S(2)}) collective-permute-start(bf16[8,4,64,128]{3,2,1,0:T(8,128)(2,1)} %bitcast.13), channel_id=1, source_target_pairs={{0,1},{1,0},{2,3},{3,2},{4,5},{5,4},{6,7},{7,6},{8,10},{9,11},{10,... | collective-permute-start | bytes 1572872 | tf_op jit(solution)/shard_map/ppermute | solution.py:168
  4.3 12.1 %collective-permute-done.1 = s32[3,8]{1,0:T(4,128)S(1)} collective-permute-done((s32[3,8]{1,0:T(4,128)S(1)}, s32[3,8]{1,0:T(4,128)S(1)}, u32[]{:S(2)}, u32[]{:S(2)}) %collective-permute-start.1) | collective-permute-done | bytes 128 | tf_op jit(solution)/shard_map/ppermute | solution.py:168
  16.4 1.0 %collective-permute-start = (s32[3,8]{1,0:T(4,128)S(1)}, s32[3,8]{1,0:T(4,128)S(1)}, u32[]{:S(2)}, u32[]{:S(2)}) collective-permute-start(s32[3,8]{1,0:T(4,128)S(1)} %bitcast.20), channel_id=1, source_target_pairs={{0,1},{1,0},{2,3},{3,2},{4,5},{5,4},{6,7},{7,6},{8,9},{9,8},{10,11... | collective-permute-start | bytes 296 | tf_op jit(solution)/shard_map/ppermute | solution.py:168
  17.4 0.8 %collective-permute-done = s32[3,8]{1,0:T(4,128)S(1)} collective-permute-done((s32[3,8]{1,0:T(4,128)S(1)}, s32[3,8]{1,0:T(4,128)S(1)}, u32[]{:S(2)}, u32[]{:S(2)}) %collective-permute-start) | collective-permute-done | bytes 128 | tf_op jit(solution)/shard_map/ppermute | solution.py:168
  18.6 1.1 %collective-permute-done.3.refs_2_ = f32[8,8,128]{2,1,0:T(8,128)S(1)} collective-permute-done((f32[8,8,128]{2,1,0:T(8,128)}, f32[8,8,128]{2,1,0:T(8,128)S(1)}, u32[]{:S(2)}, u32[]{:S(2)}) %collective-permute-start.3) | collective-permute-done | bytes 32800 | tf_op jit(solution)/shard_map/ppermute | solution.py:168
  19.6 1.2 %collective-permute-start.4 = (f32[8,8,128]{2,1,0:T(8,128)}, f32[8,8,128]{2,1,0:T(8,128)S(1)}, u32[]{:S(2)}, u32[]{:S(2)}) collective-permute-start(f32[8,8,128]{2,1,0:T(8,128)} %bitcast.16), channel_id=1, source_target_pairs={{0,2},{1,3},{2,0},{3,1},{4,6},{5,7},{6,4},{7,5},{8,10},{9,11},{10,... | collective-permute-start | bytes 98312 | tf_op jit(solution)/shard_map/ppermute | solution.py:168
  20.8 1.0 %copy-done = bf16[1,8,4,64,128]{4,3,2,1,0:T(8,128)(2,1)S(1)} copy-done((bf16[1,8,4,64,128]{4,3,2,1,0:T(8,128)(2,1)S(1)}, bf16[1,8,4,64,128]{4,3,2,1,0:T(8,128)(2,1)}, u32[]{:S(2)}) %copy-start) | copy-done | bytes 524312
  22.6 2.6 %collective-permute-start.5 = (f32[8,8,128]{2,1,0:T(8,128)S(1)}, f32[8,8,128]{2,1,0:T(8,128)S(1)}, u32[]{:S(2)}, u32[]{:S(2)}) collective-permute-start(f32[8,8,128]{2,1,0:T(8,128)S(1)} %bitcast.17), channel_id=1, source_target_pairs={{0,3},{1,2},{2,1},{3,0},{4,7},{5,6},{6,5},{7,4},{8,11},{9,10},{10,... | collective-permute-start | bytes 98312 | tf_op jit(solution)/shard_map/ppermute | solution.py:168
  25.2 2.1 %collective-permute-done.5.refs_4_ = f32[8,8,128]{2,1,0:T(8,128)S(1)} collective-permute-done((f32[8,8,128]{2,1,0:T(8,128)S(1)}, f32[8,8,128]{2,1,0:T(8,128)S(1)}, u32[]{:S(2)}, u32[]{:S(2)}) %collective-permute-start.5) | collective-permute-done | bytes 32800 | tf_op jit(solution)/shard_map/ppermute | solution.py:168
  27.4 1.2 %shard_map.37 = (f32[8,8,128]{2,1,0:T(8,128)S(1)}, bf16[16,8,128]{2,1,0:T(8,128)(2,1)S(1)}, f32[32,8,128]{2,1,0:T(8,128)S(1)}) custom-call(s32[9,8]{1,0:T(8,128)S(1)} %pad_add_fusion.refs_0_, f32[8,8,128]{2,1,0:T(8,128)S(1)} %bitcast.18, f32[8,8,128]{2,1,0:T(8,128)S(1)} %collective-permute-done.3.refs_2_, f32[8,8,128]{2,1,0:T(8,128)S(1)} %collective-permute-done.4.refs_3_, ...), custom_call_target="tpu_custom_call" | custom-call | tf_op jit(solution)/shard_map/pallas_call | solution.py:108
  28.5 1.3 %collective-permute-start.7 = (bf16[16,8,128]{2,1,0:T(8,128)(2,1)S(1)}, bf16[16,8,128]{2,1,0:T(8,128)(2,1)S(1)}, u32[]{:S(2)}, u32[]{:S(2)}) collective-permute-start(bf16[16,8,128]{2,1,0:T(8,128)(2,1)S(1)} %get-tuple-element.18), channel_id=1, source_target_pairs={{0,4},{1,5},{2,6},{3,7},{4,0},{5,1},{6,2},{7,3},{8,12},{9,13},{10,... | collective-permute-start | bytes 98312 | tf_op jit(solution)/shard_map/ppermute | solution.py:168
  29.8 1.5 %collective-permute-done.7.refs_1_ = bf16[16,8,128]{2,1,0:T(8,128)(2,1)S(1)} collective-permute-done((bf16[16,8,128]{2,1,0:T(8,128)(2,1)S(1)}, bf16[16,8,128]{2,1,0:T(8,128)(2,1)S(1)}, u32[]{:S(2)}, u32[]{:S(2)}) %collective-permute-start.7) | collective-permute-done | bytes 32800 | tf_op jit(solution)/shard_map/ppermute | solution.py:168
  31.3 2.1 %collective-permute-done.8.refs_2_ = bf16[16,8,128]{2,1,0:T(8,128)(2,1)S(1)} collective-permute-done((bf16[16,8,128]{2,1,0:T(8,128)(2,1)S(1)}, bf16[16,8,128]{2,1,0:T(8,128)(2,1)S(1)}, u32[]{:S(2)}, u32[]{:S(2)}) %collective-permute-start.8) | collective-permute-done | bytes 32800 | tf_op jit(solution)/shard_map/ppermute | solution.py:168
  33.5 1.2 %shard_map.38 = (f32[8,8,128]{2,1,0:T(8,128)S(1)}, bf16[16,8,128]{2,1,0:T(8,128)(2,1)S(1)}) custom-call(s32[9,8]{1,0:T(8,128)S(1)} %pad_add_fusion.refs_0_, bf16[16,8,128]{2,1,0:T(8,128)(2,1)S(1)} %collective-permute-done.7.refs_1_, bf16[16,8,128]{2,1,0:T(8,128)(2,1)S(1)} %collective-permute-done.8.refs_2_, f32[32,8,128]{2,1,0:T(8,128)S(1)} %get-tuple-element.19.refs_3_, ...), custom_call_target="tpu_custom_call" | custom-call | tf_op jit(solution)/shard_map/pallas_call | solution.py:108
  34.7 1.9 %collective-permute-start.2 = (s32[9,8]{1,0:T(8,128)S(1)}, s32[9,8]{1,0:T(8,128)S(1)}, u32[]{:S(2)}, u32[]{:S(2)}) collective-permute-start(s32[9,8]{1,0:T(8,128)S(1)} %pad_add_fusion.refs_0_), channel_id=1, source_target_pairs={{0,4},{1,5},{2,6},{3,7},{4,0},{5,1},{6,2},{7,3},{8,9},{9,8},{10,11... | collective-permute-start | bytes 872 | tf_op jit(solution)/shard_map/ppermute | solution.py:168
  37.8 1.2 %collective-permute-start.10 = (bf16[16,8,128]{2,1,0:T(8,128)(2,1)S(1)}, bf16[16,8,128]{2,1,0:T(8,128)(2,1)S(1)}, u32[]{:S(2)}, u32[]{:S(2)}) collective-permute-start(bf16[16,8,128]{2,1,0:T(8,128)(2,1)S(1)} %get-tuple-element.20), channel_id=1, source_target_pairs={{0,1},{1,0},{2,3},{3,2},{4,5},{5,4},{6,7},{7,6},{8,18},{9,19},{10,... | collective-permute-start | bytes 98312 | tf_op jit(solution)/shard_map/ppermute | solution.py:168
  39.0 2.4 %collective-permute-done.10.refs_2_ = bf16[16,8,128]{2,1,0:T(8,128)(2,1)S(1)} collective-permute-done((bf16[16,8,128]{2,1,0:T(8,128)(2,1)S(1)}, bf16[16,8,128]{2,1,0:T(8,128)(2,1)S(1)}, u32[]{:S(2)}, u32[]{:S(2)}) %collective-permute-start.10) | collective-permute-done | bytes 32800 | tf_op jit(solution)/shard_map/ppermute | solution.py:168
  41.4 3.9 %collective-permute-start.11 = (f32[32,8,128]{2,1,0:T(8,128)S(1)}, f32[32,8,128]{2,1,0:T(8,128)S(1)}, u32[]{:S(2)}, u32[]{:S(2)}) collective-permute-start(f32[32,8,128]{2,1,0:T(8,128)S(1)} %get-tuple-element.19.refs_3_), channel_id=1, source_target_pairs={{0,4},{1,5},{2,6},{3,7},{4,0},{5,1},{6,2},{7,3},{8,9},{9,8},{10,11... | collective-permute-start | bytes 393224 | tf_op jit(solution)/shard_map/ppermute | solution.py:168
  45.3 1.0 %collective-permute-done.11.refs_3_ = f32[32,8,128]{2,1,0:T(8,128)S(1)} collective-permute-done((f32[32,8,128]{2,1,0:T(8,128)S(1)}, f32[32,8,128]{2,1,0:T(8,128)S(1)}, u32[]{:S(2)}, u32[]{:S(2)}) %collective-permute-start.11) | collective-permute-done | bytes 131104 | tf_op jit(solution)/shard_map/ppermute | solution.py:168
  46.3 1.2 %shard_map.39 = (f32[8,8,128]{2,1,0:T(8,128)S(1)}, bf16[16,8,128]{2,1,0:T(8,128)(2,1)S(1)}) custom-call(s32[9,8]{1,0:T(8,128)S(1)} %collective-permute-done.2.refs_0_, bf16[16,8,128]{2,1,0:T(8,128)(2,1)S(1)} %collective-permute-done.9.refs_1_, bf16[16,8,128]{2,1,0:T(8,128)(2,1)S(1)} %collective-permute-done.10.refs_2_, ...), custom_call_target="tpu_custom_call" | custom-call | tf_op jit(solution)/shard_map/pallas_call | solution.py:108
  48.7 1.1 %shard_map.40 = (f32[16,8,128]{2,1,0:T(8,128)S(1)}, bf16[16,8,128]{2,1,0:T(8,128)(2,1)S(1)}) custom-call(s32[9,8]{1,0:T(8,128)S(1)} %pad_add_fusion.refs_0_, bf16[16,8,128]{2,1,0:T(8,128)(2,1)S(1)} %get-tuple-element.21.refs_1_, bf16[16,8,128]{2,1,0:T(8,128)(2,1)S(1)} %collective-permute-done.14.refs_2_, f32[32,8,128]{2,1,0:T(8,128)S(1)} %get-tuple-element.19.refs_3_, ...), custom_call_target="tpu_custom_call" | custom-call | tf_op jit(solution)/shard_map/pallas_call | solution.py:108
  50.3 0.8 %collective-permute-start.23 = (f32[8,8,128]{2,1,0:T(8,128)S(1)}, f32[8,8,128]{2,1,0:T(8,128)S(1)}, u32[]{:S(2)}, u32[]{:S(2)}) collective-permute-start(f32[8,8,128]{2,1,0:T(8,128)S(1)} %get-tuple-element.25.refs_5_), channel_id=1, source_target_pairs={{0,2},{1,3},{2,0},{3,1},{4,6},{5,7},{6,4},{7,5},{8,10},{9,11},{10,... | collective-permute-start | bytes 98312 | tf_op jit(solution)/shard_map/ppermute | solution.py:168
  51.2 1.2 %shard_map.41 = (f32[16,8,128]{2,1,0:T(8,128)S(1)}, bf16[16,8,128]{2,1,0:T(8,128)(2,1)S(1)}) custom-call(s32[9,8]{1,0:T(8,128)S(1)} %collective-permute-done.2.refs_0_, bf16[16,8,128]{2,1,0:T(8,128)(2,1)S(1)} %get-tuple-element.22.refs_1_, bf16[16,8,128]{2,1,0:T(8,128)(2,1)S(1)} %collective-permute-done.16.refs_2_, ...), custom_call_target="tpu_custom_call" | custom-call | tf_op jit(solution)/shard_map/pallas_call | solution.py:108
  52.3 8.4 %collective-permute-start.20 = (bf16[16,8,128]{2,1,0:T(8,128)(2,1)S(1)}, bf16[16,8,128]{2,1,0:T(8,128)(2,1)S(1)}, u32[]{:S(2)}, u32[]{:S(2)}) collective-permute-start(bf16[16,8,128]{2,1,0:T(8,128)(2,1)S(1)} %get-tuple-element.24), channel_id=1, source_target_pairs={{0,1},{1,0},{2,3},{3,2},{4,5},{5,4},{6,7},{7,6},{8,16},{9,17},{10,... | collective-permute-start | bytes 98312 | tf_op jit(solution)/shard_map/ppermute | solution.py:168
  62.0 2.6 %collective-permute-done.21.refs_2_ = bf16[16,8,128]{2,1,0:T(8,128)(2,1)S(1)} collective-permute-done((bf16[16,8,128]{2,1,0:T(8,128)(2,1)S(1)}, bf16[16,8,128]{2,1,0:T(8,128)(2,1)S(1)}, u32[]{:S(2)}, u32[]{:S(2)}) %collective-permute-start.21) | collective-permute-done | bytes 32800 | tf_op jit(solution)/shard_map/ppermute | solution.py:168
  64.6 1.2 %shard_map.42 = (f32[16,8,128]{2,1,0:T(8,128)S(1)}, bf16[16,8,128]{2,1,0:T(8,128)(2,1)S(1)}) custom-call(s32[9,8]{1,0:T(8,128)S(1)} %pad_add_fusion.refs_0_, bf16[16,8,128]{2,1,0:T(8,128)(2,1)S(1)} %collective-permute-done.20.refs_1_, bf16[16,8,128]{2,1,0:T(8,128)(2,1)S(1)} %collective-permute-done.21.refs_2_, ...), custom_call_target="tpu_custom_call" | custom-call | tf_op jit(solution)/shard_map/pallas_call | solution.py:108
  65.7 1.3 %collective-permute-start.24 = (bf16[16,8,128]{2,1,0:T(8,128)(2,1)S(1)}, bf16[16,8,128]{2,1,0:T(8,128)(2,1)S(1)}, u32[]{:S(2)}, u32[]{:S(2)}) collective-permute-start(bf16[16,8,128]{2,1,0:T(8,128)(2,1)S(1)} %get-tuple-element.26), channel_id=1, source_target_pairs={{0,4},{1,5},{2,6},{3,7},{4,0},{5,1},{6,2},{7,3},{8,12},{9,13},{10,... | collective-permute-start | bytes 98312 | tf_op jit(solution)/shard_map/ppermute | solution.py:168
  67.1 0.8 %collective-permute-start.25 = (bf16[16,8,128]{2,1,0:T(8,128)(2,1)S(1)}, bf16[16,8,128]{2,1,0:T(8,128)(2,1)S(1)}, u32[]{:S(2)}, u32[]{:S(2)}) collective-permute-start(bf16[16,8,128]{2,1,0:T(8,128)(2,1)S(1)} %get-tuple-element.26), channel_id=1, source_target_pairs={{0,5},{1,4},{2,7},{3,6},{4,1},{5,0},{6,3},{7,2},{8,13},{9,12},{10,... | collective-permute-start | bytes 98312 | tf_op jit(solution)/shard_map/ppermute | solution.py:168
  67.8 0.7 %collective-permute-done.24.refs_1_ = bf16[16,8,128]{2,1,0:T(8,128)(2,1)S(1)} collective-permute-done((bf16[16,8,128]{2,1,0:T(8,128)(2,1)S(1)}, bf16[16,8,128]{2,1,0:T(8,128)(2,1)S(1)}, u32[]{:S(2)}, u32[]{:S(2)}) %collective-permute-start.24) | collective-permute-done | bytes 32800 | tf_op jit(solution)/shard_map/ppermute | solution.py:168
  68.6 2.4 %collective-permute-done.25.refs_2_ = bf16[16,8,128]{2,1,0:T(8,128)(2,1)S(1)} collective-permute-done((bf16[16,8,128]{2,1,0:T(8,128)(2,1)S(1)}, bf16[16,8,128]{2,1,0:T(8,128)(2,1)S(1)}, u32[]{:S(2)}, u32[]{:S(2)}) %collective-permute-start.25) | collective-permute-done | bytes 32800 | tf_op jit(solution)/shard_map/ppermute | solution.py:168
  71.0 1.7 %shard_map.43 = f32[8,1024]{1,0:T(8,128)} custom-call(s32[9,8]{1,0:T(8,128)S(1)} %pad_add_fusion.refs_0_, bf16[16,8,128]{2,1,0:T(8,128)(2,1)S(1)} %collective-permute-done.24.refs_1_, bf16[16,8,128]{2,1,0:T(8,128)(2,1)S(1)} %collective-permute-done.25.refs_2_, bf16[8,4,64,128]{3,2,1,0:T(8,128)(2,1)S(1)} %stage_in.1.refs_5_.refs_4_.refs_3_, ...), custom_call_target="tpu_custom_call" | custom-call | tf_op jit(solution)/shard_map/pallas_call | solution.py:108
  (41 shorter events, 7.1 us)
Async XLA Ops:
  0.0 4.0 %copy-start.2 = (s32[1,8,3]{1,0,2:T(1,128)S(1)}, s32[1,8,3]{1,0,2:T(1,128)}, u32[]{:S(2)}) copy-start(s32[1,8,3]{1,0,2:T(1,128)} %param.5) | copy-start | bytes 292
  0.0 2.4 %collective-permute-start.12 = (bf16[8,4,64,128]{3,2,1,0:T(8,128)(2,1)}, bf16[8,4,64,128]{3,2,1,0:T(8,128)(2,1)S(1)}, u32[]{:S(2)}, u32[]{:S(2)}) collective-permute-start(bf16[8,4,64,128]{3,2,1,0:T(8,128)(2,1)} %bitcast.10), channel_id=1, source_target_pairs={{0,4},{1,5},{2,6},{3,7},{4,0},{5,1},{6,2},{7,3},{8,9},{9,8},{10,11... | collective-permute-start | bytes 1572872 | tf_op jit(solution)/shard_map/ppermute | solution.py:168
  0.7 26.7 %collective-permute-start.6 = (bf16[8,4,64,128]{3,2,1,0:T(8,128)(2,1)}, bf16[8,4,64,128]{3,2,1,0:T(8,128)(2,1)S(1)}, u32[]{:S(2)}, u32[]{:S(2)}) collective-permute-start(bf16[8,4,64,128]{3,2,1,0:T(8,128)(2,1)} %bitcast.11), channel_id=1, source_target_pairs={{0,1},{1,0},{2,3},{3,2},{4,5},{5,4},{6,7},{7,6},{8,9},{9,8},{10,11... | collective-permute-start | bytes 1572872 | tf_op jit(solution)/shard_map/ppermute | solution.py:168
  0.7 35.9 %collective-permute-start.15 = (bf16[8,4,64,128]{3,2,1,0:T(8,128)(2,1)}, bf16[8,4,64,128]{3,2,1,0:T(8,128)(2,1)S(1)}, u32[]{:S(2)}, u32[]{:S(2)}) collective-permute-start(bf16[8,4,64,128]{3,2,1,0:T(8,128)(2,1)} %bitcast.12), channel_id=1, source_target_pairs={{0,2},{1,3},{2,0},{3,1},{4,6},{5,7},{6,4},{7,5},{8,9},{9,8},{10,11... | collective-permute-start | bytes 1572872 | tf_op jit(solution)/shard_map/ppermute | solution.py:168
  2.4 43.9 %collective-permute-start.13 = (bf16[8,4,64,128]{3,2,1,0:T(8,128)(2,1)S(1)}, bf16[8,4,64,128]{3,2,1,0:T(8,128)(2,1)S(1)}, u32[]{:S(2)}, u32[]{:S(2)}) collective-permute-start(bf16[8,4,64,128]{3,2,1,0:T(8,128)(2,1)S(1)} %collective-permute-done.12.refs_4_.refs_3_), channel_id=1, source_target_pairs={{0,1},{1,0},{2,3},{3,2},{4,5},{5,4},{6,7},{7,6},{8,9},{9,8},{10,11... | collective-permute-start | bytes 1572872 | tf_op jit(solution)/shard_map/ppermute | solution.py:168
  2.8 58.5 %collective-permute-start.22 = (bf16[8,4,64,128]{3,2,1,0:T(8,128)(2,1)}, bf16[8,4,64,128]{3,2,1,0:T(8,128)(2,1)S(1)}, u32[]{:S(2)}, u32[]{:S(2)}) collective-permute-start(bf16[8,4,64,128]{3,2,1,0:T(8,128)(2,1)} %bitcast.13), channel_id=1, source_target_pairs={{0,1},{1,0},{2,3},{3,2},{4,5},{5,4},{6,7},{7,6},{8,10},{9,11},{10,... | collective-permute-start | bytes 1572872 | tf_op jit(solution)/shard_map/ppermute | solution.py:168
  4.0 12.4 %collective-permute-start.1 = (s32[3,8]{1,0:T(4,128)S(1)}, s32[3,8]{1,0:T(4,128)S(1)}, u32[]{:S(2)}, u32[]{:S(2)}) collective-permute-start(s32[3,8]{1,0:T(4,128)S(1)} %bitcast.19), channel_id=1, source_target_pairs={{0,2},{1,3},{2,0},{3,1},{4,6},{5,7},{6,4},{7,5},{8,10},{9,11},{10,... | collective-permute-start | bytes 296 | tf_op jit(solution)/shard_map/ppermute | solution.py:168
  16.4 1.8 %collective-permute-start = (s32[3,8]{1,0:T(4,128)S(1)}, s32[3,8]{1,0:T(4,128)S(1)}, u32[]{:S(2)}, u32[]{:S(2)}) collective-permute-start(s32[3,8]{1,0:T(4,128)S(1)} %bitcast.20), channel_id=1, source_target_pairs={{0,1},{1,0},{2,3},{3,2},{4,5},{5,4},{6,7},{7,6},{8,9},{9,8},{10,11... | collective-permute-start | bytes 296 | tf_op jit(solution)/shard_map/ppermute | solution.py:168
  18.2 1.4 %collective-permute-start.3 = (f32[8,8,128]{2,1,0:T(8,128)}, f32[8,8,128]{2,1,0:T(8,128)S(1)}, u32[]{:S(2)}, u32[]{:S(2)}) collective-permute-start(f32[8,8,128]{2,1,0:T(8,128)} %bitcast.15), channel_id=1, source_target_pairs={{0,1},{1,0},{2,3},{3,2},{4,5},{5,4},{6,7},{7,6},{8,9},{9,8},{10,11... | collective-permute-start | bytes 98312 | tf_op jit(solution)/shard_map/ppermute | solution.py:168
  19.6 3.0 %collective-permute-start.4 = (f32[8,8,128]{2,1,0:T(8,128)}, f32[8,8,128]{2,1,0:T(8,128)S(1)}, u32[]{:S(2)}, u32[]{:S(2)}) collective-permute-start(f32[8,8,128]{2,1,0:T(8,128)} %bitcast.16), channel_id=1, source_target_pairs={{0,2},{1,3},{2,0},{3,1},{4,6},{5,7},{6,4},{7,5},{8,10},{9,11},{10,... | collective-permute-start | bytes 98312 | tf_op jit(solution)/shard_map/ppermute | solution.py:168
  20.8 1.0 %copy-start = (bf16[1,8,4,64,128]{4,3,2,1,0:T(8,128)(2,1)S(1)}, bf16[1,8,4,64,128]{4,3,2,1,0:T(8,128)(2,1)}, u32[]{:S(2)}) copy-start(bf16[1,8,4,64,128]{4,3,2,1,0:T(8,128)(2,1)} %param.4) | copy-start | bytes 1572868
  21.9 0.8 %copy-start.1 = (f32[1,8,1024]{2,1,0:T(8,128)S(1)}, f32[1,8,1024]{2,1,0:T(8,128)}, u32[]{:S(2)}) copy-start(f32[1,8,1024]{2,1,0:T(8,128)} %param.3) | copy-start | bytes 98308
  22.6 4.7 %collective-permute-start.5 = (f32[8,8,128]{2,1,0:T(8,128)S(1)}, f32[8,8,128]{2,1,0:T(8,128)S(1)}, u32[]{:S(2)}, u32[]{:S(2)}) collective-permute-start(f32[8,8,128]{2,1,0:T(8,128)S(1)} %bitcast.17), channel_id=1, source_target_pairs={{0,3},{1,2},{2,1},{3,0},{4,7},{5,6},{6,5},{7,4},{8,11},{9,10},{10,... | collective-permute-start | bytes 98312 | tf_op jit(solution)/shard_map/ppermute | solution.py:168
  28.5 2.8 %collective-permute-start.7 = (bf16[16,8,128]{2,1,0:T(8,128)(2,1)S(1)}, bf16[16,8,128]{2,1,0:T(8,128)(2,1)S(1)}, u32[]{:S(2)}, u32[]{:S(2)}) collective-permute-start(bf16[16,8,128]{2,1,0:T(8,128)(2,1)S(1)} %get-tuple-element.18), channel_id=1, source_target_pairs={{0,4},{1,5},{2,6},{3,7},{4,0},{5,1},{6,2},{7,3},{8,12},{9,13},{10,... | collective-permute-start | bytes 98312 | tf_op jit(solution)/shard_map/ppermute | solution.py:168
  29.8 3.7 %collective-permute-start.8 = (bf16[16,8,128]{2,1,0:T(8,128)(2,1)S(1)}, bf16[16,8,128]{2,1,0:T(8,128)(2,1)S(1)}, u32[]{:S(2)}, u32[]{:S(2)}) collective-permute-start(bf16[16,8,128]{2,1,0:T(8,128)(2,1)S(1)} %get-tuple-element.18), channel_id=1, source_target_pairs={{0,6},{1,7},{2,4},{3,5},{4,2},{5,3},{6,0},{7,1},{8,14},{9,15},{10,... | collective-permute-start | bytes 98312 | tf_op jit(solution)/shard_map/ppermute | solution.py:168
  34.7 3.1 %collective-permute-start.9 = (bf16[16,8,128]{2,1,0:T(8,128)(2,1)S(1)}, bf16[16,8,128]{2,1,0:T(8,128)(2,1)S(1)}, u32[]{:S(2)}, u32[]{:S(2)}) collective-permute-start(bf16[16,8,128]{2,1,0:T(8,128)(2,1)S(1)} %get-tuple-element.20), channel_id=1, source_target_pairs={{0,1},{1,0},{2,3},{3,2},{4,5},{5,4},{6,7},{7,6},{8,16},{9,17},{10,... | collective-permute-start | bytes 98312 | tf_op jit(solution)/shard_map/ppermute | solution.py:168
  34.7 2.7 %collective-permute-start.2 = (s32[9,8]{1,0:T(8,128)S(1)}, s32[9,8]{1,0:T(8,128)S(1)}, u32[]{:S(2)}, u32[]{:S(2)}) collective-permute-start(s32[9,8]{1,0:T(8,128)S(1)} %pad_add_fusion.refs_0_), channel_id=1, source_target_pairs={{0,4},{1,5},{2,6},{3,7},{4,0},{5,1},{6,2},{7,3},{8,9},{9,8},{10,11... | collective-permute-start | bytes 872 | tf_op jit(solution)/shard_map/ppermute | solution.py:168
  36.6 13.7 %collective-permute-start.17 = (bf16[4,4,64,128]{3,2,1,0:T(8,128)(2,1)S(1)}, bf16[4,4,64,128]{3,2,1,0:T(8,128)(2,1)S(1)}, u32[]{:S(2)}, u32[]{:S(2)}) collective-permute-start(bf16[4,4,64,128]{3,2,1,0:T(8,128)(2,1)S(1)} %slice.12), channel_id=1, source_target_pairs={{0,2},{1,3},{2,0},{3,1},{4,6},{5,7},{6,4},{7,5},{8,9},{9,8},{10,11... | collective-permute-start | bytes 786440 | tf_op jit(solution)/shard_map/ppermute | solution.py:168
  37.4 13.7 %collective-permute-start.18 = (bf16[4,4,64,128]{3,2,1,0:T(8,128)(2,1)S(1)}, bf16[4,4,64,128]{3,2,1,0:T(8,128)(2,1)S(1)}, u32[]{:S(2)}, u32[]{:S(2)}) collective-permute-start(bf16[4,4,64,128]{3,2,1,0:T(8,128)(2,1)S(1)} %slice.13), channel_id=1, source_target_pairs={{0,4},{1,5},{2,6},{3,7},{4,0},{5,1},{6,2},{7,3},{8,9},{9,8},{10,11... | collective-permute-start | bytes 786440 | tf_op jit(solution)/shard_map/ppermute | solution.py:168
  37.8 3.7 %collective-permute-start.10 = (bf16[16,8,128]{2,1,0:T(8,128)(2,1)S(1)}, bf16[16,8,128]{2,1,0:T(8,128)(2,1)S(1)}, u32[]{:S(2)}, u32[]{:S(2)}) collective-permute-start(bf16[16,8,128]{2,1,0:T(8,128)(2,1)S(1)} %get-tuple-element.20), channel_id=1, source_target_pairs={{0,1},{1,0},{2,3},{3,2},{4,5},{5,4},{6,7},{7,6},{8,18},{9,19},{10,... | collective-permute-start | bytes 98312 | tf_op jit(solution)/shard_map/ppermute | solution.py:168
  41.4 4.9 %collective-permute-start.11 = (f32[32,8,128]{2,1,0:T(8,128)S(1)}, f32[32,8,128]{2,1,0:T(8,128)S(1)}, u32[]{:S(2)}, u32[]{:S(2)}) collective-permute-start(f32[32,8,128]{2,1,0:T(8,128)S(1)} %get-tuple-element.19.refs_3_), channel_id=1, source_target_pairs={{0,4},{1,5},{2,6},{3,7},{4,0},{5,1},{6,2},{7,3},{8,9},{9,8},{10,11... | collective-permute-start | bytes 393224 | tf_op jit(solution)/shard_map/ppermute | solution.py:168
  47.5 1.3 %collective-permute-start.14 = (bf16[16,8,128]{2,1,0:T(8,128)(2,1)S(1)}, bf16[16,8,128]{2,1,0:T(8,128)(2,1)S(1)}, u32[]{:S(2)}, u32[]{:S(2)}) collective-permute-start(bf16[16,8,128]{2,1,0:T(8,128)(2,1)S(1)} %get-tuple-element.21.refs_1_), channel_id=1, source_target_pairs={{0,2},{1,3},{2,0},{3,1},{4,6},{5,7},{6,4},{7,5},{8,9},{9,8},{10,11... | collective-permute-start | bytes 98312 | tf_op jit(solution)/shard_map/ppermute | solution.py:168
  47.9 3.3 %collective-permute-start.19 = (f32[8,8,128]{2,1,0:T(8,128)S(1)}, f32[8,8,128]{2,1,0:T(8,128)S(1)}, u32[]{:S(2)}, u32[]{:S(2)}) collective-permute-start(f32[8,8,128]{2,1,0:T(8,128)S(1)} %get-tuple-element.23.refs_6_), channel_id=1, source_target_pairs={{0,2},{1,3},{2,0},{3,1},{4,6},{5,7},{6,4},{7,5},{8,9},{9,8},{10,11... | collective-permute-start | bytes 98312 | tf_op jit(solution)/shard_map/ppermute | solution.py:168
  49.9 1.3 %collective-permute-start.16 = (bf16[16,8,128]{2,1,0:T(8,128)(2,1)S(1)}, bf16[16,8,128]{2,1,0:T(8,128)(2,1)S(1)}, u32[]{:S(2)}, u32[]{:S(2)}) collective-permute-start(bf16[16,8,128]{2,1,0:T(8,128)(2,1)S(1)} %get-tuple-element.22.refs_1_), channel_id=1, source_target_pairs={{0,1},{1,0},{2,3},{3,2},{4,5},{5,4},{6,7},{7,6},{8,9},{9,8},{10,11... | collective-permute-start | bytes 98312 | tf_op jit(solution)/shard_map/ppermute | solution.py:168
  50.3 11.1 %collective-permute-start.23 = (f32[8,8,128]{2,1,0:T(8,128)S(1)}, f32[8,8,128]{2,1,0:T(8,128)S(1)}, u32[]{:S(2)}, u32[]{:S(2)}) collective-permute-start(f32[8,8,128]{2,1,0:T(8,128)S(1)} %get-tuple-element.25.refs_5_), channel_id=1, source_target_pairs={{0,2},{1,3},{2,0},{3,1},{4,6},{5,7},{6,4},{7,5},{8,10},{9,11},{10,... | collective-permute-start | bytes 98312 | tf_op jit(solution)/shard_map/ppermute | solution.py:168
  52.3 9.7 %collective-permute-start.20 = (bf16[16,8,128]{2,1,0:T(8,128)(2,1)S(1)}, bf16[16,8,128]{2,1,0:T(8,128)(2,1)S(1)}, u32[]{:S(2)}, u32[]{:S(2)}) collective-permute-start(bf16[16,8,128]{2,1,0:T(8,128)(2,1)S(1)} %get-tuple-element.24), channel_id=1, source_target_pairs={{0,1},{1,0},{2,3},{3,2},{4,5},{5,4},{6,7},{7,6},{8,16},{9,17},{10,... | collective-permute-start | bytes 98312 | tf_op jit(solution)/shard_map/ppermute | solution.py:168
  60.7 3.9 %collective-permute-start.21 = (bf16[16,8,128]{2,1,0:T(8,128)(2,1)S(1)}, bf16[16,8,128]{2,1,0:T(8,128)(2,1)S(1)}, u32[]{:S(2)}, u32[]{:S(2)}) collective-permute-start(bf16[16,8,128]{2,1,0:T(8,128)(2,1)S(1)} %get-tuple-element.24), channel_id=1, source_target_pairs={{0,1},{1,0},{2,3},{3,2},{4,5},{5,4},{6,7},{7,6},{8,17},{9,16},{10,... | collective-permute-start | bytes 98312 | tf_op jit(solution)/shard_map/ppermute | solution.py:168
  61.0 6.8 %collective-permute-start.26 = (f32[8,8,128]{2,1,0:T(8,128)S(1)}, f32[8,8,128]{2,1,0:T(8,128)S(1)}, u32[]{:S(2)}, u32[]{:S(2)}) collective-permute-start(f32[8,8,128]{2,1,0:T(8,128)S(1)} %slice.11), channel_id=1, source_target_pairs={{0,4},{1,5},{2,6},{3,7},{4,0},{5,1},{6,2},{7,3},{8,9},{9,8},{10,11... | collective-permute-start | bytes 98312 | tf_op jit(solution)/shard_map/ppermute | solution.py:168
  65.7 2.8 %collective-permute-start.24 = (bf16[16,8,128]{2,1,0:T(8,128)(2,1)S(1)}, bf16[16,8,128]{2,1,0:T(8,128)(2,1)S(1)}, u32[]{:S(2)}, u32[]{:S(2)}) collective-permute-start(bf16[16,8,128]{2,1,0:T(8,128)(2,1)S(1)} %get-tuple-element.26), channel_id=1, source_target_pairs={{0,4},{1,5},{2,6},{3,7},{4,0},{5,1},{6,2},{7,3},{8,12},{9,13},{10,... | collective-permute-start | bytes 98312 | tf_op jit(solution)/shard_map/ppermute | solution.py:168
  67.1 4.0 %collective-permute-start.25 = (bf16[16,8,128]{2,1,0:T(8,128)(2,1)S(1)}, bf16[16,8,128]{2,1,0:T(8,128)(2,1)S(1)}, u32[]{:S(2)}, u32[]{:S(2)}) collective-permute-start(bf16[16,8,128]{2,1,0:T(8,128)(2,1)S(1)} %get-tuple-element.26), channel_id=1, source_target_pairs={{0,5},{1,4},{2,7},{3,6},{4,1},{5,0},{6,3},{7,2},{8,13},{9,12},{10,... | collective-permute-start | bytes 98312 | tf_op jit(solution)/shard_map/ppermute | solution.py:168

commit v4 on v3

--- a/solution.py
+++ b/solution.py
@@ -31,7 +31,7 @@
     (vec,) = refs
     width = blocks[0].shape[-1]
     half = width // 2
-    off, nb = patterns.shape[0] // 3, patterns.shape[1]
+    off, nb = patterns.shape[0] // 2, patterns.shape[1]
     base = lax.axis_index("tile") * nb
     place = place_of(lax.axis_index("sweep"))
     lane = lax.broadcasted_iota(jnp.int32, (1, 1, width), 2)
@@ -53,7 +53,7 @@
         group, local = divmod(row, nb)
         flip = row_flips[group]
         slots = [flip * nb + local]
-        slots += [patterns[flip * off + j, local] ^ base for j in range(off)]
+        slots += [patterns[group * off + j, local] ^ base for j in range(off)]
         mats = jnp.concatenate([ref[at, j] for j in range(off + 1)], axis=1)
         inputs = jnp.concatenate([vec[slot] for slot in slots], axis=1)
         out = lax.dot_general(
@@ -62,7 +62,7 @@
         rhs = out.shape[0] // 2
         result = jnp.concatenate([out[:rhs], out[rhs:]], axis=1)
         if stage == 4:
-            result = states[group][local] + result
+            result = states[0][row] + result
         if stage == 5:
             sweep = lax.axis_index("sweep")
             inner = (sweep >= SEG // 2) & (sweep < lax.axis_size("sweep") - SEG // 2)
@@ -86,7 +86,7 @@
     rows = sum(b.shape[0] for b in blocks)
     has_msg = stage < 2 * SEG - 2
     if has_msg:
-        kept = nb if stage < 3 else rows
+        kept = nb if stage < 2 else rows
         out_shape = [
             jax.ShapeDtypeStruct((kept, rhs, width), jnp.float32),
             jax.ShapeDtypeStruct((rows, rhs, width), jnp.bfloat16),
@@ -136,7 +136,7 @@
     sweeps, tiles = lax.axis_size("sweep"), lax.axis_size("tile")
     own_blocks, own_pattern = blocks[0], pattern[0].T
     nb, width = own_blocks.shape[0], own_blocks.shape[-1]
-    rhs, hn = sources.shape[1], nb // 2
+    rhs = sources.shape[1]
     layers = range(sweeps)
 
     def place(layer):
@@ -179,51 +179,47 @@
     src_pieces += [(swap(src_own, everyone, f), (f,)) for f in range(1, tiles)]
     core_blocks = swap(own_blocks, everyone, 1)
     core_pattern = swap(own_pattern, everyone, 1)
-    x_pattern = swap(own_pattern, everyone, 2)
+    core_patterns = jnp.concatenate([own_pattern, core_pattern], axis=0)
     y_blocks = swap(own_blocks, late_y, 0)
     x_blocks = swap(own_blocks, late, 2)
     own = stage_in(own_blocks)
 
-    patterns = jnp.concatenate([own_pattern, core_pattern, x_pattern], axis=0)
-    core_rows = dict(patterns=patterns, row_flips=(0, 1))
+    core_rows = dict(patterns=core_patterns, row_flips=(0, 1))
     down_0, msg, src_all = layer_apply(
         0, recs=src_pieces, blocks=[own, core_blocks], keep_src=True, **core_rows
     )
     recs = hop(msg, start_y, even_flips, 1)
 
-    y_patterns = swap(patterns, late_y, 0)
+    y_patterns = swap(core_patterns, late_y, 0)
     src_other = swap(src_all, late_y, 0)
-    diag_0 = swap(y_blocks[:hn], late, 2)
-    diag_1 = swap(x_blocks[hn:], late_y, 0)
+    later_pattern = lax.optimization_barrier((own_pattern, msg))[0]
+    x_pattern = swap(later_pattern, everyone, 2)
+    x_patterns = jnp.concatenate([later_pattern, x_pattern], axis=0)
 
     down_1, msg = layer_apply(
         1, recs=recs, blocks=[own, core_blocks], src=src_all, **core_rows
     )
     recs = hop(msg, across_z, even_flips, 1)
+    y_core = swap(y_blocks, everyone, 1)
     down_1_x = swap(down_1, starts, 2)
     x_late = swap(own_blocks, early, 2)
 
-    y_core = swap(y_blocks, everyone, 1)
-    down_2, msg = layer_apply(2, y_patterns, (0, 1), recs, [y_blocks, y_core], src=src_other)
+    other_rows = dict(patterns=y_patterns, row_flips=(0, 1), blocks=[y_blocks, y_core])
+    x_rows = dict(patterns=x_patterns, row_flips=(0, 2))
+    down_2, msg = layer_apply(2, recs=recs, src=src_other, **other_rows)
     recs = hop(msg, late, even_flips, 1, own=True)
-    down_2_x = swap(down_2, late, 2)
-    own_rows = dict(patterns=patterns, row_flips=(0, 2))
-    down_3, msg = layer_apply(
-        3, recs=recs, blocks=[own, x_blocks], src=src_all, **own_rows
-    )
+    down_3, msg = layer_apply(3, recs=recs, blocks=[own, x_blocks], src=src_all, **x_rows)
     recs = hop(msg, everyone, core_flips, 2, own=True)
-    up_2, msg = layer_apply(
-        4, y_patterns, (0, 2), recs, [y_blocks, diag_0, diag_1], states=[down_2, down_2_x]
-    )
-    recs = hop(msg, across_z, core_flips, 2)
+    up_2, msg = layer_apply(4, recs=recs, states=[down_2], **other_rows)
+    recs = hop(msg, across_z, even_flips, 1)
     up_2_own = swap(up_2[:nb], late_y, 0)
     up_1, msg = layer_apply(
-        5, recs=recs, blocks=[own, x_late], states=[down_1, down_1_x], **own_rows
+        5, recs=recs, blocks=[own, x_late], states=[down_1, down_1_x], **x_rows
     )
     recs = hop(msg, across_y, core_flips, 2)
     (upper,) = layer_apply(
         6,
-        patterns=patterns,
+        patterns=core_patterns,
         row_flips=(0,),
         recs=recs,
         blocks=[own],

time: 72.9 us -> 73.1 us (level)
  starting transfers between devices: 29.8 us -> 37.5 us
  waiting for transfers between devices: 33 us -> 26 us
    ppermute x27 -> x24, starting transfers between devices: 29.8 us -> 37.5 us  [swap(): return lax.ppermute(value, AXES, route)]
    ppermute x27 -> x24, waiting for transfers between devices: 33 us -> 26 us  [swap(): return lax.ppermute(value, AXES, route)]
  transfers between devices with their start and end apart: 27 -> 24, of which waited for: 16 -> 13; matrix products, arithmetic and copies ran while one was open for 0% -> 0% of each run, Pallas kernels for 10% -> 9%
where the time goes in v4:
time: 73.1 us; the launch traced here: 72.9 us
  starting transfers between devices  37.5 us (51%)
  waiting for transfers between devices  26 us (36%)
  Pallas kernels  8.22 us (11%)
  local copies, waits for them, and re-layouts  1.05 us (1%)
    ppermute x24, starting transfers between devices, swap(): return lax.ppermute(value, AXES, route)  37.5 us
    ppermute x24, waiting for transfers between devices, swap(): return lax.ppermute(value, AXES, route)  26 us
    pallas_call x7, Pallas kernels, layer_apply(): pl.pallas_call(functools.partial(apply_kernel, stage, plan), in_specs=[SM...  8.18 us
  transfers between devices with their start and end apart: 24, of which 13 were waited for; matrix products, arithmetic and copies ran while one was open for 0% of the time, Pallas kernels for 9%

profile of v4, /device:TPU:9, one launch (start us, length us, event | category | flops | bytes accessed | tf_op | source)
XLA Modules:
  0.0 72.9 jit_solution(5729153331557915431)
XLA Ops:
  0.7 1.7 %collective-permute-done.12.refs_4_.refs_3_ = bf16[8,4,64,128]{3,2,1,0:T(8,128)(2,1)S(1)} collective-permute-done((bf16[8,4,64,128]{3,2,1,0:T(8,128)(2,1)}, bf16[8,4,64,128]{3,2,1,0:T(8,128)(2,1)S(1)}, u32[]{:S(2)}, u32[]{:S(2)}) %collective-permute-start.12) | collective-permute-done | bytes 524320 | tf_op jit(solution)/shard_map/ppermute | solution.py:168
  2.9 1.2 %collective-permute-start.19 = (bf16[8,4,64,128]{3,2,1,0:T(8,128)(2,1)}, bf16[8,4,64,128]{3,2,1,0:T(8,128)(2,1)S(1)}, u32[]{:S(2)}, u32[]{:S(2)}) collective-permute-start(bf16[8,4,64,128]{3,2,1,0:T(8,128)(2,1)} %bitcast.13), channel_id=1, source_target_pairs={{0,1},{1,0},{2,3},{3,2},{4,5},{5,4},{6,7},{7,6},{8,10},{9,11},{10,... | collective-permute-start | bytes 1572872 | tf_op jit(solution)/shard_map/ppermute | solution.py:168
  6.0 1.1 %collective-permute-done.1.refs_2_ = f32[8,8,128]{2,1,0:T(8,128)S(1)} collective-permute-done((f32[8,8,128]{2,1,0:T(8,128)}, f32[8,8,128]{2,1,0:T(8,128)S(1)}, u32[]{:S(2)}, u32[]{:S(2)}) %collective-permute-start.1) | collective-permute-done | bytes 32800 | tf_op jit(solution)/shard_map/ppermute | solution.py:168
  7.7 1.0 %copy-done = bf16[1,8,4,64,128]{4,3,2,1,0:T(8,128)(2,1)S(1)} copy-done((bf16[1,8,4,64,128]{4,3,2,1,0:T(8,128)(2,1)S(1)}, bf16[1,8,4,64,128]{4,3,2,1,0:T(8,128)(2,1)}, u32[]{:S(2)}) %copy-start) | copy-done | bytes 524312
  8.8 8.1 %collective-permute-done.2.refs_3_ = f32[8,8,128]{2,1,0:T(8,128)S(1)} collective-permute-done((f32[8,8,128]{2,1,0:T(8,128)}, f32[8,8,128]{2,1,0:T(8,128)S(1)}, u32[]{:S(2)}, u32[]{:S(2)}) %collective-permute-start.2) | collective-permute-done | bytes 32800 | tf_op jit(solution)/shard_map/ppermute | solution.py:168
  17.0 2.3 %collective-permute-start.3 = (f32[8,8,128]{2,1,0:T(8,128)S(1)}, f32[8,8,128]{2,1,0:T(8,128)S(1)}, u32[]{:S(2)}, u32[]{:S(2)}) collective-permute-start(f32[8,8,128]{2,1,0:T(8,128)S(1)} %bitcast.17), channel_id=1, source_target_pairs={{0,3},{1,2},{2,1},{3,0},{4,7},{5,6},{6,5},{7,4},{8,11},{9,10},{10,... | collective-permute-start | bytes 98312 | tf_op jit(solution)/shard_map/ppermute | solution.py:168
  19.3 2.1 %collective-permute-done.3.refs_4_ = f32[8,8,128]{2,1,0:T(8,128)S(1)} collective-permute-done((f32[8,8,128]{2,1,0:T(8,128)S(1)}, f32[8,8,128]{2,1,0:T(8,128)S(1)}, u32[]{:S(2)}, u32[]{:S(2)}) %collective-permute-start.3) | collective-permute-done | bytes 32800 | tf_op jit(solution)/shard_map/ppermute | solution.py:168
  21.4 1.1 %shard_map.37 = (f32[8,8,128]{2,1,0:T(8,128)S(1)}, bf16[16,8,128]{2,1,0:T(8,128)(2,1)S(1)}, f32[32,8,128]{2,1,0:T(8,128)S(1)}) custom-call(s32[6,8]{1,0:T(8,128)S(1)} %pad_add_fusion.refs_0_, f32[8,8,128]{2,1,0:T(8,128)S(1)} %bitcast.18, f32[8,8,128]{2,1,0:T(8,128)S(1)} %collective-permute-done.1.refs_2_, f32[8,8,128]{2,1,0:T(8,128)S(1)} %collective-permute-done.2.refs_3_, ...), custom_call_target="tpu_custom_call" | custom-call | tf_op jit(solution)/shard_map/pallas_call | solution.py:108
  22.6 1.3 %collective-permute-start.7 = (bf16[16,8,128]{2,1,0:T(8,128)(2,1)S(1)}, bf16[16,8,128]{2,1,0:T(8,128)(2,1)S(1)}, u32[]{:S(2)}, u32[]{:S(2)}) collective-permute-start(bf16[16,8,128]{2,1,0:T(8,128)(2,1)S(1)} %get-tuple-element.19), channel_id=1, source_target_pairs={{0,4},{1,5},{2,6},{3,7},{4,0},{5,1},{6,2},{7,3},{8,12},{9,13},{10,... | collective-permute-start | bytes 98312 | tf_op jit(solution)/shard_map/ppermute | solution.py:168
  24.5 0.8 %collective-permute-done.7.refs_1_ = bf16[16,8,128]{2,1,0:T(8,128)(2,1)S(1)} collective-permute-done((bf16[16,8,128]{2,1,0:T(8,128)(2,1)S(1)}, bf16[16,8,128]{2,1,0:T(8,128)(2,1)S(1)}, u32[]{:S(2)}, u32[]{:S(2)}) %collective-permute-start.7) | collective-permute-done | bytes 32800 | tf_op jit(solution)/shard_map/ppermute | solution.py:168
  25.4 1.0 %collective-permute-start.8 = (bf16[16,8,128]{2,1,0:T(8,128)(2,1)S(1)}, bf16[16,8,128]{2,1,0:T(8,128)(2,1)S(1)}, u32[]{:S(2)}, u32[]{:S(2)}) collective-permute-start(bf16[16,8,128]{2,1,0:T(8,128)(2,1)S(1)} %get-tuple-element.19), channel_id=1, source_target_pairs={{0,6},{1,7},{2,4},{3,5},{4,2},{5,3},{6,0},{7,1},{8,14},{9,15},{10,... | collective-permute-start | bytes 98312 | tf_op jit(solution)/shard_map/ppermute | solution.py:168
  26.4 2.6 %collective-permute-done.8.refs_2_ = bf16[16,8,128]{2,1,0:T(8,128)(2,1)S(1)} collective-permute-done((bf16[16,8,128]{2,1,0:T(8,128)(2,1)S(1)}, bf16[16,8,128]{2,1,0:T(8,128)(2,1)S(1)}, u32[]{:S(2)}, u32[]{:S(2)}) %collective-permute-start.8) | collective-permute-done | bytes 32800 | tf_op jit(solution)/shard_map/ppermute | solution.py:168
  29.0 2.7 %collective-permute-start.6 = (s32[6,8]{1,0:T(8,128)S(1)}, s32[6,8]{1,0:T(8,128)S(1)}, u32[]{:S(2)}, u32[]{:S(2)}) collective-permute-start(s32[6,8]{1,0:T(8,128)S(1)} %pad_add_fusion.refs_0_), channel_id=1, source_target_pairs={{0,4},{1,5},{2,6},{3,7},{4,0},{5,1},{6,2},{7,3},{8,9},{9,8},{10,11... | collective-permute-start | bytes 584 | tf_op jit(solution)/shard_map/ppermute | solution.py:168
  31.7 1.1 %shard_map.38 = (f32[8,8,128]{2,1,0:T(8,128)S(1)}, bf16[16,8,128]{2,1,0:T(8,128)(2,1)S(1)}) custom-call(s32[6,8]{1,0:T(8,128)S(1)} %pad_add_fusion.refs_0_, bf16[16,8,128]{2,1,0:T(8,128)(2,1)S(1)} %collective-permute-done.7.refs_1_, bf16[16,8,128]{2,1,0:T(8,128)(2,1)S(1)} %collective-permute-done.8.refs_2_, f32[32,8,128]{2,1,0:T(8,128)S(1)} %get-tuple-element.21.refs_3_, ...), custom_call_target="tpu_custom_call" | custom-call | tf_op jit(solution)/shard_map/pallas_call | solution.py:108
  32.8 9.1 %collective-permute-start.10 = (bf16[16,8,128]{2,1,0:T(8,128)(2,1)S(1)}, bf16[16,8,128]{2,1,0:T(8,128)(2,1)S(1)}, u32[]{:S(2)}, u32[]{:S(2)}) collective-permute-start(bf16[16,8,128]{2,1,0:T(8,128)(2,1)S(1)} %get-tuple-element.22), channel_id=1, source_target_pairs={{0,1},{1,0},{2,3},{3,2},{4,5},{5,4},{6,7},{7,6},{8,18},{9,19},{10,... | collective-permute-start | bytes 98312 | tf_op jit(solution)/shard_map/ppermute | solution.py:168
  42.0 1.3 %collective-permute-done.10.refs_2_ = bf16[16,8,128]{2,1,0:T(8,128)(2,1)S(1)} collective-permute-done((bf16[16,8,128]{2,1,0:T(8,128)(2,1)S(1)}, bf16[16,8,128]{2,1,0:T(8,128)(2,1)S(1)}, u32[]{:S(2)}, u32[]{:S(2)}) %collective-permute-start.10) | collective-permute-done | bytes 32800 | tf_op jit(solution)/shard_map/ppermute | solution.py:168
  43.3 1.6 %collective-permute-start.9 = (bf16[16,8,128]{2,1,0:T(8,128)(2,1)S(1)}, bf16[16,8,128]{2,1,0:T(8,128)(2,1)S(1)}, u32[]{:S(2)}, u32[]{:S(2)}) collective-permute-start(bf16[16,8,128]{2,1,0:T(8,128)(2,1)S(1)} %get-tuple-element.22), channel_id=1, source_target_pairs={{0,1},{1,0},{2,3},{3,2},{4,5},{5,4},{6,7},{7,6},{8,16},{9,17},{10,... | collective-permute-start | bytes 98312 | tf_op jit(solution)/shard_map/ppermute | solution.py:168
  44.9 1.3 %collective-permute-done.9.refs_1_ = bf16[16,8,128]{2,1,0:T(8,128)(2,1)S(1)} collective-permute-done((bf16[16,8,128]{2,1,0:T(8,128)(2,1)S(1)}, bf16[16,8,128]{2,1,0:T(8,128)(2,1)S(1)}, u32[]{:S(2)}, u32[]{:S(2)}) %collective-permute-start.9) | collective-permute-done | bytes 32800 | tf_op jit(solution)/shard_map/ppermute | solution.py:168
  46.2 1.1 %collective-permute-start.5 = (s32[3,8]{1,0:T(4,128)S(1)}, s32[3,8]{1,0:T(4,128)S(1)}, u32[]{:S(2)}, u32[]{:S(2)}) collective-permute-start(s32[3,8]{1,0:T(4,128)S(1)} %bitcast.21), channel_id=1, source_target_pairs={{0,2},{1,3},{2,0},{3,1},{4,6},{5,7},{6,4},{7,5},{8,10},{9,11},{10,... | collective-permute-start | bytes 296 | tf_op jit(solution)/shard_map/ppermute | solution.py:168
  47.2 1.1 %shard_map.39 = (f32[16,8,128]{2,1,0:T(8,128)S(1)}, bf16[16,8,128]{2,1,0:T(8,128)(2,1)S(1)}) custom-call(s32[6,8]{1,0:T(8,128)S(1)} %collective-permute-done.6.refs_0_, bf16[16,8,128]{2,1,0:T(8,128)(2,1)S(1)} %collective-permute-done.9.refs_1_, bf16[16,8,128]{2,1,0:T(8,128)(2,1)S(1)} %collective-permute-done.10.refs_2_, ...), custom_call_target="tpu_custom_call" | custom-call | tf_op jit(solution)/shard_map/pallas_call | solution.py:108
  48.3 3.5 %collective-permute-start.14 = (bf16[16,8,128]{2,1,0:T(8,128)(2,1)S(1)}, bf16[16,8,128]{2,1,0:T(8,128)(2,1)S(1)}, u32[]{:S(2)}, u32[]{:S(2)}) collective-permute-start(bf16[16,8,128]{2,1,0:T(8,128)(2,1)S(1)} %get-tuple-element.23.refs_1_), channel_id=1, source_target_pairs={{0,2},{1,3},{2,0},{3,1},{4,6},{5,7},{6,4},{7,5},{8,9},{9,8},{10,11... | collective-permute-start | bytes 98312 | tf_op jit(solution)/shard_map/ppermute | solution.py:168
  51.8 0.8 %collective-permute-done.14.refs_2_ = bf16[16,8,128]{2,1,0:T(8,128)(2,1)S(1)} collective-permute-done((bf16[16,8,128]{2,1,0:T(8,128)(2,1)S(1)}, bf16[16,8,128]{2,1,0:T(8,128)(2,1)S(1)}, u32[]{:S(2)}, u32[]{:S(2)}) %collective-permute-start.14) | collective-permute-done | bytes 32800 | tf_op jit(solution)/shard_map/ppermute | solution.py:168
  52.7 1.1 %shard_map.40 = (f32[16,8,128]{2,1,0:T(8,128)S(1)}, bf16[16,8,128]{2,1,0:T(8,128)(2,1)S(1)}) custom-call(s32[6,8]{1,0:T(8,128)S(1)} %pad_add_fusion.1.refs_0_, bf16[16,8,128]{2,1,0:T(8,128)(2,1)S(1)} %get-tuple-element.23.refs_1_, bf16[16,8,128]{2,1,0:T(8,128)(2,1)S(1)} %collective-permute-done.14.refs_2_, f32[32,8,128]{2,1,0:T(8,128)S(1)} %get-tuple-element.21.refs_3_, ...), custom_call_target="tpu_custom_call" | custom-call | tf_op jit(solution)/shard_map/pallas_call | solution.py:108
  54.2 1.0 %collective-permute-start.20 = (f32[8,8,128]{2,1,0:T(8,128)S(1)}, f32[8,8,128]{2,1,0:T(8,128)S(1)}, u32[]{:S(2)}, u32[]{:S(2)}) collective-permute-start(f32[8,8,128]{2,1,0:T(8,128)S(1)} %get-tuple-element.27.refs_5_), channel_id=1, source_target_pairs={{0,2},{1,3},{2,0},{3,1},{4,6},{5,7},{6,4},{7,5},{8,10},{9,11},{10,... | collective-permute-start | bytes 98312 | tf_op jit(solution)/shard_map/ppermute | solution.py:168
  55.2 1.1 %shard_map.41 = (f32[16,8,128]{2,1,0:T(8,128)S(1)}, bf16[16,8,128]{2,1,0:T(8,128)(2,1)S(1)}) custom-call(s32[6,8]{1,0:T(8,128)S(1)} %collective-permute-done.6.refs_0_, bf16[16,8,128]{2,1,0:T(8,128)(2,1)S(1)} %get-tuple-element.24.refs_1_, bf16[16,8,128]{2,1,0:T(8,128)(2,1)S(1)} %collective-permute-done.16.refs_2_, ...), custom_call_target="tpu_custom_call" | custom-call | tf_op jit(solution)/shard_map/pallas_call | solution.py:108
  56.3 4.4 %collective-permute-start.17 = (bf16[16,8,128]{2,1,0:T(8,128)(2,1)S(1)}, bf16[16,8,128]{2,1,0:T(8,128)(2,1)S(1)}, u32[]{:S(2)}, u32[]{:S(2)}) collective-permute-start(bf16[16,8,128]{2,1,0:T(8,128)(2,1)S(1)} %get-tuple-element.26), channel_id=1, source_target_pairs={{0,1},{1,0},{2,3},{3,2},{4,5},{5,4},{6,7},{7,6},{8,16},{9,17},{10,... | collective-permute-start | bytes 98312 | tf_op jit(solution)/shard_map/ppermute | solution.py:168
  61.9 2.4 %collective-permute-done.18.refs_2_ = bf16[16,8,128]{2,1,0:T(8,128)(2,1)S(1)} collective-permute-done((bf16[16,8,128]{2,1,0:T(8,128)(2,1)S(1)}, bf16[16,8,128]{2,1,0:T(8,128)(2,1)S(1)}, u32[]{:S(2)}, u32[]{:S(2)}) %collective-permute-start.18) | collective-permute-done | bytes 32800 | tf_op jit(solution)/shard_map/ppermute | solution.py:168
  64.3 1.1 %shard_map.42 = (f32[16,8,128]{2,1,0:T(8,128)S(1)}, bf16[16,8,128]{2,1,0:T(8,128)(2,1)S(1)}) custom-call(s32[6,8]{1,0:T(8,128)S(1)} %pad_add_fusion.1.refs_0_, bf16[16,8,128]{2,1,0:T(8,128)(2,1)S(1)} %collective-permute-done.17.refs_1_, bf16[16,8,128]{2,1,0:T(8,128)(2,1)S(1)} %collective-permute-done.18.refs_2_, ...), custom_call_target="tpu_custom_call" | custom-call | tf_op jit(solution)/shard_map/pallas_call | solution.py:108
  65.4 0.9 %collective-permute-start.21 = (bf16[16,8,128]{2,1,0:T(8,128)(2,1)S(1)}, bf16[16,8,128]{2,1,0:T(8,128)(2,1)S(1)}, u32[]{:S(2)}, u32[]{:S(2)}) collective-permute-start(bf16[16,8,128]{2,1,0:T(8,128)(2,1)S(1)} %get-tuple-element.28), channel_id=1, source_target_pairs={{0,4},{1,5},{2,6},{3,7},{4,0},{5,1},{6,2},{7,3},{8,12},{9,13},{10,... | collective-permute-start | bytes 98312 | tf_op jit(solution)/shard_map/ppermute | solution.py:168
  66.3 2.6 %collective-permute-start.22 = (bf16[16,8,128]{2,1,0:T(8,128)(2,1)S(1)}, bf16[16,8,128]{2,1,0:T(8,128)(2,1)S(1)}, u32[]{:S(2)}, u32[]{:S(2)}) collective-permute-start(bf16[16,8,128]{2,1,0:T(8,128)(2,1)S(1)} %get-tuple-element.28), channel_id=1, source_target_pairs={{0,5},{1,4},{2,7},{3,6},{4,1},{5,0},{6,3},{7,2},{8,13},{9,12},{10,... | collective-permute-start | bytes 98312 | tf_op jit(solution)/shard_map/ppermute | solution.py:168
  68.9 2.4 %collective-permute-done.22.refs_2_ = bf16[16,8,128]{2,1,0:T(8,128)(2,1)S(1)} collective-permute-done((bf16[16,8,128]{2,1,0:T(8,128)(2,1)S(1)}, bf16[16,8,128]{2,1,0:T(8,128)(2,1)S(1)}, u32[]{:S(2)}, u32[]{:S(2)}) %collective-permute-start.22) | collective-permute-done | bytes 32800 | tf_op jit(solution)/shard_map/ppermute | solution.py:168
  71.3 1.6 %shard_map.43 = f32[8,1024]{1,0:T(8,128)} custom-call(s32[6,8]{1,0:T(8,128)S(1)} %pad_add_fusion.refs_0_, bf16[16,8,128]{2,1,0:T(8,128)(2,1)S(1)} %collective-permute-done.21.refs_1_, bf16[16,8,128]{2,1,0:T(8,128)(2,1)S(1)} %collective-permute-done.22.refs_2_, bf16[8,4,64,128]{3,2,1,0:T(8,128)(2,1)S(1)} %stage_in.1.refs_5_.refs_4_.refs_3_, ...), custom_call_target="tpu_custom_call" | custom-call | tf_op jit(solution)/shard_map/pallas_call | solution.py:108
  (34 shorter events, 6.3 us)
Async XLA Ops:
  0.0 4.2 %copy-start.2 = (s32[1,8,3]{1,0,2:T(1,128)S(1)}, s32[1,8,3]{1,0,2:T(1,128)}, u32[]{:S(2)}) copy-start(s32[1,8,3]{1,0,2:T(1,128)} %param.5) | copy-start | bytes 292
  0.0 2.4 %collective-permute-start.12 = (bf16[8,4,64,128]{3,2,1,0:T(8,128)(2,1)}, bf16[8,4,64,128]{3,2,1,0:T(8,128)(2,1)S(1)}, u32[]{:S(2)}, u32[]{:S(2)}) collective-permute-start(bf16[8,4,64,128]{3,2,1,0:T(8,128)(2,1)} %bitcast.10), channel_id=1, source_target_pairs={{0,4},{1,5},{2,6},{3,7},{4,0},{5,1},{6,2},{7,3},{8,9},{9,8},{10,11... | collective-permute-start | bytes 1572872 | tf_op jit(solution)/shard_map/ppermute | solution.py:168
  0.7 20.8 %collective-permute-start.4 = (bf16[8,4,64,128]{3,2,1,0:T(8,128)(2,1)}, bf16[8,4,64,128]{3,2,1,0:T(8,128)(2,1)S(1)}, u32[]{:S(2)}, u32[]{:S(2)}) collective-permute-start(bf16[8,4,64,128]{3,2,1,0:T(8,128)(2,1)} %bitcast.11), channel_id=1, source_target_pairs={{0,1},{1,0},{2,3},{3,2},{4,5},{5,4},{6,7},{7,6},{8,9},{9,8},{10,11... | collective-permute-start | bytes 1572872 | tf_op jit(solution)/shard_map/ppermute | solution.py:168
  2.4 44.8 %collective-permute-start.13 = (bf16[8,4,64,128]{3,2,1,0:T(8,128)(2,1)S(1)}, bf16[8,4,64,128]{3,2,1,0:T(8,128)(2,1)S(1)}, u32[]{:S(2)}, u32[]{:S(2)}) collective-permute-start(bf16[8,4,64,128]{3,2,1,0:T(8,128)(2,1)S(1)} %collective-permute-done.12.refs_4_.refs_3_), channel_id=1, source_target_pairs={{0,1},{1,0},{2,3},{3,2},{4,5},{5,4},{6,7},{7,6},{8,9},{9,8},{10,11... | collective-permute-start | bytes 1572872 | tf_op jit(solution)/shard_map/ppermute | solution.py:168
  2.8 49.0 %collective-permute-start.15 = (bf16[8,4,64,128]{3,2,1,0:T(8,128)(2,1)}, bf16[8,4,64,128]{3,2,1,0:T(8,128)(2,1)S(1)}, u32[]{:S(2)}, u32[]{:S(2)}) collective-permute-start(bf16[8,4,64,128]{3,2,1,0:T(8,128)(2,1)} %bitcast.12), channel_id=1, source_target_pairs={{0,2},{1,3},{2,0},{3,1},{4,6},{5,7},{6,4},{7,5},{8,9},{9,8},{10,11... | collective-permute-start | bytes 1572872 | tf_op jit(solution)/shard_map/ppermute | solution.py:168
  2.9 58.6 %collective-permute-start.19 = (bf16[8,4,64,128]{3,2,1,0:T(8,128)(2,1)}, bf16[8,4,64,128]{3,2,1,0:T(8,128)(2,1)S(1)}, u32[]{:S(2)}, u32[]{:S(2)}) collective-permute-start(bf16[8,4,64,128]{3,2,1,0:T(8,128)(2,1)} %bitcast.13), channel_id=1, source_target_pairs={{0,1},{1,0},{2,3},{3,2},{4,5},{5,4},{6,7},{7,6},{8,10},{9,11},{10,... | collective-permute-start | bytes 1572872 | tf_op jit(solution)/shard_map/ppermute | solution.py:168
  4.2 1.5 %collective-permute-start = (s32[3,8]{1,0:T(4,128)S(1)}, s32[3,8]{1,0:T(4,128)S(1)}, u32[]{:S(2)}, u32[]{:S(2)}) collective-permute-start(s32[3,8]{1,0:T(4,128)S(1)} %bitcast.19), channel_id=1, source_target_pairs={{0,1},{1,0},{2,3},{3,2},{4,5},{5,4},{6,7},{7,6},{8,9},{9,8},{10,11... | collective-permute-start | bytes 296 | tf_op jit(solution)/shard_map/ppermute | solution.py:168
  5.6 1.4 %collective-permute-start.1 = (f32[8,8,128]{2,1,0:T(8,128)}, f32[8,8,128]{2,1,0:T(8,128)S(1)}, u32[]{:S(2)}, u32[]{:S(2)}) collective-permute-start(f32[8,8,128]{2,1,0:T(8,128)} %bitcast.15), channel_id=1, source_target_pairs={{0,1},{1,0},{2,3},{3,2},{4,5},{5,4},{6,7},{7,6},{8,9},{9,8},{10,11... | collective-permute-start | bytes 98312 | tf_op jit(solution)/shard_map/ppermute | solution.py:168
  7.0 9.9 %collective-permute-start.2 = (f32[8,8,128]{2,1,0:T(8,128)}, f32[8,8,128]{2,1,0:T(8,128)S(1)}, u32[]{:S(2)}, u32[]{:S(2)}) collective-permute-start(f32[8,8,128]{2,1,0:T(8,128)} %bitcast.16), channel_id=1, source_target_pairs={{0,2},{1,3},{2,0},{3,1},{4,6},{5,7},{6,4},{7,5},{8,10},{9,11},{10,... | collective-permute-start | bytes 98312 | tf_op jit(solution)/shard_map/ppermute | solution.py:168
  7.7 1.0 %copy-start = (bf16[1,8,4,64,128]{4,3,2,1,0:T(8,128)(2,1)S(1)}, bf16[1,8,4,64,128]{4,3,2,1,0:T(8,128)(2,1)}, u32[]{:S(2)}) copy-start(bf16[1,8,4,64,128]{4,3,2,1,0:T(8,128)(2,1)} %param.4) | copy-start | bytes 1572868
  8.8 8.2 %copy-start.1 = (f32[1,8,1024]{2,1,0:T(8,128)S(1)}, f32[1,8,1024]{2,1,0:T(8,128)}, u32[]{:S(2)}) copy-start(f32[1,8,1024]{2,1,0:T(8,128)} %param.3) | copy-start | bytes 98308
  17.0 4.5 %collective-permute-start.3 = (f32[8,8,128]{2,1,0:T(8,128)S(1)}, f32[8,8,128]{2,1,0:T(8,128)S(1)}, u32[]{:S(2)}, u32[]{:S(2)}) collective-permute-start(f32[8,8,128]{2,1,0:T(8,128)S(1)} %bitcast.17), channel_id=1, source_target_pairs={{0,3},{1,2},{2,1},{3,0},{4,7},{5,6},{6,5},{7,4},{8,11},{9,10},{10,... | collective-permute-start | bytes 98312 | tf_op jit(solution)/shard_map/ppermute | solution.py:168
  22.6 2.8 %collective-permute-start.7 = (bf16[16,8,128]{2,1,0:T(8,128)(2,1)S(1)}, bf16[16,8,128]{2,1,0:T(8,128)(2,1)S(1)}, u32[]{:S(2)}, u32[]{:S(2)}) collective-permute-start(bf16[16,8,128]{2,1,0:T(8,128)(2,1)S(1)} %get-tuple-element.19), channel_id=1, source_target_pairs={{0,4},{1,5},{2,6},{3,7},{4,0},{5,1},{6,2},{7,3},{8,12},{9,13},{10,... | collective-permute-start | bytes 98312 | tf_op jit(solution)/shard_map/ppermute | solution.py:168
  23.8 23.4 %collective-permute-start.11 = (f32[32,8,128]{2,1,0:T(8,128)S(1)}, f32[32,8,128]{2,1,0:T(8,128)S(1)}, u32[]{:S(2)}, u32[]{:S(2)}) collective-permute-start(f32[32,8,128]{2,1,0:T(8,128)S(1)} %get-tuple-element.21.refs_3_), channel_id=1, source_target_pairs={{0,4},{1,5},{2,6},{3,7},{4,0},{5,1},{6,2},{7,3},{8,9},{9,8},{10,11... | collective-permute-start | bytes 393224 | tf_op jit(solution)/shard_map/ppermute | solution.py:168
  25.4 3.7 %collective-permute-start.8 = (bf16[16,8,128]{2,1,0:T(8,128)(2,1)S(1)}, bf16[16,8,128]{2,1,0:T(8,128)(2,1)S(1)}, u32[]{:S(2)}, u32[]{:S(2)}) collective-permute-start(bf16[16,8,128]{2,1,0:T(8,128)(2,1)S(1)} %get-tuple-element.19), channel_id=1, source_target_pairs={{0,6},{1,7},{2,4},{3,5},{4,2},{5,3},{6,0},{7,1},{8,14},{9,15},{10,... | collective-permute-start | bytes 98312 | tf_op jit(solution)/shard_map/ppermute | solution.py:168
  29.0 3.8 %collective-permute-start.6 = (s32[6,8]{1,0:T(8,128)S(1)}, s32[6,8]{1,0:T(8,128)S(1)}, u32[]{:S(2)}, u32[]{:S(2)}) collective-permute-start(s32[6,8]{1,0:T(8,128)S(1)} %pad_add_fusion.refs_0_), channel_id=1, source_target_pairs={{0,4},{1,5},{2,6},{3,7},{4,0},{5,1},{6,2},{7,3},{8,9},{9,8},{10,11... | collective-permute-start | bytes 584 | tf_op jit(solution)/shard_map/ppermute | solution.py:168
  32.8 10.4 %collective-permute-start.10 = (bf16[16,8,128]{2,1,0:T(8,128)(2,1)S(1)}, bf16[16,8,128]{2,1,0:T(8,128)(2,1)S(1)}, u32[]{:S(2)}, u32[]{:S(2)}) collective-permute-start(bf16[16,8,128]{2,1,0:T(8,128)(2,1)S(1)} %get-tuple-element.22), channel_id=1, source_target_pairs={{0,1},{1,0},{2,3},{3,2},{4,5},{5,4},{6,7},{7,6},{8,18},{9,19},{10,... | collective-permute-start | bytes 98312 | tf_op jit(solution)/shard_map/ppermute | solution.py:168
  43.3 2.9 %collective-permute-start.9 = (bf16[16,8,128]{2,1,0:T(8,128)(2,1)S(1)}, bf16[16,8,128]{2,1,0:T(8,128)(2,1)S(1)}, u32[]{:S(2)}, u32[]{:S(2)}) collective-permute-start(bf16[16,8,128]{2,1,0:T(8,128)(2,1)S(1)} %get-tuple-element.22), channel_id=1, source_target_pairs={{0,1},{1,0},{2,3},{3,2},{4,5},{5,4},{6,7},{7,6},{8,16},{9,17},{10,... | collective-permute-start | bytes 98312 | tf_op jit(solution)/shard_map/ppermute | solution.py:168
  46.2 5.7 %collective-permute-start.5 = (s32[3,8]{1,0:T(4,128)S(1)}, s32[3,8]{1,0:T(4,128)S(1)}, u32[]{:S(2)}, u32[]{:S(2)}) collective-permute-start(s32[3,8]{1,0:T(4,128)S(1)} %bitcast.21), channel_id=1, source_target_pairs={{0,2},{1,3},{2,0},{3,1},{4,6},{5,7},{6,4},{7,5},{8,10},{9,11},{10,... | collective-permute-start | bytes 296 | tf_op jit(solution)/shard_map/ppermute | solution.py:168
  48.3 4.4 %collective-permute-start.14 = (bf16[16,8,128]{2,1,0:T(8,128)(2,1)S(1)}, bf16[16,8,128]{2,1,0:T(8,128)(2,1)S(1)}, u32[]{:S(2)}, u32[]{:S(2)}) collective-permute-start(bf16[16,8,128]{2,1,0:T(8,128)(2,1)S(1)} %get-tuple-element.23.refs_1_), channel_id=1, source_target_pairs={{0,2},{1,3},{2,0},{3,1},{4,6},{5,7},{6,4},{7,5},{8,9},{9,8},{10,11... | collective-permute-start | bytes 98312 | tf_op jit(solution)/shard_map/ppermute | solution.py:168
  53.8 1.4 %collective-permute-start.16 = (bf16[16,8,128]{2,1,0:T(8,128)(2,1)S(1)}, bf16[16,8,128]{2,1,0:T(8,128)(2,1)S(1)}, u32[]{:S(2)}, u32[]{:S(2)}) collective-permute-start(bf16[16,8,128]{2,1,0:T(8,128)(2,1)S(1)} %get-tuple-element.24.refs_1_), channel_id=1, source_target_pairs={{0,1},{1,0},{2,3},{3,2},{4,5},{5,4},{6,7},{7,6},{8,9},{9,8},{10,11... | collective-permute-start | bytes 98312 | tf_op jit(solution)/shard_map/ppermute | solution.py:168
  54.2 7.3 %collective-permute-start.20 = (f32[8,8,128]{2,1,0:T(8,128)S(1)}, f32[8,8,128]{2,1,0:T(8,128)S(1)}, u32[]{:S(2)}, u32[]{:S(2)}) collective-permute-start(f32[8,8,128]{2,1,0:T(8,128)S(1)} %get-tuple-element.27.refs_5_), channel_id=1, source_target_pairs={{0,2},{1,3},{2,0},{3,1},{4,6},{5,7},{6,4},{7,5},{8,10},{9,11},{10,... | collective-permute-start | bytes 98312 | tf_op jit(solution)/shard_map/ppermute | solution.py:168
  56.3 5.7 %collective-permute-start.17 = (bf16[16,8,128]{2,1,0:T(8,128)(2,1)S(1)}, bf16[16,8,128]{2,1,0:T(8,128)(2,1)S(1)}, u32[]{:S(2)}, u32[]{:S(2)}) collective-permute-start(bf16[16,8,128]{2,1,0:T(8,128)(2,1)S(1)} %get-tuple-element.26), channel_id=1, source_target_pairs={{0,1},{1,0},{2,3},{3,2},{4,5},{5,4},{6,7},{7,6},{8,16},{9,17},{10,... | collective-permute-start | bytes 98312 | tf_op jit(solution)/shard_map/ppermute | solution.py:168
  60.6 3.7 %collective-permute-start.18 = (bf16[16,8,128]{2,1,0:T(8,128)(2,1)S(1)}, bf16[16,8,128]{2,1,0:T(8,128)(2,1)S(1)}, u32[]{:S(2)}, u32[]{:S(2)}) collective-permute-start(bf16[16,8,128]{2,1,0:T(8,128)(2,1)S(1)} %get-tuple-element.26), channel_id=1, source_target_pairs={{0,1},{1,0},{2,3},{3,2},{4,5},{5,4},{6,7},{7,6},{8,18},{9,19},{10,... | collective-permute-start | bytes 98312 | tf_op jit(solution)/shard_map/ppermute | solution.py:168
  60.9 8.0 %collective-permute-start.23 = (f32[8,8,128]{2,1,0:T(8,128)S(1)}, f32[8,8,128]{2,1,0:T(8,128)S(1)}, u32[]{:S(2)}, u32[]{:S(2)}) collective-permute-start(f32[8,8,128]{2,1,0:T(8,128)S(1)} %slice.3), channel_id=1, source_target_pairs={{0,4},{1,5},{2,6},{3,7},{4,0},{5,1},{6,2},{7,3},{8,9},{9,8},{10,11... | collective-permute-start | bytes 98312 | tf_op jit(solution)/shard_map/ppermute | solution.py:168
  65.4 3.5 %collective-permute-start.21 = (bf16[16,8,128]{2,1,0:T(8,128)(2,1)S(1)}, bf16[16,8,128]{2,1,0:T(8,128)(2,1)S(1)}, u32[]{:S(2)}, u32[]{:S(2)}) collective-permute-start(bf16[16,8,128]{2,1,0:T(8,128)(2,1)S(1)} %get-tuple-element.28), channel_id=1, source_target_pairs={{0,4},{1,5},{2,6},{3,7},{4,0},{5,1},{6,2},{7,3},{8,12},{9,13},{10,... | collective-permute-start | bytes 98312 | tf_op jit(solution)/shard_map/ppermute | solution.py:168
  66.3 5.0 %collective-permute-start.22 = (bf16[16,8,128]{2,1,0:T(8,128)(2,1)S(1)}, bf16[16,8,128]{2,1,0:T(8,128)(2,1)S(1)}, u32[]{:S(2)}, u32[]{:S(2)}) collective-permute-start(bf16[16,8,128]{2,1,0:T(8,128)(2,1)S(1)} %get-tuple-element.28), channel_id=1, source_target_pairs={{0,5},{1,4},{2,7},{3,6},{4,1},{5,0},{6,3},{7,2},{8,13},{9,12},{10,... | collective-permute-start | bytes 98312 | tf_op jit(solution)/shard_map/ppermute | solution.py:168

commit v5 on v4

--- a/solution.py
+++ b/solution.py
@@ -32,7 +32,7 @@
     width = blocks[0].shape[-1]
     half = width // 2
     off, nb = patterns.shape[0] // 2, patterns.shape[1]
-    base = lax.axis_index("tile") * nb
+    columns = patterns[...] ^ (lax.axis_index("tile") * nb)
     place = place_of(lax.axis_index("sweep"))
     lane = lax.broadcasted_iota(jnp.int32, (1, 1, width), 2)
     sign = jnp.where(lane < half, 1.0, -1.0).astype(jnp.float32)
@@ -53,7 +53,7 @@
         group, local = divmod(row, nb)
         flip = row_flips[group]
         slots = [flip * nb + local]
-        slots += [patterns[group * off + j, local] ^ base for j in range(off)]
+        slots += [columns[group * off + j, local] for j in range(off)]
         mats = jnp.concatenate([ref[at, j] for j in range(off + 1)], axis=1)
         inputs = jnp.concatenate([vec[slot] for slot in slots], axis=1)
         out = lax.dot_general(
@@ -107,7 +107,7 @@
     args = [*arrays, *([] if src is None else [src]), *blocks, *states]
     return pl.pallas_call(
         functools.partial(apply_kernel, stage, plan),
-        in_specs=[SMEM] + [VMEM] * len(args),
+        in_specs=[VMEM] * (1 + len(args)),
         out_specs=[VMEM] * len(out_shape),
         out_shape=out_shape,
         scratch_shapes=[pltpu.VMEM((total, 2 * rhs, width), jnp.bfloat16)],

time: 73.1 us -> 69.7 us (0.953)
  Pallas kernels: 8.22 us -> 4.29 us
    pallas_call x7, Pallas kernels: 8.18 us -> 4.25 us  [layer_apply(): pl.pallas_call(functools.partial(apply_kernel, stage, plan), in_specs=[VM...]
  transfers between devices with their start and end apart: 24 -> 24, of which waited for: 13 -> 14; matrix products, arithmetic and copies ran while one was open for 0% -> 0% of each run, Pallas kernels for 9% -> 5%
where the time goes in v5:
time: 69.7 us; the launch traced here: 69.5 us
  starting transfers between devices  37.8 us (54%)
  waiting for transfers between devices  26.3 us (38%)
  Pallas kernels  4.29 us (6%)
  local copies, waits for them, and re-layouts  1.05 us (2%)
    ppermute x24, starting transfers between devices, swap(): return lax.ppermute(value, AXES, route)  37.8 us
    ppermute x24, waiting for transfers between devices, swap(): return lax.ppermute(value, AXES, route)  26.3 us
    pallas_call x7, Pallas kernels, layer_apply(): pl.pallas_call(functools.partial(apply_kernel, stage, plan), in_specs=[VM...  4.25 us
  transfers between devices with their start and end apart: 24, of which 14 were waited for; matrix products, arithmetic and copies ran while one was open for 0% of the time, Pallas kernels for 5%

profile of v5, /device:TPU:9, one launch (start us, length us, event | category | flops | bytes accessed | tf_op | source)
XLA Modules:
  0.0 69.5 jit_solution(15782437307178626447)
XLA Ops:
  0.0 0.7 collective-permute-start.12
  0.7 1.7 %collective-permute-done.12.refs_4_.refs_3_ = bf16[8,4,64,128]{3,2,1,0:T(8,128)(2,1)S(1)} collective-permute-done((bf16[8,4,64,128]{3,2,1,0:T(8,128)(2,1)}, bf16[8,4,64,128]{3,2,1,0:T(8,128)(2,1)S(1)}, u32[]{:S(2)}, u32[]{:S(2)}) %collective-permute-start.12) | collective-permute-done | bytes 524320 | tf_op jit(solution)/shard_map/ppermute | solution.py:168
  2.9 1.2 %collective-permute-start.19 = (bf16[8,4,64,128]{3,2,1,0:T(8,128)(2,1)}, bf16[8,4,64,128]{3,2,1,0:T(8,128)(2,1)S(1)}, u32[]{:S(2)}, u32[]{:S(2)}) collective-permute-start(bf16[8,4,64,128]{3,2,1,0:T(8,128)(2,1)} %bitcast.13), channel_id=1, source_target_pairs={{0,1},{1,0},{2,3},{3,2},{4,5},{5,4},{6,7},{7,6},{8,10},{9,11},{10,... | collective-permute-start | bytes 1572872 | tf_op jit(solution)/shard_map/ppermute | solution.py:168
  4.2 0.7 collective-permute-start
  4.8 0.8 %collective-permute-done = s32[3,8]{1,0:T(4,128)S(1)} collective-permute-done((s32[3,8]{1,0:T(4,128)S(1)}, s32[3,8]{1,0:T(4,128)S(1)}, u32[]{:S(2)}, u32[]{:S(2)}) %collective-permute-start) | collective-permute-done | bytes 128 | tf_op jit(solution)/shard_map/ppermute | solution.py:168
  6.0 1.1 %collective-permute-done.1.refs_2_ = f32[8,8,128]{2,1,0:T(8,128)S(1)} collective-permute-done((f32[8,8,128]{2,1,0:T(8,128)}, f32[8,8,128]{2,1,0:T(8,128)S(1)}, u32[]{:S(2)}, u32[]{:S(2)}) %collective-permute-start.1) | collective-permute-done | bytes 32800 | tf_op jit(solution)/shard_map/ppermute | solution.py:168
  7.0 0.7 %collective-permute-start.2 = (f32[8,8,128]{2,1,0:T(8,128)}, f32[8,8,128]{2,1,0:T(8,128)S(1)}, u32[]{:S(2)}, u32[]{:S(2)}) collective-permute-start(f32[8,8,128]{2,1,0:T(8,128)} %bitcast.16), channel_id=1, source_target_pairs={{0,2},{1,3},{2,0},{3,1},{4,6},{5,7},{6,4},{7,5},{8,10},{9,11},{10,... | collective-permute-start | bytes 98312 | tf_op jit(solution)/shard_map/ppermute | solution.py:168
  7.7 1.0 %copy-done = bf16[1,8,4,64,128]{4,3,2,1,0:T(8,128)(2,1)S(1)} copy-done((bf16[1,8,4,64,128]{4,3,2,1,0:T(8,128)(2,1)S(1)}, bf16[1,8,4,64,128]{4,3,2,1,0:T(8,128)(2,1)}, u32[]{:S(2)}) %copy-start) | copy-done | bytes 524312
  8.8 8.1 %collective-permute-done.2.refs_3_ = f32[8,8,128]{2,1,0:T(8,128)S(1)} collective-permute-done((f32[8,8,128]{2,1,0:T(8,128)}, f32[8,8,128]{2,1,0:T(8,128)S(1)}, u32[]{:S(2)}, u32[]{:S(2)}) %collective-permute-start.2) | collective-permute-done | bytes 32800 | tf_op jit(solution)/shard_map/ppermute | solution.py:168
  17.0 2.3 %collective-permute-start.3 = (f32[8,8,128]{2,1,0:T(8,128)S(1)}, f32[8,8,128]{2,1,0:T(8,128)S(1)}, u32[]{:S(2)}, u32[]{:S(2)}) collective-permute-start(f32[8,8,128]{2,1,0:T(8,128)S(1)} %bitcast.17), channel_id=1, source_target_pairs={{0,3},{1,2},{2,1},{3,0},{4,7},{5,6},{6,5},{7,4},{8,11},{9,10},{10,... | collective-permute-start | bytes 98312 | tf_op jit(solution)/shard_map/ppermute | solution.py:168
  19.3 2.1 %collective-permute-done.3.refs_4_ = f32[8,8,128]{2,1,0:T(8,128)S(1)} collective-permute-done((f32[8,8,128]{2,1,0:T(8,128)S(1)}, f32[8,8,128]{2,1,0:T(8,128)S(1)}, u32[]{:S(2)}, u32[]{:S(2)}) %collective-permute-start.3) | collective-permute-done | bytes 32800 | tf_op jit(solution)/shard_map/ppermute | solution.py:168
  22.0 1.3 %collective-permute-start.7 = (bf16[16,8,128]{2,1,0:T(8,128)(2,1)S(1)}, bf16[16,8,128]{2,1,0:T(8,128)(2,1)S(1)}, u32[]{:S(2)}, u32[]{:S(2)}) collective-permute-start(bf16[16,8,128]{2,1,0:T(8,128)(2,1)S(1)} %get-tuple-element.19), channel_id=1, source_target_pairs={{0,4},{1,5},{2,6},{3,7},{4,0},{5,1},{6,2},{7,3},{8,12},{9,13},{10,... | collective-permute-start | bytes 98312 | tf_op jit(solution)/shard_map/ppermute | solution.py:168
  23.3 0.7 collective-permute-start.11
  23.9 0.8 %collective-permute-done.7.refs_1_ = bf16[16,8,128]{2,1,0:T(8,128)(2,1)S(1)} collective-permute-done((bf16[16,8,128]{2,1,0:T(8,128)(2,1)S(1)}, bf16[16,8,128]{2,1,0:T(8,128)(2,1)S(1)}, u32[]{:S(2)}, u32[]{:S(2)}) %collective-permute-start.7) | collective-permute-done | bytes 32800 | tf_op jit(solution)/shard_map/ppermute | solution.py:168
  24.8 1.0 %collective-permute-start.8 = (bf16[16,8,128]{2,1,0:T(8,128)(2,1)S(1)}, bf16[16,8,128]{2,1,0:T(8,128)(2,1)S(1)}, u32[]{:S(2)}, u32[]{:S(2)}) collective-permute-start(bf16[16,8,128]{2,1,0:T(8,128)(2,1)S(1)} %get-tuple-element.19), channel_id=1, source_target_pairs={{0,6},{1,7},{2,4},{3,5},{4,2},{5,3},{6,0},{7,1},{8,14},{9,15},{10,... | collective-permute-start | bytes 98312 | tf_op jit(solution)/shard_map/ppermute | solution.py:168
  25.8 2.6 %collective-permute-done.8.refs_2_ = bf16[16,8,128]{2,1,0:T(8,128)(2,1)S(1)} collective-permute-done((bf16[16,8,128]{2,1,0:T(8,128)(2,1)S(1)}, bf16[16,8,128]{2,1,0:T(8,128)(2,1)S(1)}, u32[]{:S(2)}, u32[]{:S(2)}) %collective-permute-start.8) | collective-permute-done | bytes 32800 | tf_op jit(solution)/shard_map/ppermute | solution.py:168
  28.5 2.7 %collective-permute-start.6 = (s32[6,8]{1,0:T(8,128)S(1)}, s32[6,8]{1,0:T(8,128)S(1)}, u32[]{:S(2)}, u32[]{:S(2)}) collective-permute-start(s32[6,8]{1,0:T(8,128)S(1)} %pad_add_fusion.refs_0_), channel_id=1, source_target_pairs={{0,4},{1,5},{2,6},{3,7},{4,0},{5,1},{6,2},{7,3},{8,9},{9,8},{10,11... | collective-permute-start | bytes 584 | tf_op jit(solution)/shard_map/ppermute | solution.py:168
  32.0 9.4 %collective-permute-start.10 = (bf16[16,8,128]{2,1,0:T(8,128)(2,1)S(1)}, bf16[16,8,128]{2,1,0:T(8,128)(2,1)S(1)}, u32[]{:S(2)}, u32[]{:S(2)}) collective-permute-start(bf16[16,8,128]{2,1,0:T(8,128)(2,1)S(1)} %get-tuple-element.22), channel_id=1, source_target_pairs={{0,1},{1,0},{2,3},{3,2},{4,5},{5,4},{6,7},{7,6},{8,18},{9,19},{10,... | collective-permute-start | bytes 98312 | tf_op jit(solution)/shard_map/ppermute | solution.py:168
  41.4 1.3 %collective-permute-done.10.refs_2_ = bf16[16,8,128]{2,1,0:T(8,128)(2,1)S(1)} collective-permute-done((bf16[16,8,128]{2,1,0:T(8,128)(2,1)S(1)}, bf16[16,8,128]{2,1,0:T(8,128)(2,1)S(1)}, u32[]{:S(2)}, u32[]{:S(2)}) %collective-permute-start.10) | collective-permute-done | bytes 32800 | tf_op jit(solution)/shard_map/ppermute | solution.py:168
  42.7 1.6 %collective-permute-start.9 = (bf16[16,8,128]{2,1,0:T(8,128)(2,1)S(1)}, bf16[16,8,128]{2,1,0:T(8,128)(2,1)S(1)}, u32[]{:S(2)}, u32[]{:S(2)}) collective-permute-start(bf16[16,8,128]{2,1,0:T(8,128)(2,1)S(1)} %get-tuple-element.22), channel_id=1, source_target_pairs={{0,1},{1,0},{2,3},{3,2},{4,5},{5,4},{6,7},{7,6},{8,16},{9,17},{10,... | collective-permute-start | bytes 98312 | tf_op jit(solution)/shard_map/ppermute | solution.py:168
  44.3 1.3 %collective-permute-done.9.refs_1_ = bf16[16,8,128]{2,1,0:T(8,128)(2,1)S(1)} collective-permute-done((bf16[16,8,128]{2,1,0:T(8,128)(2,1)S(1)}, bf16[16,8,128]{2,1,0:T(8,128)(2,1)S(1)}, u32[]{:S(2)}, u32[]{:S(2)}) %collective-permute-start.9) | collective-permute-done | bytes 32800 | tf_op jit(solution)/shard_map/ppermute | solution.py:168
  45.6 1.0 %collective-permute-start.5 = (s32[3,8]{1,0:T(4,128)S(1)}, s32[3,8]{1,0:T(4,128)S(1)}, u32[]{:S(2)}, u32[]{:S(2)}) collective-permute-start(s32[3,8]{1,0:T(4,128)S(1)} %bitcast.21), channel_id=1, source_target_pairs={{0,2},{1,3},{2,0},{3,1},{4,6},{5,7},{6,4},{7,5},{8,10},{9,11},{10,... | collective-permute-start | bytes 296 | tf_op jit(solution)/shard_map/ppermute | solution.py:168
  47.2 3.5 %collective-permute-start.14 = (bf16[16,8,128]{2,1,0:T(8,128)(2,1)S(1)}, bf16[16,8,128]{2,1,0:T(8,128)(2,1)S(1)}, u32[]{:S(2)}, u32[]{:S(2)}) collective-permute-start(bf16[16,8,128]{2,1,0:T(8,128)(2,1)S(1)} %get-tuple-element.23.refs_1_), channel_id=1, source_target_pairs={{0,2},{1,3},{2,0},{3,1},{4,6},{5,7},{6,4},{7,5},{8,9},{9,8},{10,11... | collective-permute-start | bytes 98312 | tf_op jit(solution)/shard_map/ppermute | solution.py:168
  50.7 0.8 %collective-permute-done.14.refs_2_ = bf16[16,8,128]{2,1,0:T(8,128)(2,1)S(1)} collective-permute-done((bf16[16,8,128]{2,1,0:T(8,128)(2,1)S(1)}, bf16[16,8,128]{2,1,0:T(8,128)(2,1)S(1)}, u32[]{:S(2)}, u32[]{:S(2)}) %collective-permute-start.14) | collective-permute-done | bytes 32800 | tf_op jit(solution)/shard_map/ppermute | solution.py:168
  52.1 0.9 %collective-permute-start.16 = (bf16[16,8,128]{2,1,0:T(8,128)(2,1)S(1)}, bf16[16,8,128]{2,1,0:T(8,128)(2,1)S(1)}, u32[]{:S(2)}, u32[]{:S(2)}) collective-permute-start(bf16[16,8,128]{2,1,0:T(8,128)(2,1)S(1)} %get-tuple-element.24.refs_1_), channel_id=1, source_target_pairs={{0,1},{1,0},{2,3},{3,2},{4,5},{5,4},{6,7},{7,6},{8,9},{9,8},{10,11... | collective-permute-start | bytes 98312 | tf_op jit(solution)/shard_map/ppermute | solution.py:168
  53.0 1.0 %collective-permute-start.20 = (f32[8,8,128]{2,1,0:T(8,128)S(1)}, f32[8,8,128]{2,1,0:T(8,128)S(1)}, u32[]{:S(2)}, u32[]{:S(2)}) collective-permute-start(f32[8,8,128]{2,1,0:T(8,128)S(1)} %get-tuple-element.27.refs_5_), channel_id=1, source_target_pairs={{0,2},{1,3},{2,0},{3,1},{4,6},{5,7},{6,4},{7,5},{8,10},{9,11},{10,... | collective-permute-start | bytes 98312 | tf_op jit(solution)/shard_map/ppermute | solution.py:168
  54.6 3.8 %collective-permute-start.17 = (bf16[16,8,128]{2,1,0:T(8,128)(2,1)S(1)}, bf16[16,8,128]{2,1,0:T(8,128)(2,1)S(1)}, u32[]{:S(2)}, u32[]{:S(2)}) collective-permute-start(bf16[16,8,128]{2,1,0:T(8,128)(2,1)S(1)} %get-tuple-element.26), channel_id=1, source_target_pairs={{0,1},{1,0},{2,3},{3,2},{4,5},{5,4},{6,7},{7,6},{8,16},{9,17},{10,... | collective-permute-start | bytes 98312 | tf_op jit(solution)/shard_map/ppermute | solution.py:168
  59.7 2.4 %collective-permute-done.18.refs_2_ = bf16[16,8,128]{2,1,0:T(8,128)(2,1)S(1)} collective-permute-done((bf16[16,8,128]{2,1,0:T(8,128)(2,1)S(1)}, bf16[16,8,128]{2,1,0:T(8,128)(2,1)S(1)}, u32[]{:S(2)}, u32[]{:S(2)}) %collective-permute-start.18) | collective-permute-done | bytes 32800 | tf_op jit(solution)/shard_map/ppermute | solution.py:168
  62.6 0.9 %collective-permute-start.21 = (bf16[16,8,128]{2,1,0:T(8,128)(2,1)S(1)}, bf16[16,8,128]{2,1,0:T(8,128)(2,1)S(1)}, u32[]{:S(2)}, u32[]{:S(2)}) collective-permute-start(bf16[16,8,128]{2,1,0:T(8,128)(2,1)S(1)} %get-tuple-element.28), channel_id=1, source_target_pairs={{0,4},{1,5},{2,6},{3,7},{4,0},{5,1},{6,2},{7,3},{8,12},{9,13},{10,... | collective-permute-start | bytes 98312 | tf_op jit(solution)/shard_map/ppermute | solution.py:168
  63.5 2.6 %collective-permute-start.22 = (bf16[16,8,128]{2,1,0:T(8,128)(2,1)S(1)}, bf16[16,8,128]{2,1,0:T(8,128)(2,1)S(1)}, u32[]{:S(2)}, u32[]{:S(2)}) collective-permute-start(bf16[16,8,128]{2,1,0:T(8,128)(2,1)S(1)} %get-tuple-element.28), channel_id=1, source_target_pairs={{0,5},{1,4},{2,7},{3,6},{4,1},{5,0},{6,3},{7,2},{8,13},{9,12},{10,... | collective-permute-start | bytes 98312 | tf_op jit(solution)/shard_map/ppermute | solution.py:168
  66.1 2.4 %collective-permute-done.22.refs_2_ = bf16[16,8,128]{2,1,0:T(8,128)(2,1)S(1)} collective-permute-done((bf16[16,8,128]{2,1,0:T(8,128)(2,1)S(1)}, bf16[16,8,128]{2,1,0:T(8,128)(2,1)S(1)}, u32[]{:S(2)}, u32[]{:S(2)}) %collective-permute-start.22) | collective-permute-done | bytes 32800 | tf_op jit(solution)/shard_map/ppermute | solution.py:168
  68.5 1.0 %shard_map.43 = f32[8,1024]{1,0:T(8,128)} custom-call(s32[6,8]{1,0:T(8,128)S(1)} %pad_add_fusion.refs_0_, bf16[16,8,128]{2,1,0:T(8,128)(2,1)S(1)} %collective-permute-done.21.refs_1_, bf16[16,8,128]{2,1,0:T(8,128)(2,1)S(1)} %collective-permute-done.22.refs_2_, bf16[8,4,64,128]{3,2,1,0:T(8,128)(2,1)S(1)} %stage_in.1.refs_5_.refs_4_.refs_3_, ...), custom_call_target="tpu_custom_call" | custom-call | tf_op jit(solution)/shard_map/pallas_call | solution.py:108
  (34 shorter events, 5.8 us)
Async XLA Ops:
  0.0 4.2 %copy-start.2 = (s32[1,8,3]{1,0,2:T(1,128)S(1)}, s32[1,8,3]{1,0,2:T(1,128)}, u32[]{:S(2)}) copy-start(s32[1,8,3]{1,0,2:T(1,128)} %param.5) | copy-start | bytes 292
  0.0 2.4 %collective-permute-start.12 = (bf16[8,4,64,128]{3,2,1,0:T(8,128)(2,1)}, bf16[8,4,64,128]{3,2,1,0:T(8,128)(2,1)S(1)}, u32[]{:S(2)}, u32[]{:S(2)}) collective-permute-start(bf16[8,4,64,128]{3,2,1,0:T(8,128)(2,1)} %bitcast.10), channel_id=1, source_target_pairs={{0,4},{1,5},{2,6},{3,7},{4,0},{5,1},{6,2},{7,3},{8,9},{9,8},{10,11... | collective-permute-start | bytes 1572872 | tf_op jit(solution)/shard_map/ppermute | solution.py:168
  0.7 20.8 %collective-permute-start.4 = (bf16[8,4,64,128]{3,2,1,0:T(8,128)(2,1)}, bf16[8,4,64,128]{3,2,1,0:T(8,128)(2,1)S(1)}, u32[]{:S(2)}, u32[]{:S(2)}) collective-permute-start(bf16[8,4,64,128]{3,2,1,0:T(8,128)(2,1)} %bitcast.11), channel_id=1, source_target_pairs={{0,1},{1,0},{2,3},{3,2},{4,5},{5,4},{6,7},{7,6},{8,9},{9,8},{10,11... | collective-permute-start | bytes 1572872 | tf_op jit(solution)/shard_map/ppermute | solution.py:168
  2.4 44.2 %collective-permute-start.13 = (bf16[8,4,64,128]{3,2,1,0:T(8,128)(2,1)S(1)}, bf16[8,4,64,128]{3,2,1,0:T(8,128)(2,1)S(1)}, u32[]{:S(2)}, u32[]{:S(2)}) collective-permute-start(bf16[8,4,64,128]{3,2,1,0:T(8,128)(2,1)S(1)} %collective-permute-done.12.refs_4_.refs_3_), channel_id=1, source_target_pairs={{0,1},{1,0},{2,3},{3,2},{4,5},{5,4},{6,7},{7,6},{8,9},{9,8},{10,11... | collective-permute-start | bytes 1572872 | tf_op jit(solution)/shard_map/ppermute | solution.py:168
  2.8 47.9 %collective-permute-start.15 = (bf16[8,4,64,128]{3,2,1,0:T(8,128)(2,1)}, bf16[8,4,64,128]{3,2,1,0:T(8,128)(2,1)S(1)}, u32[]{:S(2)}, u32[]{:S(2)}) collective-permute-start(bf16[8,4,64,128]{3,2,1,0:T(8,128)(2,1)} %bitcast.12), channel_id=1, source_target_pairs={{0,2},{1,3},{2,0},{3,1},{4,6},{5,7},{6,4},{7,5},{8,9},{9,8},{10,11... | collective-permute-start | bytes 1572872 | tf_op jit(solution)/shard_map/ppermute | solution.py:168
  2.9 56.3 %collective-permute-start.19 = (bf16[8,4,64,128]{3,2,1,0:T(8,128)(2,1)}, bf16[8,4,64,128]{3,2,1,0:T(8,128)(2,1)S(1)}, u32[]{:S(2)}, u32[]{:S(2)}) collective-permute-start(bf16[8,4,64,128]{3,2,1,0:T(8,128)(2,1)} %bitcast.13), channel_id=1, source_target_pairs={{0,1},{1,0},{2,3},{3,2},{4,5},{5,4},{6,7},{7,6},{8,10},{9,11},{10,... | collective-permute-start | bytes 1572872 | tf_op jit(solution)/shard_map/ppermute | solution.py:168
  4.2 1.5 %collective-permute-start = (s32[3,8]{1,0:T(4,128)S(1)}, s32[3,8]{1,0:T(4,128)S(1)}, u32[]{:S(2)}, u32[]{:S(2)}) collective-permute-start(s32[3,8]{1,0:T(4,128)S(1)} %bitcast.19), channel_id=1, source_target_pairs={{0,1},{1,0},{2,3},{3,2},{4,5},{5,4},{6,7},{7,6},{8,9},{9,8},{10,11... | collective-permute-start | bytes 296 | tf_op jit(solution)/shard_map/ppermute | solution.py:168
  5.6 1.4 %collective-permute-start.1 = (f32[8,8,128]{2,1,0:T(8,128)}, f32[8,8,128]{2,1,0:T(8,128)S(1)}, u32[]{:S(2)}, u32[]{:S(2)}) collective-permute-start(f32[8,8,128]{2,1,0:T(8,128)} %bitcast.15), channel_id=1, source_target_pairs={{0,1},{1,0},{2,3},{3,2},{4,5},{5,4},{6,7},{7,6},{8,9},{9,8},{10,11... | collective-permute-start | bytes 98312 | tf_op jit(solution)/shard_map/ppermute | solution.py:168
  7.0 9.9 %collective-permute-start.2 = (f32[8,8,128]{2,1,0:T(8,128)}, f32[8,8,128]{2,1,0:T(8,128)S(1)}, u32[]{:S(2)}, u32[]{:S(2)}) collective-permute-start(f32[8,8,128]{2,1,0:T(8,128)} %bitcast.16), channel_id=1, source_target_pairs={{0,2},{1,3},{2,0},{3,1},{4,6},{5,7},{6,4},{7,5},{8,10},{9,11},{10,... | collective-permute-start | bytes 98312 | tf_op jit(solution)/shard_map/ppermute | solution.py:168
  7.7 1.0 %copy-start = (bf16[1,8,4,64,128]{4,3,2,1,0:T(8,128)(2,1)S(1)}, bf16[1,8,4,64,128]{4,3,2,1,0:T(8,128)(2,1)}, u32[]{:S(2)}) copy-start(bf16[1,8,4,64,128]{4,3,2,1,0:T(8,128)(2,1)} %param.4) | copy-start | bytes 1572868
  8.8 8.2 %copy-start.1 = (f32[1,8,1024]{2,1,0:T(8,128)S(1)}, f32[1,8,1024]{2,1,0:T(8,128)}, u32[]{:S(2)}) copy-start(f32[1,8,1024]{2,1,0:T(8,128)} %param.3) | copy-start | bytes 98308
  17.0 4.5 %collective-permute-start.3 = (f32[8,8,128]{2,1,0:T(8,128)S(1)}, f32[8,8,128]{2,1,0:T(8,128)S(1)}, u32[]{:S(2)}, u32[]{:S(2)}) collective-permute-start(f32[8,8,128]{2,1,0:T(8,128)S(1)} %bitcast.17), channel_id=1, source_target_pairs={{0,3},{1,2},{2,1},{3,0},{4,7},{5,6},{6,5},{7,4},{8,11},{9,10},{10,... | collective-permute-start | bytes 98312 | tf_op jit(solution)/shard_map/ppermute | solution.py:168
  22.0 2.8 %collective-permute-start.7 = (bf16[16,8,128]{2,1,0:T(8,128)(2,1)S(1)}, bf16[16,8,128]{2,1,0:T(8,128)(2,1)S(1)}, u32[]{:S(2)}, u32[]{:S(2)}) collective-permute-start(bf16[16,8,128]{2,1,0:T(8,128)(2,1)S(1)} %get-tuple-element.19), channel_id=1, source_target_pairs={{0,4},{1,5},{2,6},{3,7},{4,0},{5,1},{6,2},{7,3},{8,12},{9,13},{10,... | collective-permute-start | bytes 98312 | tf_op jit(solution)/shard_map/ppermute | solution.py:168
  23.3 23.4 %collective-permute-start.11 = (f32[32,8,128]{2,1,0:T(8,128)S(1)}, f32[32,8,128]{2,1,0:T(8,128)S(1)}, u32[]{:S(2)}, u32[]{:S(2)}) collective-permute-start(f32[32,8,128]{2,1,0:T(8,128)S(1)} %get-tuple-element.21.refs_3_), channel_id=1, source_target_pairs={{0,4},{1,5},{2,6},{3,7},{4,0},{5,1},{6,2},{7,3},{8,9},{9,8},{10,11... | collective-permute-start | bytes 393224 | tf_op jit(solution)/shard_map/ppermute | solution.py:168
  24.8 3.7 %collective-permute-start.8 = (bf16[16,8,128]{2,1,0:T(8,128)(2,1)S(1)}, bf16[16,8,128]{2,1,0:T(8,128)(2,1)S(1)}, u32[]{:S(2)}, u32[]{:S(2)}) collective-permute-start(bf16[16,8,128]{2,1,0:T(8,128)(2,1)S(1)} %get-tuple-element.19), channel_id=1, source_target_pairs={{0,6},{1,7},{2,4},{3,5},{4,2},{5,3},{6,0},{7,1},{8,14},{9,15},{10,... | collective-permute-start | bytes 98312 | tf_op jit(solution)/shard_map/ppermute | solution.py:168
  28.5 3.5 %collective-permute-start.6 = (s32[6,8]{1,0:T(8,128)S(1)}, s32[6,8]{1,0:T(8,128)S(1)}, u32[]{:S(2)}, u32[]{:S(2)}) collective-permute-start(s32[6,8]{1,0:T(8,128)S(1)} %pad_add_fusion.refs_0_), channel_id=1, source_target_pairs={{0,4},{1,5},{2,6},{3,7},{4,0},{5,1},{6,2},{7,3},{8,9},{9,8},{10,11... | collective-permute-start | bytes 584 | tf_op jit(solution)/shard_map/ppermute | solution.py:168
  32.0 10.7 %collective-permute-start.10 = (bf16[16,8,128]{2,1,0:T(8,128)(2,1)S(1)}, bf16[16,8,128]{2,1,0:T(8,128)(2,1)S(1)}, u32[]{:S(2)}, u32[]{:S(2)}) collective-permute-start(bf16[16,8,128]{2,1,0:T(8,128)(2,1)S(1)} %get-tuple-element.22), channel_id=1, source_target_pairs={{0,1},{1,0},{2,3},{3,2},{4,5},{5,4},{6,7},{7,6},{8,18},{9,19},{10,... | collective-permute-start | bytes 98312 | tf_op jit(solution)/shard_map/ppermute | solution.py:168
  42.7 2.9 %collective-permute-start.9 = (bf16[16,8,128]{2,1,0:T(8,128)(2,1)S(1)}, bf16[16,8,128]{2,1,0:T(8,128)(2,1)S(1)}, u32[]{:S(2)}, u32[]{:S(2)}) collective-permute-start(bf16[16,8,128]{2,1,0:T(8,128)(2,1)S(1)} %get-tuple-element.22), channel_id=1, source_target_pairs={{0,1},{1,0},{2,3},{3,2},{4,5},{5,4},{6,7},{7,6},{8,16},{9,17},{10,... | collective-permute-start | bytes 98312 | tf_op jit(solution)/shard_map/ppermute | solution.py:168
  45.6 5.1 %collective-permute-start.5 = (s32[3,8]{1,0:T(4,128)S(1)}, s32[3,8]{1,0:T(4,128)S(1)}, u32[]{:S(2)}, u32[]{:S(2)}) collective-permute-start(s32[3,8]{1,0:T(4,128)S(1)} %bitcast.21), channel_id=1, source_target_pairs={{0,2},{1,3},{2,0},{3,1},{4,6},{5,7},{6,4},{7,5},{8,10},{9,11},{10,... | collective-permute-start | bytes 296 | tf_op jit(solution)/shard_map/ppermute | solution.py:168
  47.2 4.4 %collective-permute-start.14 = (bf16[16,8,128]{2,1,0:T(8,128)(2,1)S(1)}, bf16[16,8,128]{2,1,0:T(8,128)(2,1)S(1)}, u32[]{:S(2)}, u32[]{:S(2)}) collective-permute-start(bf16[16,8,128]{2,1,0:T(8,128)(2,1)S(1)} %get-tuple-element.23.refs_1_), channel_id=1, source_target_pairs={{0,2},{1,3},{2,0},{3,1},{4,6},{5,7},{6,4},{7,5},{8,9},{9,8},{10,11... | collective-permute-start | bytes 98312 | tf_op jit(solution)/shard_map/ppermute | solution.py:168
  52.1 1.9 %collective-permute-start.16 = (bf16[16,8,128]{2,1,0:T(8,128)(2,1)S(1)}, bf16[16,8,128]{2,1,0:T(8,128)(2,1)S(1)}, u32[]{:S(2)}, u32[]{:S(2)}) collective-permute-start(bf16[16,8,128]{2,1,0:T(8,128)(2,1)S(1)} %get-tuple-element.24.refs_1_), channel_id=1, source_target_pairs={{0,1},{1,0},{2,3},{3,2},{4,5},{5,4},{6,7},{7,6},{8,9},{9,8},{10,11... | collective-permute-start | bytes 98312 | tf_op jit(solution)/shard_map/ppermute | solution.py:168
  53.0 6.3 %collective-permute-start.20 = (f32[8,8,128]{2,1,0:T(8,128)S(1)}, f32[8,8,128]{2,1,0:T(8,128)S(1)}, u32[]{:S(2)}, u32[]{:S(2)}) collective-permute-start(f32[8,8,128]{2,1,0:T(8,128)S(1)} %get-tuple-element.27.refs_5_), channel_id=1, source_target_pairs={{0,2},{1,3},{2,0},{3,1},{4,6},{5,7},{6,4},{7,5},{8,10},{9,11},{10,... | collective-permute-start | bytes 98312 | tf_op jit(solution)/shard_map/ppermute | solution.py:168
  54.6 5.1 %collective-permute-start.17 = (bf16[16,8,128]{2,1,0:T(8,128)(2,1)S(1)}, bf16[16,8,128]{2,1,0:T(8,128)(2,1)S(1)}, u32[]{:S(2)}, u32[]{:S(2)}) collective-permute-start(bf16[16,8,128]{2,1,0:T(8,128)(2,1)S(1)} %get-tuple-element.26), channel_id=1, source_target_pairs={{0,1},{1,0},{2,3},{3,2},{4,5},{5,4},{6,7},{7,6},{8,16},{9,17},{10,... | collective-permute-start | bytes 98312 | tf_op jit(solution)/shard_map/ppermute | solution.py:168
  58.4 3.7 %collective-permute-start.18 = (bf16[16,8,128]{2,1,0:T(8,128)(2,1)S(1)}, bf16[16,8,128]{2,1,0:T(8,128)(2,1)S(1)}, u32[]{:S(2)}, u32[]{:S(2)}) collective-permute-start(bf16[16,8,128]{2,1,0:T(8,128)(2,1)S(1)} %get-tuple-element.26), channel_id=1, source_target_pairs={{0,1},{1,0},{2,3},{3,2},{4,5},{5,4},{6,7},{7,6},{8,18},{9,19},{10,... | collective-permute-start | bytes 98312 | tf_op jit(solution)/shard_map/ppermute | solution.py:168
  58.6 7.5 %collective-permute-start.23 = (f32[8,8,128]{2,1,0:T(8,128)S(1)}, f32[8,8,128]{2,1,0:T(8,128)S(1)}, u32[]{:S(2)}, u32[]{:S(2)}) collective-permute-start(f32[8,8,128]{2,1,0:T(8,128)S(1)} %slice.3), channel_id=1, source_target_pairs={{0,4},{1,5},{2,6},{3,7},{4,0},{5,1},{6,2},{7,3},{8,9},{9,8},{10,11... | collective-permute-start | bytes 98312 | tf_op jit(solution)/shard_map/ppermute | solution.py:168
  62.6 3.5 %collective-permute-start.21 = (bf16[16,8,128]{2,1,0:T(8,128)(2,1)S(1)}, bf16[16,8,128]{2,1,0:T(8,128)(2,1)S(1)}, u32[]{:S(2)}, u32[]{:S(2)}) collective-permute-start(bf16[16,8,128]{2,1,0:T(8,128)(2,1)S(1)} %get-tuple-element.28), channel_id=1, source_target_pairs={{0,4},{1,5},{2,6},{3,7},{4,0},{5,1},{6,2},{7,3},{8,12},{9,13},{10,... | collective-permute-start | bytes 98312 | tf_op jit(solution)/shard_map/ppermute | solution.py:168
  63.5 5.0 %collective-permute-start.22 = (bf16[16,8,128]{2,1,0:T(8,128)(2,1)S(1)}, bf16[16,8,128]{2,1,0:T(8,128)(2,1)S(1)}, u32[]{:S(2)}, u32[]{:S(2)}) collective-permute-start(bf16[16,8,128]{2,1,0:T(8,128)(2,1)S(1)} %get-tuple-element.28), channel_id=1, source_target_pairs={{0,5},{1,4},{2,7},{3,6},{4,1},{5,0},{6,3},{7,2},{8,13},{9,12},{10,... | collective-permute-start | bytes 98312 | tf_op jit(solution)/shard_map/ppermute | solution.py:168

commit v6 on v5

--- a/solution.py
+++ b/solution.py
@@ -146,16 +146,14 @@
         return (layer + SEG // 2) % SEG >= 2
 
     everyone = {layer: layer for layer in layers}
-    early = {layer: layer for layer in layers if not plane_late(layer)}
-    late = {layer: layer for layer in layers if plane_late(layer)}
+    inner = range(SEG // 2, sweeps - SEG // 2)
+    early = {layer: layer for layer in inner if not plane_late(layer)}
+    late = {layer: layer for layer in inner if plane_late(layer)}
     late_y = {layer: layer ^ 1 for layer in late}
     starts = {layer: layer for layer in layers if place(layer) < 2}
     start_y = {layer: layer ^ 1 for layer in layers if place(layer) < 2}
     across_y = {layer: layer ^ 1 for layer in layers}
-    across_z = {
-        layer: layer + (2 if not plane_late(layer) else -2)
-        for layer in range(SEG // 2, sweeps - SEG // 2)
-    }
+    across_z = {layer: layer + (-2 if plane_late(layer) else 2) for layer in inner}
     core_flips = [f for f in range(tiles) if not f & 2]
     even_flips = [f for f in range(tiles) if not f & 1]
 

time: 69.7 us -> 69.7 us (level)
  no operation moved by 1% of the time
where the time goes in v6:
time: 69.7 us; the launch traced here: 69.5 us
  starting transfers between devices  37.8 us (54%)
  waiting for transfers between devices  26.3 us (38%)
  Pallas kernels  4.29 us (6%)
  local copies, waits for them, and re-layouts  1.05 us (2%)
    ppermute x24, starting transfers between devices, swap(): return lax.ppermute(value, AXES, route)  37.8 us
    ppermute x24, waiting for transfers between devices, swap(): return lax.ppermute(value, AXES, route)  26.3 us
    pallas_call x7, Pallas kernels, layer_apply(): pl.pallas_call(functools.partial(apply_kernel, stage, plan), in_specs=[VM...  4.25 us
  transfers between devices with their start and end apart: 24, of which 14 were waited for; matrix products, arithmetic and copies ran while one was open for 0% of the time, Pallas kernels for 5%

profile of v6, /device:TPU:9, one launch (start us, length us, event | category | flops | bytes accessed | tf_op | source)
XLA Modules:
  0.0 69.5 jit_solution(10015016631136315384)
XLA Ops:
  0.0 0.7 collective-permute-start.12
  0.7 1.7 %collective-permute-done.12.refs_4_.refs_3_ = bf16[8,4,64,128]{3,2,1,0:T(8,128)(2,1)S(1)} collective-permute-done((bf16[8,4,64,128]{3,2,1,0:T(8,128)(2,1)}, bf16[8,4,64,128]{3,2,1,0:T(8,128)(2,1)S(1)}, u32[]{:S(2)}, u32[]{:S(2)}) %collective-permute-start.12) | collective-permute-done | bytes 524320 | tf_op jit(solution)/shard_map/ppermute | solution.py:166
  2.9 1.2 %collective-permute-start.19 = (bf16[8,4,64,128]{3,2,1,0:T(8,128)(2,1)}, bf16[8,4,64,128]{3,2,1,0:T(8,128)(2,1)S(1)}, u32[]{:S(2)}, u32[]{:S(2)}) collective-permute-start(bf16[8,4,64,128]{3,2,1,0:T(8,128)(2,1)} %bitcast.13), channel_id=1, source_target_pairs={{0,1},{1,0},{2,3},{3,2},{4,5},{5,4},{6,7},{7,6},{8,10},{9,11},{10,... | collective-permute-start | bytes 1572872 | tf_op jit(solution)/shard_map/ppermute | solution.py:166
  4.2 0.7 collective-permute-start
  4.8 0.8 %collective-permute-done = s32[3,8]{1,0:T(4,128)S(1)} collective-permute-done((s32[3,8]{1,0:T(4,128)S(1)}, s32[3,8]{1,0:T(4,128)S(1)}, u32[]{:S(2)}, u32[]{:S(2)}) %collective-permute-start) | collective-permute-done | bytes 128 | tf_op jit(solution)/shard_map/ppermute | solution.py:166
  6.0 1.1 %collective-permute-done.1.refs_2_ = f32[8,8,128]{2,1,0:T(8,128)S(1)} collective-permute-done((f32[8,8,128]{2,1,0:T(8,128)}, f32[8,8,128]{2,1,0:T(8,128)S(1)}, u32[]{:S(2)}, u32[]{:S(2)}) %collective-permute-start.1) | collective-permute-done | bytes 32800 | tf_op jit(solution)/shard_map/ppermute | solution.py:166
  7.0 0.7 %collective-permute-start.2 = (f32[8,8,128]{2,1,0:T(8,128)}, f32[8,8,128]{2,1,0:T(8,128)S(1)}, u32[]{:S(2)}, u32[]{:S(2)}) collective-permute-start(f32[8,8,128]{2,1,0:T(8,128)} %bitcast.16), channel_id=1, source_target_pairs={{0,2},{1,3},{2,0},{3,1},{4,6},{5,7},{6,4},{7,5},{8,10},{9,11},{10,... | collective-permute-start | bytes 98312 | tf_op jit(solution)/shard_map/ppermute | solution.py:166
  7.7 1.0 %copy-done = bf16[1,8,4,64,128]{4,3,2,1,0:T(8,128)(2,1)S(1)} copy-done((bf16[1,8,4,64,128]{4,3,2,1,0:T(8,128)(2,1)S(1)}, bf16[1,8,4,64,128]{4,3,2,1,0:T(8,128)(2,1)}, u32[]{:S(2)}) %copy-start) | copy-done | bytes 524312
  8.8 8.1 %collective-permute-done.2.refs_3_ = f32[8,8,128]{2,1,0:T(8,128)S(1)} collective-permute-done((f32[8,8,128]{2,1,0:T(8,128)}, f32[8,8,128]{2,1,0:T(8,128)S(1)}, u32[]{:S(2)}, u32[]{:S(2)}) %collective-permute-start.2) | collective-permute-done | bytes 32800 | tf_op jit(solution)/shard_map/ppermute | solution.py:166
  17.0 2.3 %collective-permute-start.3 = (f32[8,8,128]{2,1,0:T(8,128)S(1)}, f32[8,8,128]{2,1,0:T(8,128)S(1)}, u32[]{:S(2)}, u32[]{:S(2)}) collective-permute-start(f32[8,8,128]{2,1,0:T(8,128)S(1)} %bitcast.17), channel_id=1, source_target_pairs={{0,3},{1,2},{2,1},{3,0},{4,7},{5,6},{6,5},{7,4},{8,11},{9,10},{10,... | collective-permute-start | bytes 98312 | tf_op jit(solution)/shard_map/ppermute | solution.py:166
  19.3 2.1 %collective-permute-done.3.refs_4_ = f32[8,8,128]{2,1,0:T(8,128)S(1)} collective-permute-done((f32[8,8,128]{2,1,0:T(8,128)S(1)}, f32[8,8,128]{2,1,0:T(8,128)S(1)}, u32[]{:S(2)}, u32[]{:S(2)}) %collective-permute-start.3) | collective-permute-done | bytes 32800 | tf_op jit(solution)/shard_map/ppermute | solution.py:166
  22.0 1.3 %collective-permute-start.7 = (bf16[16,8,128]{2,1,0:T(8,128)(2,1)S(1)}, bf16[16,8,128]{2,1,0:T(8,128)(2,1)S(1)}, u32[]{:S(2)}, u32[]{:S(2)}) collective-permute-start(bf16[16,8,128]{2,1,0:T(8,128)(2,1)S(1)} %get-tuple-element.19), channel_id=1, source_target_pairs={{0,4},{1,5},{2,6},{3,7},{4,0},{5,1},{6,2},{7,3},{8,12},{9,13},{10,... | collective-permute-start | bytes 98312 | tf_op jit(solution)/shard_map/ppermute | solution.py:166
  23.3 0.7 collective-permute-start.11
  23.9 0.8 %collective-permute-done.7.refs_1_ = bf16[16,8,128]{2,1,0:T(8,128)(2,1)S(1)} collective-permute-done((bf16[16,8,128]{2,1,0:T(8,128)(2,1)S(1)}, bf16[16,8,128]{2,1,0:T(8,128)(2,1)S(1)}, u32[]{:S(2)}, u32[]{:S(2)}) %collective-permute-start.7) | collective-permute-done | bytes 32800 | tf_op jit(solution)/shard_map/ppermute | solution.py:166
  24.8 1.0 %collective-permute-start.8 = (bf16[16,8,128]{2,1,0:T(8,128)(2,1)S(1)}, bf16[16,8,128]{2,1,0:T(8,128)(2,1)S(1)}, u32[]{:S(2)}, u32[]{:S(2)}) collective-permute-start(bf16[16,8,128]{2,1,0:T(8,128)(2,1)S(1)} %get-tuple-element.19), channel_id=1, source_target_pairs={{0,6},{1,7},{2,4},{3,5},{4,2},{5,3},{6,0},{7,1},{8,14},{9,15},{10,... | collective-permute-start | bytes 98312 | tf_op jit(solution)/shard_map/ppermute | solution.py:166
  25.8 2.6 %collective-permute-done.8.refs_2_ = bf16[16,8,128]{2,1,0:T(8,128)(2,1)S(1)} collective-permute-done((bf16[16,8,128]{2,1,0:T(8,128)(2,1)S(1)}, bf16[16,8,128]{2,1,0:T(8,128)(2,1)S(1)}, u32[]{:S(2)}, u32[]{:S(2)}) %collective-permute-start.8) | collective-permute-done | bytes 32800 | tf_op jit(solution)/shard_map/ppermute | solution.py:166
  28.5 2.7 %collective-permute-start.6 = (s32[6,8]{1,0:T(8,128)S(1)}, s32[6,8]{1,0:T(8,128)S(1)}, u32[]{:S(2)}, u32[]{:S(2)}) collective-permute-start(s32[6,8]{1,0:T(8,128)S(1)} %pad_add_fusion.refs_0_), channel_id=1, source_target_pairs={{0,1},{1,0},{2,3},{3,2},{4,5},{5,4},{6,7},{7,6},{8,9},{9,8},{10,11... | collective-permute-start | bytes 584 | tf_op jit(solution)/shard_map/ppermute | solution.py:166
  32.0 9.4 %collective-permute-start.10 = (bf16[16,8,128]{2,1,0:T(8,128)(2,1)S(1)}, bf16[16,8,128]{2,1,0:T(8,128)(2,1)S(1)}, u32[]{:S(2)}, u32[]{:S(2)}) collective-permute-start(bf16[16,8,128]{2,1,0:T(8,128)(2,1)S(1)} %get-tuple-element.22), channel_id=1, source_target_pairs={{0,1},{1,0},{2,3},{3,2},{4,5},{5,4},{6,7},{7,6},{8,18},{9,19},{10,... | collective-permute-start | bytes 98312 | tf_op jit(solution)/shard_map/ppermute | solution.py:166
  41.4 1.3 %collective-permute-done.10.refs_2_ = bf16[16,8,128]{2,1,0:T(8,128)(2,1)S(1)} collective-permute-done((bf16[16,8,128]{2,1,0:T(8,128)(2,1)S(1)}, bf16[16,8,128]{2,1,0:T(8,128)(2,1)S(1)}, u32[]{:S(2)}, u32[]{:S(2)}) %collective-permute-start.10) | collective-permute-done | bytes 32800 | tf_op jit(solution)/shard_map/ppermute | solution.py:166
  42.7 1.6 %collective-permute-start.9 = (bf16[16,8,128]{2,1,0:T(8,128)(2,1)S(1)}, bf16[16,8,128]{2,1,0:T(8,128)(2,1)S(1)}, u32[]{:S(2)}, u32[]{:S(2)}) collective-permute-start(bf16[16,8,128]{2,1,0:T(8,128)(2,1)S(1)} %get-tuple-element.22), channel_id=1, source_target_pairs={{0,1},{1,0},{2,3},{3,2},{4,5},{5,4},{6,7},{7,6},{8,16},{9,17},{10,... | collective-permute-start | bytes 98312 | tf_op jit(solution)/shard_map/ppermute | solution.py:166
  44.3 1.3 %collective-permute-done.9.refs_1_ = bf16[16,8,128]{2,1,0:T(8,128)(2,1)S(1)} collective-permute-done((bf16[16,8,128]{2,1,0:T(8,128)(2,1)S(1)}, bf16[16,8,128]{2,1,0:T(8,128)(2,1)S(1)}, u32[]{:S(2)}, u32[]{:S(2)}) %collective-permute-start.9) | collective-permute-done | bytes 32800 | tf_op jit(solution)/shard_map/ppermute | solution.py:166
  45.6 1.0 %collective-permute-start.5 = (s32[3,8]{1,0:T(4,128)S(1)}, s32[3,8]{1,0:T(4,128)S(1)}, u32[]{:S(2)}, u32[]{:S(2)}) collective-permute-start(s32[3,8]{1,0:T(4,128)S(1)} %bitcast.21), channel_id=1, source_target_pairs={{0,2},{1,3},{2,0},{3,1},{4,6},{5,7},{6,4},{7,5},{8,10},{9,11},{10,... | collective-permute-start | bytes 296 | tf_op jit(solution)/shard_map/ppermute | solution.py:166
  47.2 3.5 %collective-permute-start.14 = (bf16[16,8,128]{2,1,0:T(8,128)(2,1)S(1)}, bf16[16,8,128]{2,1,0:T(8,128)(2,1)S(1)}, u32[]{:S(2)}, u32[]{:S(2)}) collective-permute-start(bf16[16,8,128]{2,1,0:T(8,128)(2,1)S(1)} %get-tuple-element.23.refs_1_), channel_id=1, source_target_pairs={{0,1},{1,0},{2,3},{3,2},{4,5},{5,4},{6,7},{7,6},{8,9},{9,8},{10,11... | collective-permute-start | bytes 98312 | tf_op jit(solution)/shard_map/ppermute | solution.py:166
  50.7 0.8 %collective-permute-done.14.refs_2_ = bf16[16,8,128]{2,1,0:T(8,128)(2,1)S(1)} collective-permute-done((bf16[16,8,128]{2,1,0:T(8,128)(2,1)S(1)}, bf16[16,8,128]{2,1,0:T(8,128)(2,1)S(1)}, u32[]{:S(2)}, u32[]{:S(2)}) %collective-permute-start.14) | collective-permute-done | bytes 32800 | tf_op jit(solution)/shard_map/ppermute | solution.py:166
  52.1 0.9 %collective-permute-start.16 = (bf16[16,8,128]{2,1,0:T(8,128)(2,1)S(1)}, bf16[16,8,128]{2,1,0:T(8,128)(2,1)S(1)}, u32[]{:S(2)}, u32[]{:S(2)}) collective-permute-start(bf16[16,8,128]{2,1,0:T(8,128)(2,1)S(1)} %get-tuple-element.24.refs_1_), channel_id=1, source_target_pairs={{0,1},{1,0},{2,3},{3,2},{4,5},{5,4},{6,7},{7,6},{8,9},{9,8},{10,11... | collective-permute-start | bytes 98312 | tf_op jit(solution)/shard_map/ppermute | solution.py:166
  53.0 1.0 %collective-permute-start.20 = (f32[8,8,128]{2,1,0:T(8,128)S(1)}, f32[8,8,128]{2,1,0:T(8,128)S(1)}, u32[]{:S(2)}, u32[]{:S(2)}) collective-permute-start(f32[8,8,128]{2,1,0:T(8,128)S(1)} %get-tuple-element.27.refs_5_), channel_id=1, source_target_pairs={{0,2},{1,3},{2,0},{3,1},{4,6},{5,7},{6,4},{7,5},{8,10},{9,11},{10,... | collective-permute-start | bytes 98312 | tf_op jit(solution)/shard_map/ppermute | solution.py:166
  54.6 3.8 %collective-permute-start.17 = (bf16[16,8,128]{2,1,0:T(8,128)(2,1)S(1)}, bf16[16,8,128]{2,1,0:T(8,128)(2,1)S(1)}, u32[]{:S(2)}, u32[]{:S(2)}) collective-permute-start(bf16[16,8,128]{2,1,0:T(8,128)(2,1)S(1)} %get-tuple-element.26), channel_id=1, source_target_pairs={{0,1},{1,0},{2,3},{3,2},{4,5},{5,4},{6,7},{7,6},{8,16},{9,17},{10,... | collective-permute-start | bytes 98312 | tf_op jit(solution)/shard_map/ppermute | solution.py:166
  59.7 2.4 %collective-permute-done.18.refs_2_ = bf16[16,8,128]{2,1,0:T(8,128)(2,1)S(1)} collective-permute-done((bf16[16,8,128]{2,1,0:T(8,128)(2,1)S(1)}, bf16[16,8,128]{2,1,0:T(8,128)(2,1)S(1)}, u32[]{:S(2)}, u32[]{:S(2)}) %collective-permute-start.18) | collective-permute-done | bytes 32800 | tf_op jit(solution)/shard_map/ppermute | solution.py:166
  62.6 0.9 %collective-permute-start.21 = (bf16[16,8,128]{2,1,0:T(8,128)(2,1)S(1)}, bf16[16,8,128]{2,1,0:T(8,128)(2,1)S(1)}, u32[]{:S(2)}, u32[]{:S(2)}) collective-permute-start(bf16[16,8,128]{2,1,0:T(8,128)(2,1)S(1)} %get-tuple-element.28), channel_id=1, source_target_pairs={{0,4},{1,5},{2,6},{3,7},{4,0},{5,1},{6,2},{7,3},{8,12},{9,13},{10,... | collective-permute-start | bytes 98312 | tf_op jit(solution)/shard_map/ppermute | solution.py:166
  63.5 2.6 %collective-permute-start.22 = (bf16[16,8,128]{2,1,0:T(8,128)(2,1)S(1)}, bf16[16,8,128]{2,1,0:T(8,128)(2,1)S(1)}, u32[]{:S(2)}, u32[]{:S(2)}) collective-permute-start(bf16[16,8,128]{2,1,0:T(8,128)(2,1)S(1)} %get-tuple-element.28), channel_id=1, source_target_pairs={{0,5},{1,4},{2,7},{3,6},{4,1},{5,0},{6,3},{7,2},{8,13},{9,12},{10,... | collective-permute-start | bytes 98312 | tf_op jit(solution)/shard_map/ppermute | solution.py:166
  66.1 2.4 %collective-permute-done.22.refs_2_ = bf16[16,8,128]{2,1,0:T(8,128)(2,1)S(1)} collective-permute-done((bf16[16,8,128]{2,1,0:T(8,128)(2,1)S(1)}, bf16[16,8,128]{2,1,0:T(8,128)(2,1)S(1)}, u32[]{:S(2)}, u32[]{:S(2)}) %collective-permute-start.22) | collective-permute-done | bytes 32800 | tf_op jit(solution)/shard_map/ppermute | solution.py:166
  68.5 1.0 %shard_map.43 = f32[8,1024]{1,0:T(8,128)} custom-call(s32[6,8]{1,0:T(8,128)S(1)} %pad_add_fusion.refs_0_, bf16[16,8,128]{2,1,0:T(8,128)(2,1)S(1)} %collective-permute-done.21.refs_1_, bf16[16,8,128]{2,1,0:T(8,128)(2,1)S(1)} %collective-permute-done.22.refs_2_, bf16[8,4,64,128]{3,2,1,0:T(8,128)(2,1)S(1)} %stage_in.1.refs_5_.refs_4_.refs_3_, ...), custom_call_target="tpu_custom_call" | custom-call | tf_op jit(solution)/shard_map/pallas_call | solution.py:108
  (34 shorter events, 5.8 us)
Async XLA Ops:
  0.0 4.2 %copy-start.2 = (s32[1,8,3]{1,0,2:T(1,128)S(1)}, s32[1,8,3]{1,0,2:T(1,128)}, u32[]{:S(2)}) copy-start(s32[1,8,3]{1,0,2:T(1,128)} %param.5) | copy-start | bytes 292
  0.0 2.4 %collective-permute-start.12 = (bf16[8,4,64,128]{3,2,1,0:T(8,128)(2,1)}, bf16[8,4,64,128]{3,2,1,0:T(8,128)(2,1)S(1)}, u32[]{:S(2)}, u32[]{:S(2)}) collective-permute-start(bf16[8,4,64,128]{3,2,1,0:T(8,128)(2,1)} %bitcast.10), channel_id=1, source_target_pairs={{0,1},{1,0},{2,3},{3,2},{4,5},{5,4},{6,7},{7,6},{8,9},{9,8},{10,11... | collective-permute-start | bytes 1572872 | tf_op jit(solution)/shard_map/ppermute | solution.py:166
  0.7 20.8 %collective-permute-start.4 = (bf16[8,4,64,128]{3,2,1,0:T(8,128)(2,1)}, bf16[8,4,64,128]{3,2,1,0:T(8,128)(2,1)S(1)}, u32[]{:S(2)}, u32[]{:S(2)}) collective-permute-start(bf16[8,4,64,128]{3,2,1,0:T(8,128)(2,1)} %bitcast.11), channel_id=1, source_target_pairs={{0,1},{1,0},{2,3},{3,2},{4,5},{5,4},{6,7},{7,6},{8,9},{9,8},{10,11... | collective-permute-start | bytes 1572872 | tf_op jit(solution)/shard_map/ppermute | solution.py:166
  2.4 44.2 %collective-permute-start.13 = (bf16[8,4,64,128]{3,2,1,0:T(8,128)(2,1)S(1)}, bf16[8,4,64,128]{3,2,1,0:T(8,128)(2,1)S(1)}, u32[]{:S(2)}, u32[]{:S(2)}) collective-permute-start(bf16[8,4,64,128]{3,2,1,0:T(8,128)(2,1)S(1)} %collective-permute-done.12.refs_4_.refs_3_), channel_id=1, source_target_pairs={{0,1},{1,0},{2,3},{3,2},{4,5},{5,4},{6,7},{7,6},{8,9},{9,8},{10,11... | collective-permute-start | bytes 1572872 | tf_op jit(solution)/shard_map/ppermute | solution.py:166
  2.8 47.9 %collective-permute-start.15 = (bf16[8,4,64,128]{3,2,1,0:T(8,128)(2,1)}, bf16[8,4,64,128]{3,2,1,0:T(8,128)(2,1)S(1)}, u32[]{:S(2)}, u32[]{:S(2)}) collective-permute-start(bf16[8,4,64,128]{3,2,1,0:T(8,128)(2,1)} %bitcast.12), channel_id=1, source_target_pairs={{0,1},{1,0},{2,3},{3,2},{4,5},{5,4},{6,7},{7,6},{8,9},{9,8},{10,11... | collective-permute-start | bytes 1572872 | tf_op jit(solution)/shard_map/ppermute | solution.py:166
  2.9 56.3 %collective-permute-start.19 = (bf16[8,4,64,128]{3,2,1,0:T(8,128)(2,1)}, bf16[8,4,64,128]{3,2,1,0:T(8,128)(2,1)S(1)}, u32[]{:S(2)}, u32[]{:S(2)}) collective-permute-start(bf16[8,4,64,128]{3,2,1,0:T(8,128)(2,1)} %bitcast.13), channel_id=1, source_target_pairs={{0,1},{1,0},{2,3},{3,2},{4,5},{5,4},{6,7},{7,6},{8,10},{9,11},{10,... | collective-permute-start | bytes 1572872 | tf_op jit(solution)/shard_map/ppermute | solution.py:166
  4.2 1.5 %collective-permute-start = (s32[3,8]{1,0:T(4,128)S(1)}, s32[3,8]{1,0:T(4,128)S(1)}, u32[]{:S(2)}, u32[]{:S(2)}) collective-permute-start(s32[3,8]{1,0:T(4,128)S(1)} %bitcast.19), channel_id=1, source_target_pairs={{0,1},{1,0},{2,3},{3,2},{4,5},{5,4},{6,7},{7,6},{8,9},{9,8},{10,11... | collective-permute-start | bytes 296 | tf_op jit(solution)/shard_map/ppermute | solution.py:166
  5.6 1.4 %collective-permute-start.1 = (f32[8,8,128]{2,1,0:T(8,128)}, f32[8,8,128]{2,1,0:T(8,128)S(1)}, u32[]{:S(2)}, u32[]{:S(2)}) collective-permute-start(f32[8,8,128]{2,1,0:T(8,128)} %bitcast.15), channel_id=1, source_target_pairs={{0,1},{1,0},{2,3},{3,2},{4,5},{5,4},{6,7},{7,6},{8,9},{9,8},{10,11... | collective-permute-start | bytes 98312 | tf_op jit(solution)/shard_map/ppermute | solution.py:166
  7.0 9.9 %collective-permute-start.2 = (f32[8,8,128]{2,1,0:T(8,128)}, f32[8,8,128]{2,1,0:T(8,128)S(1)}, u32[]{:S(2)}, u32[]{:S(2)}) collective-permute-start(f32[8,8,128]{2,1,0:T(8,128)} %bitcast.16), channel_id=1, source_target_pairs={{0,2},{1,3},{2,0},{3,1},{4,6},{5,7},{6,4},{7,5},{8,10},{9,11},{10,... | collective-permute-start | bytes 98312 | tf_op jit(solution)/shard_map/ppermute | solution.py:166
  7.7 1.0 %copy-start = (bf16[1,8,4,64,128]{4,3,2,1,0:T(8,128)(2,1)S(1)}, bf16[1,8,4,64,128]{4,3,2,1,0:T(8,128)(2,1)}, u32[]{:S(2)}) copy-start(bf16[1,8,4,64,128]{4,3,2,1,0:T(8,128)(2,1)} %param.4) | copy-start | bytes 1572868
  8.8 8.2 %copy-start.1 = (f32[1,8,1024]{2,1,0:T(8,128)S(1)}, f32[1,8,1024]{2,1,0:T(8,128)}, u32[]{:S(2)}) copy-start(f32[1,8,1024]{2,1,0:T(8,128)} %param.3) | copy-start | bytes 98308
  17.0 4.5 %collective-permute-start.3 = (f32[8,8,128]{2,1,0:T(8,128)S(1)}, f32[8,8,128]{2,1,0:T(8,128)S(1)}, u32[]{:S(2)}, u32[]{:S(2)}) collective-permute-start(f32[8,8,128]{2,1,0:T(8,128)S(1)} %bitcast.17), channel_id=1, source_target_pairs={{0,3},{1,2},{2,1},{3,0},{4,7},{5,6},{6,5},{7,4},{8,11},{9,10},{10,... | collective-permute-start | bytes 98312 | tf_op jit(solution)/shard_map/ppermute | solution.py:166
  22.0 2.8 %collective-permute-start.7 = (bf16[16,8,128]{2,1,0:T(8,128)(2,1)S(1)}, bf16[16,8,128]{2,1,0:T(8,128)(2,1)S(1)}, u32[]{:S(2)}, u32[]{:S(2)}) collective-permute-start(bf16[16,8,128]{2,1,0:T(8,128)(2,1)S(1)} %get-tuple-element.19), channel_id=1, source_target_pairs={{0,4},{1,5},{2,6},{3,7},{4,0},{5,1},{6,2},{7,3},{8,12},{9,13},{10,... | collective-permute-start | bytes 98312 | tf_op jit(solution)/shard_map/ppermute | solution.py:166
  23.3 23.4 %collective-permute-start.11 = (f32[32,8,128]{2,1,0:T(8,128)S(1)}, f32[32,8,128]{2,1,0:T(8,128)S(1)}, u32[]{:S(2)}, u32[]{:S(2)}) collective-permute-start(f32[32,8,128]{2,1,0:T(8,128)S(1)} %get-tuple-element.21.refs_3_), channel_id=1, source_target_pairs={{0,1},{1,0},{2,3},{3,2},{4,5},{5,4},{6,7},{7,6},{8,9},{9,8},{10,11... | collective-permute-start | bytes 393224 | tf_op jit(solution)/shard_map/ppermute | solution.py:166
  24.8 3.7 %collective-permute-start.8 = (bf16[16,8,128]{2,1,0:T(8,128)(2,1)S(1)}, bf16[16,8,128]{2,1,0:T(8,128)(2,1)S(1)}, u32[]{:S(2)}, u32[]{:S(2)}) collective-permute-start(bf16[16,8,128]{2,1,0:T(8,128)(2,1)S(1)} %get-tuple-element.19), channel_id=1, source_target_pairs={{0,6},{1,7},{2,4},{3,5},{4,2},{5,3},{6,0},{7,1},{8,14},{9,15},{10,... | collective-permute-start | bytes 98312 | tf_op jit(solution)/shard_map/ppermute | solution.py:166
  28.5 3.5 %collective-permute-start.6 = (s32[6,8]{1,0:T(8,128)S(1)}, s32[6,8]{1,0:T(8,128)S(1)}, u32[]{:S(2)}, u32[]{:S(2)}) collective-permute-start(s32[6,8]{1,0:T(8,128)S(1)} %pad_add_fusion.refs_0_), channel_id=1, source_target_pairs={{0,1},{1,0},{2,3},{3,2},{4,5},{5,4},{6,7},{7,6},{8,9},{9,8},{10,11... | collective-permute-start | bytes 584 | tf_op jit(solution)/shard_map/ppermute | solution.py:166
  32.0 10.7 %collective-permute-start.10 = (bf16[16,8,128]{2,1,0:T(8,128)(2,1)S(1)}, bf16[16,8,128]{2,1,0:T(8,128)(2,1)S(1)}, u32[]{:S(2)}, u32[]{:S(2)}) collective-permute-start(bf16[16,8,128]{2,1,0:T(8,128)(2,1)S(1)} %get-tuple-element.22), channel_id=1, source_target_pairs={{0,1},{1,0},{2,3},{3,2},{4,5},{5,4},{6,7},{7,6},{8,18},{9,19},{10,... | collective-permute-start | bytes 98312 | tf_op jit(solution)/shard_map/ppermute | solution.py:166
  42.7 2.9 %collective-permute-start.9 = (bf16[16,8,128]{2,1,0:T(8,128)(2,1)S(1)}, bf16[16,8,128]{2,1,0:T(8,128)(2,1)S(1)}, u32[]{:S(2)}, u32[]{:S(2)}) collective-permute-start(bf16[16,8,128]{2,1,0:T(8,128)(2,1)S(1)} %get-tuple-element.22), channel_id=1, source_target_pairs={{0,1},{1,0},{2,3},{3,2},{4,5},{5,4},{6,7},{7,6},{8,16},{9,17},{10,... | collective-permute-start | bytes 98312 | tf_op jit(solution)/shard_map/ppermute | solution.py:166
  45.6 5.1 %collective-permute-start.5 = (s32[3,8]{1,0:T(4,128)S(1)}, s32[3,8]{1,0:T(4,128)S(1)}, u32[]{:S(2)}, u32[]{:S(2)}) collective-permute-start(s32[3,8]{1,0:T(4,128)S(1)} %bitcast.21), channel_id=1, source_target_pairs={{0,2},{1,3},{2,0},{3,1},{4,6},{5,7},{6,4},{7,5},{8,10},{9,11},{10,... | collective-permute-start | bytes 296 | tf_op jit(solution)/shard_map/ppermute | solution.py:166
  47.2 4.4 %collective-permute-start.14 = (bf16[16,8,128]{2,1,0:T(8,128)(2,1)S(1)}, bf16[16,8,128]{2,1,0:T(8,128)(2,1)S(1)}, u32[]{:S(2)}, u32[]{:S(2)}) collective-permute-start(bf16[16,8,128]{2,1,0:T(8,128)(2,1)S(1)} %get-tuple-element.23.refs_1_), channel_id=1, source_target_pairs={{0,1},{1,0},{2,3},{3,2},{4,5},{5,4},{6,7},{7,6},{8,9},{9,8},{10,11... | collective-permute-start | bytes 98312 | tf_op jit(solution)/shard_map/ppermute | solution.py:166
  52.1 1.9 %collective-permute-start.16 = (bf16[16,8,128]{2,1,0:T(8,128)(2,1)S(1)}, bf16[16,8,128]{2,1,0:T(8,128)(2,1)S(1)}, u32[]{:S(2)}, u32[]{:S(2)}) collective-permute-start(bf16[16,8,128]{2,1,0:T(8,128)(2,1)S(1)} %get-tuple-element.24.refs_1_), channel_id=1, source_target_pairs={{0,1},{1,0},{2,3},{3,2},{4,5},{5,4},{6,7},{7,6},{8,9},{9,8},{10,11... | collective-permute-start | bytes 98312 | tf_op jit(solution)/shard_map/ppermute | solution.py:166
  53.0 6.3 %collective-permute-start.20 = (f32[8,8,128]{2,1,0:T(8,128)S(1)}, f32[8,8,128]{2,1,0:T(8,128)S(1)}, u32[]{:S(2)}, u32[]{:S(2)}) collective-permute-start(f32[8,8,128]{2,1,0:T(8,128)S(1)} %get-tuple-element.27.refs_5_), channel_id=1, source_target_pairs={{0,2},{1,3},{2,0},{3,1},{4,6},{5,7},{6,4},{7,5},{8,10},{9,11},{10,... | collective-permute-start | bytes 98312 | tf_op jit(solution)/shard_map/ppermute | solution.py:166
  54.6 5.1 %collective-permute-start.17 = (bf16[16,8,128]{2,1,0:T(8,128)(2,1)S(1)}, bf16[16,8,128]{2,1,0:T(8,128)(2,1)S(1)}, u32[]{:S(2)}, u32[]{:S(2)}) collective-permute-start(bf16[16,8,128]{2,1,0:T(8,128)(2,1)S(1)} %get-tuple-element.26), channel_id=1, source_target_pairs={{0,1},{1,0},{2,3},{3,2},{4,5},{5,4},{6,7},{7,6},{8,16},{9,17},{10,... | collective-permute-start | bytes 98312 | tf_op jit(solution)/shard_map/ppermute | solution.py:166
  58.4 3.7 %collective-permute-start.18 = (bf16[16,8,128]{2,1,0:T(8,128)(2,1)S(1)}, bf16[16,8,128]{2,1,0:T(8,128)(2,1)S(1)}, u32[]{:S(2)}, u32[]{:S(2)}) collective-permute-start(bf16[16,8,128]{2,1,0:T(8,128)(2,1)S(1)} %get-tuple-element.26), channel_id=1, source_target_pairs={{0,1},{1,0},{2,3},{3,2},{4,5},{5,4},{6,7},{7,6},{8,18},{9,19},{10,... | collective-permute-start | bytes 98312 | tf_op jit(solution)/shard_map/ppermute | solution.py:166
  58.6 7.5 %collective-permute-start.23 = (f32[8,8,128]{2,1,0:T(8,128)S(1)}, f32[8,8,128]{2,1,0:T(8,128)S(1)}, u32[]{:S(2)}, u32[]{:S(2)}) collective-permute-start(f32[8,8,128]{2,1,0:T(8,128)S(1)} %slice.3), channel_id=1, source_target_pairs={{0,1},{1,0},{2,3},{3,2},{4,5},{5,4},{6,7},{7,6},{8,9},{9,8},{10,11... | collective-permute-start | bytes 98312 | tf_op jit(solution)/shard_map/ppermute | solution.py:166
  62.6 3.5 %collective-permute-start.21 = (bf16[16,8,128]{2,1,0:T(8,128)(2,1)S(1)}, bf16[16,8,128]{2,1,0:T(8,128)(2,1)S(1)}, u32[]{:S(2)}, u32[]{:S(2)}) collective-permute-start(bf16[16,8,128]{2,1,0:T(8,128)(2,1)S(1)} %get-tuple-element.28), channel_id=1, source_target_pairs={{0,4},{1,5},{2,6},{3,7},{4,0},{5,1},{6,2},{7,3},{8,12},{9,13},{10,... | collective-permute-start | bytes 98312 | tf_op jit(solution)/shard_map/ppermute | solution.py:166
  63.5 5.0 %collective-permute-start.22 = (bf16[16,8,128]{2,1,0:T(8,128)(2,1)S(1)}, bf16[16,8,128]{2,1,0:T(8,128)(2,1)S(1)}, u32[]{:S(2)}, u32[]{:S(2)}) collective-permute-start(bf16[16,8,128]{2,1,0:T(8,128)(2,1)S(1)} %get-tuple-element.28), channel_id=1, source_target_pairs={{0,5},{1,4},{2,7},{3,6},{4,1},{5,0},{6,3},{7,2},{8,13},{9,12},{10,... | collective-permute-start | bytes 98312 | tf_op jit(solution)/shard_map/ppermute | solution.py:166

commit v7 on v6

--- a/solution.py
+++ b/solution.py
@@ -39,11 +39,13 @@
     for rec, flips in zip(recs, rec_flips):
         for index, flip in enumerate(flips):
             value = rec[pl.ds(index * nb, nb)].astype(jnp.float32)
+            if stage == 5:
+                flip = flip ^ (2 * (lax.axis_index("tile") & 1))
             slots = pl.ds(flip * nb, nb)
             if keep_src:
                 src_out[slots] = value
             if add_src:
-                value = value + srcs[0][slots]
+                value = value + srcs[0][slots].astype(jnp.float32)
             value = value.astype(jnp.bfloat16).astype(jnp.float32)
             imag_in = pltpu.roll(value, half, axis=2)
             pair = jnp.concatenate([value * sign, imag_in], axis=1)
@@ -153,16 +155,17 @@
     starts = {layer: layer for layer in layers if place(layer) < 2}
     start_y = {layer: layer ^ 1 for layer in layers if place(layer) < 2}
     across_y = {layer: layer ^ 1 for layer in layers}
-    across_z = {layer: layer + (-2 if plane_late(layer) else 2) for layer in inner}
+    across_z = {layer: layer + (-2 if plane_late(layer) else 2) for layer in inner if layer & 1}
     core_flips = [f for f in range(tiles) if not f & 2]
     even_flips = [f for f in range(tiles) if not f & 1]
 
-    def swap(value, pairs, flip):
+    def swap(value, pairs, flip, odd_flip=0):
         route = []
         for layer in layers:
-            mask = flip if layer in pairs else 1
-            other = pairs.get(layer, layer)
-            route += [(layer * tiles + t, other * tiles + (t ^ mask)) for t in range(tiles)]
+            for t in range(tiles):
+                mask = flip ^ (odd_flip * (t & 1)) if layer in pairs else 1
+                other = pairs.get(layer, layer)
+                route.append((layer * tiles + t, other * tiles + (t ^ mask)))
         return lax.ppermute(value, AXES, route)
 
     def hop(msg, pairs, flips, other, own=False):
@@ -170,6 +173,15 @@
         for f in flips:
             if f or not own:
                 recs.append((swap(msg, pairs, f), (f, f ^ other)))
+        return recs
+
+    def chip_hop(msg, pairs, other, odd_flip):
+        recs = []
+        for f in range(0, tiles, 4):
+            far = swap(msg, pairs, f, odd_flip)
+            near = swap(far, everyone, 1)
+            flip = f ^ odd_flip ^ 1
+            recs += [(far, (f, f ^ other)), (near, (flip, flip ^ other))]
         return recs
 
     src_own = sources[0].reshape(rhs, nb, width).transpose(1, 0, 2)
@@ -189,7 +201,7 @@
     recs = hop(msg, start_y, even_flips, 1)
 
     y_patterns = swap(core_patterns, late_y, 0)
-    src_other = swap(src_all, late_y, 0)
+    src_other = swap(src_all.astype(jnp.bfloat16), late_y, 0)
     later_pattern = lax.optimization_barrier((own_pattern, msg))[0]
     x_pattern = swap(later_pattern, everyone, 2)
     x_patterns = jnp.concatenate([later_pattern, x_pattern], axis=0)
@@ -209,7 +221,7 @@
     down_3, msg = layer_apply(3, recs=recs, blocks=[own, x_blocks], src=src_all, **x_rows)
     recs = hop(msg, everyone, core_flips, 2, own=True)
     up_2, msg = layer_apply(4, recs=recs, states=[down_2], **other_rows)
-    recs = hop(msg, across_z, even_flips, 1)
+    recs = chip_hop(msg, across_z, 1, 2)
     up_2_own = swap(up_2[:nb], late_y, 0)
     up_1, msg = layer_apply(
         5, recs=recs, blocks=[own, x_late], states=[down_1, down_1_x], **x_rows

time: 69.7 us -> 64.7 us (0.928)
  the two profiles are of different devices: /device:TPU:9 before, /device:TPU:17 now
where the time goes in v7:
time: 64.7 us; the launch traced here: 64.6 us
  waiting for transfers between devices  33.2 us (51%)
  starting transfers between devices  25.9 us (40%)
  Pallas kernels  4.3 us (7%)
  local copies, waits for them, and re-layouts  1.05 us (2%)
    ppermute x24, waiting for transfers between devices, swap(): return lax.ppermute(value, AXES, route)  33.2 us
    ppermute x24, starting transfers between devices, swap(): return lax.ppermute(value, AXES, route)  25.9 us
    pallas_call x7, Pallas kernels, layer_apply(): pl.pallas_call(functools.partial(apply_kernel, stage, plan), in_specs=[VM...  4.25 us
  transfers between devices with their start and end apart: 24, of which 14 were waited for; matrix products, arithmetic and copies ran while one was open for 0% of the time, Pallas kernels for 5%

profile of v7, /device:TPU:17, one launch (start us, length us, event | category | flops | bytes accessed | tf_op | source)
XLA Modules:
  0.0 64.6 jit_solution(5447990685103468117)
XLA Ops:
  0.0 1.2 %collective-permute-start.12 = (bf16[8,4,64,128]{3,2,1,0:T(8,128)(2,1)}, bf16[8,4,64,128]{3,2,1,0:T(8,128)(2,1)S(1)}, u32[]{:S(2)}, u32[]{:S(2)}) collective-permute-start(bf16[8,4,64,128]{3,2,1,0:T(8,128)(2,1)} %bitcast.10), channel_id=1, source_target_pairs={{0,1},{1,0},{2,3},{3,2},{4,5},{5,4},{6,7},{7,6},{8,9},{9,8},{10,11... | collective-permute-start | bytes 1572872 | tf_op jit(solution)/shard_map/ppermute | solution.py:169
  1.2 1.0 %collective-permute-start.4 = (bf16[8,4,64,128]{3,2,1,0:T(8,128)(2,1)}, bf16[8,4,64,128]{3,2,1,0:T(8,128)(2,1)S(1)}, u32[]{:S(2)}, u32[]{:S(2)}) collective-permute-start(bf16[8,4,64,128]{3,2,1,0:T(8,128)(2,1)} %bitcast.11), channel_id=1, source_target_pairs={{0,1},{1,0},{2,3},{3,2},{4,5},{5,4},{6,7},{7,6},{8,9},{9,8},{10,11... | collective-permute-start | bytes 1572872 | tf_op jit(solution)/shard_map/ppermute | solution.py:169
  2.2 10.8 %collective-permute-done.12.refs_4_.refs_3_ = bf16[8,4,64,128]{3,2,1,0:T(8,128)(2,1)S(1)} collective-permute-done((bf16[8,4,64,128]{3,2,1,0:T(8,128)(2,1)}, bf16[8,4,64,128]{3,2,1,0:T(8,128)(2,1)S(1)}, u32[]{:S(2)}, u32[]{:S(2)}) %collective-permute-start.12) | collective-permute-done | bytes 524320 | tf_op jit(solution)/shard_map/ppermute | solution.py:169
  13.0 1.5 %collective-permute-start.13 = (bf16[8,4,64,128]{3,2,1,0:T(8,128)(2,1)S(1)}, bf16[8,4,64,128]{3,2,1,0:T(8,128)(2,1)S(1)}, u32[]{:S(2)}, u32[]{:S(2)}) collective-permute-start(bf16[8,4,64,128]{3,2,1,0:T(8,128)(2,1)S(1)} %collective-permute-done.12.refs_4_.refs_3_), channel_id=1, source_target_pairs={{0,1},{1,0},{2,3},{3,2},{4,5},{5,4},{6,7},{7,6},{8,9},{9,8},{10,11... | collective-permute-start | bytes 1572872 | tf_op jit(solution)/shard_map/ppermute | solution.py:169
  14.6 1.2 %collective-permute-start.15 = (bf16[8,4,64,128]{3,2,1,0:T(8,128)(2,1)}, bf16[8,4,64,128]{3,2,1,0:T(8,128)(2,1)S(1)}, u32[]{:S(2)}, u32[]{:S(2)}) collective-permute-start(bf16[8,4,64,128]{3,2,1,0:T(8,128)(2,1)} %bitcast.12), channel_id=1, source_target_pairs={{0,1},{1,0},{2,3},{3,2},{4,5},{5,4},{6,7},{7,6},{8,9},{9,8},{10,11... | collective-permute-start | bytes 1572872 | tf_op jit(solution)/shard_map/ppermute | solution.py:169
  16.3 1.6 %collective-permute-done = s32[3,8]{1,0:T(4,128)S(1)} collective-permute-done((s32[3,8]{1,0:T(4,128)S(1)}, s32[3,8]{1,0:T(4,128)S(1)}, u32[]{:S(2)}, u32[]{:S(2)}) %collective-permute-start) | collective-permute-done | bytes 128 | tf_op jit(solution)/shard_map/ppermute | solution.py:169
  18.2 1.1 %collective-permute-done.1.refs_2_ = f32[8,8,128]{2,1,0:T(8,128)S(1)} collective-permute-done((f32[8,8,128]{2,1,0:T(8,128)}, f32[8,8,128]{2,1,0:T(8,128)S(1)}, u32[]{:S(2)}, u32[]{:S(2)}) %collective-permute-start.1) | collective-permute-done | bytes 32800 | tf_op jit(solution)/shard_map/ppermute | solution.py:169
  19.6 1.0 %copy-done = bf16[1,8,4,64,128]{4,3,2,1,0:T(8,128)(2,1)S(1)} copy-done((bf16[1,8,4,64,128]{4,3,2,1,0:T(8,128)(2,1)S(1)}, bf16[1,8,4,64,128]{4,3,2,1,0:T(8,128)(2,1)}, u32[]{:S(2)}) %copy-start) | copy-done | bytes 524312
  20.7 8.3 %collective-permute-done.2.refs_3_ = f32[8,8,128]{2,1,0:T(8,128)S(1)} collective-permute-done((f32[8,8,128]{2,1,0:T(8,128)}, f32[8,8,128]{2,1,0:T(8,128)S(1)}, u32[]{:S(2)}, u32[]{:S(2)}) %collective-permute-start.2) | collective-permute-done | bytes 32800 | tf_op jit(solution)/shard_map/ppermute | solution.py:169
  28.9 2.0 %collective-permute-start.3 = (f32[8,8,128]{2,1,0:T(8,128)S(1)}, f32[8,8,128]{2,1,0:T(8,128)S(1)}, u32[]{:S(2)}, u32[]{:S(2)}) collective-permute-start(f32[8,8,128]{2,1,0:T(8,128)S(1)} %bitcast.17), channel_id=1, source_target_pairs={{0,3},{1,2},{2,1},{3,0},{4,7},{5,6},{6,5},{7,4},{8,11},{9,10},{10,... | collective-permute-start | bytes 98312 | tf_op jit(solution)/shard_map/ppermute | solution.py:169
  30.9 2.1 %collective-permute-done.3.refs_4_ = f32[8,8,128]{2,1,0:T(8,128)S(1)} collective-permute-done((f32[8,8,128]{2,1,0:T(8,128)S(1)}, f32[8,8,128]{2,1,0:T(8,128)S(1)}, u32[]{:S(2)}, u32[]{:S(2)}) %collective-permute-start.3) | collective-permute-done | bytes 32800 | tf_op jit(solution)/shard_map/ppermute | solution.py:169
  33.1 0.5 shard_map.37
  34.0 1.3 %collective-permute-start.11 = (bf16[32,8,128]{2,1,0:T(8,128)(2,1)S(1)}, bf16[32,8,128]{2,1,0:T(8,128)(2,1)S(1)}, u32[]{:S(2)}, u32[]{:S(2)}) collective-permute-start(bf16[32,8,128]{2,1,0:T(8,128)(2,1)S(1)} %convert_element_type.3), channel_id=1, source_target_pairs={{0,1},{1,0},{2,3},{3,2},{4,5},{5,4},{6,7},{7,6},{8,9},{9,8},{10,11... | collective-permute-start | bytes 196616 | tf_op jit(solution)/shard_map/ppermute | solution.py:169
  35.8 0.9 %collective-permute-done.8.refs_2_ = bf16[16,8,128]{2,1,0:T(8,128)(2,1)S(1)} collective-permute-done((bf16[16,8,128]{2,1,0:T(8,128)(2,1)S(1)}, bf16[16,8,128]{2,1,0:T(8,128)(2,1)S(1)}, u32[]{:S(2)}, u32[]{:S(2)}) %collective-permute-start.8) | collective-permute-done | bytes 32800 | tf_op jit(solution)/shard_map/ppermute | solution.py:169
  36.6 0.7 %collective-permute-start.6 = (s32[6,8]{1,0:T(8,128)S(1)}, s32[6,8]{1,0:T(8,128)S(1)}, u32[]{:S(2)}, u32[]{:S(2)}) collective-permute-start(s32[6,8]{1,0:T(8,128)S(1)} %pad_add_fusion.refs_0_), channel_id=1, source_target_pairs={{0,1},{1,0},{2,3},{3,2},{4,5},{5,4},{6,7},{7,6},{8,9},{9,8},{10,11... | collective-permute-start | bytes 584 | tf_op jit(solution)/shard_map/ppermute | solution.py:169
  37.3 0.5 shard_map.38
  37.9 1.2 %collective-permute-done.6.refs_0_ = s32[6,8]{1,0:T(8,128)S(1)} collective-permute-done((s32[6,8]{1,0:T(8,128)S(1)}, s32[6,8]{1,0:T(8,128)S(1)}, u32[]{:S(2)}, u32[]{:S(2)}) %collective-permute-start.6) | collective-permute-done | bytes 224 | tf_op jit(solution)/shard_map/ppermute | solution.py:169
  39.1 1.5 %collective-permute-start.10 = (bf16[16,8,128]{2,1,0:T(8,128)(2,1)S(1)}, bf16[16,8,128]{2,1,0:T(8,128)(2,1)S(1)}, u32[]{:S(2)}, u32[]{:S(2)}) collective-permute-start(bf16[16,8,128]{2,1,0:T(8,128)(2,1)S(1)} %get-tuple-element.22), channel_id=1, source_target_pairs={{0,1},{1,0},{2,3},{3,2},{4,5},{5,4},{6,7},{7,6},{8,9},{9,8},{10,11... | collective-permute-start | bytes 98312 | tf_op jit(solution)/shard_map/ppermute | solution.py:169
  40.6 0.9 %collective-permute-done.10.refs_2_ = bf16[16,8,128]{2,1,0:T(8,128)(2,1)S(1)} collective-permute-done((bf16[16,8,128]{2,1,0:T(8,128)(2,1)S(1)}, bf16[16,8,128]{2,1,0:T(8,128)(2,1)S(1)}, u32[]{:S(2)}, u32[]{:S(2)}) %collective-permute-start.10) | collective-permute-done | bytes 32800 | tf_op jit(solution)/shard_map/ppermute | solution.py:169
  41.4 1.0 %collective-permute-start.5 = (s32[3,8]{1,0:T(4,128)S(1)}, s32[3,8]{1,0:T(4,128)S(1)}, u32[]{:S(2)}, u32[]{:S(2)}) collective-permute-start(s32[3,8]{1,0:T(4,128)S(1)} %bitcast.21), channel_id=1, source_target_pairs={{0,2},{1,3},{2,0},{3,1},{4,6},{5,7},{6,4},{7,5},{8,10},{9,11},{10,... | collective-permute-start | bytes 296 | tf_op jit(solution)/shard_map/ppermute | solution.py:169
  43.9 1.9 %collective-permute-done.14.refs_2_ = bf16[16,8,128]{2,1,0:T(8,128)(2,1)S(1)} collective-permute-done((bf16[16,8,128]{2,1,0:T(8,128)(2,1)S(1)}, bf16[16,8,128]{2,1,0:T(8,128)(2,1)S(1)}, u32[]{:S(2)}, u32[]{:S(2)}) %collective-permute-start.14) | collective-permute-done | bytes 32800 | tf_op jit(solution)/shard_map/ppermute | solution.py:169
  45.8 0.5 shard_map.40
  46.3 1.8 %collective-permute-start.16 = (bf16[16,8,128]{2,1,0:T(8,128)(2,1)S(1)}, bf16[16,8,128]{2,1,0:T(8,128)(2,1)S(1)}, u32[]{:S(2)}, u32[]{:S(2)}) collective-permute-start(bf16[16,8,128]{2,1,0:T(8,128)(2,1)S(1)} %get-tuple-element.24.refs_1_), channel_id=1, source_target_pairs={{0,1},{1,0},{2,3},{3,2},{4,5},{5,4},{6,7},{7,6},{8,9},{9,8},{10,11... | collective-permute-start | bytes 98312 | tf_op jit(solution)/shard_map/ppermute | solution.py:169
  48.1 0.9 %collective-permute-done.16.refs_2_ = bf16[16,8,128]{2,1,0:T(8,128)(2,1)S(1)} collective-permute-done((bf16[16,8,128]{2,1,0:T(8,128)(2,1)S(1)}, bf16[16,8,128]{2,1,0:T(8,128)(2,1)S(1)}, u32[]{:S(2)}, u32[]{:S(2)}) %collective-permute-start.16) | collective-permute-done | bytes 32800 | tf_op jit(solution)/shard_map/ppermute | solution.py:169
  50.1 0.7 %collective-permute-done.17.refs_1_ = bf16[16,8,128]{2,1,0:T(8,128)(2,1)S(1)} collective-permute-done((bf16[16,8,128]{2,1,0:T(8,128)(2,1)S(1)}, bf16[16,8,128]{2,1,0:T(8,128)(2,1)S(1)}, u32[]{:S(2)}, u32[]{:S(2)}) %collective-permute-start.17) | collective-permute-done | bytes 32800 | tf_op jit(solution)/shard_map/ppermute | solution.py:169
  51.1 7.1 %collective-permute-start.23 = (f32[8,8,128]{2,1,0:T(8,128)S(1)}, f32[8,8,128]{2,1,0:T(8,128)S(1)}, u32[]{:S(2)}, u32[]{:S(2)}) collective-permute-start(f32[8,8,128]{2,1,0:T(8,128)S(1)} %slice.3), channel_id=1, source_target_pairs={{0,1},{1,0},{2,3},{3,2},{4,5},{5,4},{6,7},{7,6},{8,9},{9,8},{10,11... | collective-permute-start | bytes 98312 | tf_op jit(solution)/shard_map/ppermute | solution.py:169
  58.3 0.5 shard_map.42
  58.8 1.0 %collective-permute-start.21 = (bf16[16,8,128]{2,1,0:T(8,128)(2,1)S(1)}, bf16[16,8,128]{2,1,0:T(8,128)(2,1)S(1)}, u32[]{:S(2)}, u32[]{:S(2)}) collective-permute-start(bf16[16,8,128]{2,1,0:T(8,128)(2,1)S(1)} %get-tuple-element.28), channel_id=1, source_target_pairs={{0,4},{1,5},{2,6},{3,7},{4,0},{5,1},{6,2},{7,3},{8,12},{9,13},{10,... | collective-permute-start | bytes 98312 | tf_op jit(solution)/shard_map/ppermute | solution.py:169
  59.8 1.2 %collective-permute-start.22 = (bf16[16,8,128]{2,1,0:T(8,128)(2,1)S(1)}, bf16[16,8,128]{2,1,0:T(8,128)(2,1)S(1)}, u32[]{:S(2)}, u32[]{:S(2)}) collective-permute-start(bf16[16,8,128]{2,1,0:T(8,128)(2,1)S(1)} %get-tuple-element.28), channel_id=1, source_target_pairs={{0,5},{1,4},{2,7},{3,6},{4,1},{5,0},{6,3},{7,2},{8,13},{9,12},{10,... | collective-permute-start | bytes 98312 | tf_op jit(solution)/shard_map/ppermute | solution.py:169
  61.1 0.6 collective-permute-done.21.refs_1_
  61.7 1.8 %collective-permute-done.22.refs_2_ = bf16[16,8,128]{2,1,0:T(8,128)(2,1)S(1)} collective-permute-done((bf16[16,8,128]{2,1,0:T(8,128)(2,1)S(1)}, bf16[16,8,128]{2,1,0:T(8,128)(2,1)S(1)}, u32[]{:S(2)}, u32[]{:S(2)}) %collective-permute-start.22) | collective-permute-done | bytes 32800 | tf_op jit(solution)/shard_map/ppermute | solution.py:169
  63.5 1.0 %shard_map.43 = f32[8,1024]{1,0:T(8,128)} custom-call(s32[6,8]{1,0:T(8,128)S(1)} %pad_add_fusion.refs_0_, bf16[16,8,128]{2,1,0:T(8,128)(2,1)S(1)} %collective-permute-done.21.refs_1_, bf16[16,8,128]{2,1,0:T(8,128)(2,1)S(1)} %collective-permute-done.22.refs_2_, bf16[8,4,64,128]{3,2,1,0:T(8,128)(2,1)S(1)} %stage_in.1.refs_5_.refs_4_.refs_3_, ...), custom_call_target="tpu_custom_call" | custom-call | tf_op jit(solution)/shard_map/pallas_call | solution.py:110
  (35 shorter events, 4.9 us)
Async XLA Ops:
  0.0 16.1 %copy-start.2 = (s32[1,8,3]{1,0,2:T(1,128)S(1)}, s32[1,8,3]{1,0,2:T(1,128)}, u32[]{:S(2)}) copy-start(s32[1,8,3]{1,0,2:T(1,128)} %param.5) | copy-start | bytes 292
  0.0 13.0 %collective-permute-start.12 = (bf16[8,4,64,128]{3,2,1,0:T(8,128)(2,1)}, bf16[8,4,64,128]{3,2,1,0:T(8,128)(2,1)S(1)}, u32[]{:S(2)}, u32[]{:S(2)}) collective-permute-start(bf16[8,4,64,128]{3,2,1,0:T(8,128)(2,1)} %bitcast.10), channel_id=1, source_target_pairs={{0,1},{1,0},{2,3},{3,2},{4,5},{5,4},{6,7},{7,6},{8,9},{9,8},{10,11... | collective-permute-start | bytes 1572872 | tf_op jit(solution)/shard_map/ppermute | solution.py:169
  1.2 31.8 %collective-permute-start.4 = (bf16[8,4,64,128]{3,2,1,0:T(8,128)(2,1)}, bf16[8,4,64,128]{3,2,1,0:T(8,128)(2,1)S(1)}, u32[]{:S(2)}, u32[]{:S(2)}) collective-permute-start(bf16[8,4,64,128]{3,2,1,0:T(8,128)(2,1)} %bitcast.11), channel_id=1, source_target_pairs={{0,1},{1,0},{2,3},{3,2},{4,5},{5,4},{6,7},{7,6},{8,9},{9,8},{10,11... | collective-permute-start | bytes 1572872 | tf_op jit(solution)/shard_map/ppermute | solution.py:169
  13.0 29.4 %collective-permute-start.13 = (bf16[8,4,64,128]{3,2,1,0:T(8,128)(2,1)S(1)}, bf16[8,4,64,128]{3,2,1,0:T(8,128)(2,1)S(1)}, u32[]{:S(2)}, u32[]{:S(2)}) collective-permute-start(bf16[8,4,64,128]{3,2,1,0:T(8,128)(2,1)S(1)} %collective-permute-done.12.refs_4_.refs_3_), channel_id=1, source_target_pairs={{0,1},{1,0},{2,3},{3,2},{4,5},{5,4},{6,7},{7,6},{8,9},{9,8},{10,11... | collective-permute-start | bytes 1572872 | tf_op jit(solution)/shard_map/ppermute | solution.py:169
  14.6 29.3 %collective-permute-start.15 = (bf16[8,4,64,128]{3,2,1,0:T(8,128)(2,1)}, bf16[8,4,64,128]{3,2,1,0:T(8,128)(2,1)S(1)}, u32[]{:S(2)}, u32[]{:S(2)}) collective-permute-start(bf16[8,4,64,128]{3,2,1,0:T(8,128)(2,1)} %bitcast.12), channel_id=1, source_target_pairs={{0,1},{1,0},{2,3},{3,2},{4,5},{5,4},{6,7},{7,6},{8,9},{9,8},{10,11... | collective-permute-start | bytes 1572872 | tf_op jit(solution)/shard_map/ppermute | solution.py:169
  15.8 42.5 %collective-permute-start.19 = (bf16[8,4,64,128]{3,2,1,0:T(8,128)(2,1)}, bf16[8,4,64,128]{3,2,1,0:T(8,128)(2,1)S(1)}, u32[]{:S(2)}, u32[]{:S(2)}) collective-permute-start(bf16[8,4,64,128]{3,2,1,0:T(8,128)(2,1)} %bitcast.13), channel_id=1, source_target_pairs={{0,1},{1,0},{2,3},{3,2},{4,5},{5,4},{6,7},{7,6},{8,10},{9,11},{10,... | collective-permute-start | bytes 1572872 | tf_op jit(solution)/shard_map/ppermute | solution.py:169
  16.1 1.8 %collective-permute-start = (s32[3,8]{1,0:T(4,128)S(1)}, s32[3,8]{1,0:T(4,128)S(1)}, u32[]{:S(2)}, u32[]{:S(2)}) collective-permute-start(s32[3,8]{1,0:T(4,128)S(1)} %bitcast.19), channel_id=1, source_target_pairs={{0,1},{1,0},{2,3},{3,2},{4,5},{5,4},{6,7},{7,6},{8,9},{9,8},{10,11... | collective-permute-start | bytes 296 | tf_op jit(solution)/shard_map/ppermute | solution.py:169
  17.9 1.4 %collective-permute-start.1 = (f32[8,8,128]{2,1,0:T(8,128)}, f32[8,8,128]{2,1,0:T(8,128)S(1)}, u32[]{:S(2)}, u32[]{:S(2)}) collective-permute-start(f32[8,8,128]{2,1,0:T(8,128)} %bitcast.15), channel_id=1, source_target_pairs={{0,1},{1,0},{2,3},{3,2},{4,5},{5,4},{6,7},{7,6},{8,9},{9,8},{10,11... | collective-permute-start | bytes 98312 | tf_op jit(solution)/shard_map/ppermute | solution.py:169
  19.3 9.6 %collective-permute-start.2 = (f32[8,8,128]{2,1,0:T(8,128)}, f32[8,8,128]{2,1,0:T(8,128)S(1)}, u32[]{:S(2)}, u32[]{:S(2)}) collective-permute-start(f32[8,8,128]{2,1,0:T(8,128)} %bitcast.16), channel_id=1, source_target_pairs={{0,2},{1,3},{2,0},{3,1},{4,6},{5,7},{6,4},{7,5},{8,10},{9,11},{10,... | collective-permute-start | bytes 98312 | tf_op jit(solution)/shard_map/ppermute | solution.py:169
  19.6 1.0 %copy-start = (bf16[1,8,4,64,128]{4,3,2,1,0:T(8,128)(2,1)S(1)}, bf16[1,8,4,64,128]{4,3,2,1,0:T(8,128)(2,1)}, u32[]{:S(2)}) copy-start(bf16[1,8,4,64,128]{4,3,2,1,0:T(8,128)(2,1)} %param.4) | copy-start | bytes 1572868
  20.6 8.3 %copy-start.1 = (f32[1,8,1024]{2,1,0:T(8,128)S(1)}, f32[1,8,1024]{2,1,0:T(8,128)}, u32[]{:S(2)}) copy-start(f32[1,8,1024]{2,1,0:T(8,128)} %param.3) | copy-start | bytes 98308
  28.9 4.1 %collective-permute-start.3 = (f32[8,8,128]{2,1,0:T(8,128)S(1)}, f32[8,8,128]{2,1,0:T(8,128)S(1)}, u32[]{:S(2)}, u32[]{:S(2)}) collective-permute-start(f32[8,8,128]{2,1,0:T(8,128)S(1)} %bitcast.17), channel_id=1, source_target_pairs={{0,3},{1,2},{2,1},{3,0},{4,7},{5,6},{6,5},{7,4},{8,11},{9,10},{10,... | collective-permute-start | bytes 98312 | tf_op jit(solution)/shard_map/ppermute | solution.py:169
  33.6 1.8 %collective-permute-start.7 = (bf16[16,8,128]{2,1,0:T(8,128)(2,1)S(1)}, bf16[16,8,128]{2,1,0:T(8,128)(2,1)S(1)}, u32[]{:S(2)}, u32[]{:S(2)}) collective-permute-start(bf16[16,8,128]{2,1,0:T(8,128)(2,1)S(1)} %get-tuple-element.19), channel_id=1, source_target_pairs={{0,4},{1,5},{2,6},{3,7},{4,0},{5,1},{6,2},{7,3},{8,12},{9,13},{10,... | collective-permute-start | bytes 98312 | tf_op jit(solution)/shard_map/ppermute | solution.py:169
  34.0 6.5 %collective-permute-start.11 = (bf16[32,8,128]{2,1,0:T(8,128)(2,1)S(1)}, bf16[32,8,128]{2,1,0:T(8,128)(2,1)S(1)}, u32[]{:S(2)}, u32[]{:S(2)}) collective-permute-start(bf16[32,8,128]{2,1,0:T(8,128)(2,1)S(1)} %convert_element_type.3), channel_id=1, source_target_pairs={{0,1},{1,0},{2,3},{3,2},{4,5},{5,4},{6,7},{7,6},{8,9},{9,8},{10,11... | collective-permute-start | bytes 196616 | tf_op jit(solution)/shard_map/ppermute | solution.py:169
  35.4 1.3 %collective-permute-start.8 = (bf16[16,8,128]{2,1,0:T(8,128)(2,1)S(1)}, bf16[16,8,128]{2,1,0:T(8,128)(2,1)S(1)}, u32[]{:S(2)}, u32[]{:S(2)}) collective-permute-start(bf16[16,8,128]{2,1,0:T(8,128)(2,1)S(1)} %get-tuple-element.19), channel_id=1, source_target_pairs={{0,6},{1,7},{2,4},{3,5},{4,2},{5,3},{6,0},{7,1},{8,14},{9,15},{10,... | collective-permute-start | bytes 98312 | tf_op jit(solution)/shard_map/ppermute | solution.py:169
  36.6 2.5 %collective-permute-start.6 = (s32[6,8]{1,0:T(8,128)S(1)}, s32[6,8]{1,0:T(8,128)S(1)}, u32[]{:S(2)}, u32[]{:S(2)}) collective-permute-start(s32[6,8]{1,0:T(8,128)S(1)} %pad_add_fusion.refs_0_), channel_id=1, source_target_pairs={{0,1},{1,0},{2,3},{3,2},{4,5},{5,4},{6,7},{7,6},{8,9},{9,8},{10,11... | collective-permute-start | bytes 584 | tf_op jit(solution)/shard_map/ppermute | solution.py:169
  39.1 2.4 %collective-permute-start.10 = (bf16[16,8,128]{2,1,0:T(8,128)(2,1)S(1)}, bf16[16,8,128]{2,1,0:T(8,128)(2,1)S(1)}, u32[]{:S(2)}, u32[]{:S(2)}) collective-permute-start(bf16[16,8,128]{2,1,0:T(8,128)(2,1)S(1)} %get-tuple-element.22), channel_id=1, source_target_pairs={{0,1},{1,0},{2,3},{3,2},{4,5},{5,4},{6,7},{7,6},{8,9},{9,8},{10,11... | collective-permute-start | bytes 98312 | tf_op jit(solution)/shard_map/ppermute | solution.py:169
  40.6 1.8 %collective-permute-start.9 = (bf16[16,8,128]{2,1,0:T(8,128)(2,1)S(1)}, bf16[16,8,128]{2,1,0:T(8,128)(2,1)S(1)}, u32[]{:S(2)}, u32[]{:S(2)}) collective-permute-start(bf16[16,8,128]{2,1,0:T(8,128)(2,1)S(1)} %get-tuple-element.22), channel_id=1, source_target_pairs={{0,1},{1,0},{2,3},{3,2},{4,5},{5,4},{6,7},{7,6},{8,9},{9,8},{10,11... | collective-permute-start | bytes 98312 | tf_op jit(solution)/shard_map/ppermute | solution.py:169
  41.4 2.4 %collective-permute-start.5 = (s32[3,8]{1,0:T(4,128)S(1)}, s32[3,8]{1,0:T(4,128)S(1)}, u32[]{:S(2)}, u32[]{:S(2)}) collective-permute-start(s32[3,8]{1,0:T(4,128)S(1)} %bitcast.21), channel_id=1, source_target_pairs={{0,2},{1,3},{2,0},{3,1},{4,6},{5,7},{6,4},{7,5},{8,10},{9,11},{10,... | collective-permute-start | bytes 296 | tf_op jit(solution)/shard_map/ppermute | solution.py:169
  43.0 2.8 %collective-permute-start.14 = (bf16[16,8,128]{2,1,0:T(8,128)(2,1)S(1)}, bf16[16,8,128]{2,1,0:T(8,128)(2,1)S(1)}, u32[]{:S(2)}, u32[]{:S(2)}) collective-permute-start(bf16[16,8,128]{2,1,0:T(8,128)(2,1)S(1)} %get-tuple-element.23.refs_1_), channel_id=1, source_target_pairs={{0,1},{1,0},{2,3},{3,2},{4,5},{5,4},{6,7},{7,6},{8,9},{9,8},{10,11... | collective-permute-start | bytes 98312 | tf_op jit(solution)/shard_map/ppermute | solution.py:169
  46.3 2.7 %collective-permute-start.16 = (bf16[16,8,128]{2,1,0:T(8,128)(2,1)S(1)}, bf16[16,8,128]{2,1,0:T(8,128)(2,1)S(1)}, u32[]{:S(2)}, u32[]{:S(2)}) collective-permute-start(bf16[16,8,128]{2,1,0:T(8,128)(2,1)S(1)} %get-tuple-element.24.refs_1_), channel_id=1, source_target_pairs={{0,1},{1,0},{2,3},{3,2},{4,5},{5,4},{6,7},{7,6},{8,9},{9,8},{10,11... | collective-permute-start | bytes 98312 | tf_op jit(solution)/shard_map/ppermute | solution.py:169
  49.5 1.3 %collective-permute-start.17 = (bf16[16,8,128]{2,1,0:T(8,128)(2,1)S(1)}, bf16[16,8,128]{2,1,0:T(8,128)(2,1)S(1)}, u32[]{:S(2)}, u32[]{:S(2)}) collective-permute-start(bf16[16,8,128]{2,1,0:T(8,128)(2,1)S(1)} %get-tuple-element.26), channel_id=1, source_target_pairs={{0,1},{1,0},{2,3},{3,2},{4,5},{5,4},{6,7},{7,6},{8,9},{9,8},{10,11... | collective-permute-start | bytes 98312 | tf_op jit(solution)/shard_map/ppermute | solution.py:169
  49.9 8.4 %collective-permute-start.20 = (f32[8,8,128]{2,1,0:T(8,128)S(1)}, f32[8,8,128]{2,1,0:T(8,128)S(1)}, u32[]{:S(2)}, u32[]{:S(2)}) collective-permute-start(f32[8,8,128]{2,1,0:T(8,128)S(1)} %get-tuple-element.27.refs_5_), channel_id=1, source_target_pairs={{0,2},{1,3},{2,0},{3,1},{4,6},{5,7},{6,4},{7,5},{8,10},{9,11},{10,... | collective-permute-start | bytes 98312 | tf_op jit(solution)/shard_map/ppermute | solution.py:169
  50.8 7.5 %collective-permute-start.18 = (bf16[16,8,128]{2,1,0:T(8,128)(2,1)S(1)}, bf16[16,8,128]{2,1,0:T(8,128)(2,1)S(1)}, u32[]{:S(2)}, u32[]{:S(2)}) collective-permute-start(bf16[16,8,128]{2,1,0:T(8,128)(2,1)S(1)} %collective-permute-done.17.refs_1_), channel_id=1, source_target_pairs={{0,1},{1,0},{2,3},{3,2},{4,5},{5,4},{6,7},{7,6},{8,9},{9,8},{10,11... | collective-permute-start | bytes 98312 | tf_op jit(solution)/shard_map/ppermute | solution.py:169
  51.1 9.9 %collective-permute-start.23 = (f32[8,8,128]{2,1,0:T(8,128)S(1)}, f32[8,8,128]{2,1,0:T(8,128)S(1)}, u32[]{:S(2)}, u32[]{:S(2)}) collective-permute-start(f32[8,8,128]{2,1,0:T(8,128)S(1)} %slice.3), channel_id=1, source_target_pairs={{0,1},{1,0},{2,3},{3,2},{4,5},{5,4},{6,7},{7,6},{8,9},{9,8},{10,11... | collective-permute-start | bytes 98312 | tf_op jit(solution)/shard_map/ppermute | solution.py:169
  58.8 2.8 %collective-permute-start.21 = (bf16[16,8,128]{2,1,0:T(8,128)(2,1)S(1)}, bf16[16,8,128]{2,1,0:T(8,128)(2,1)S(1)}, u32[]{:S(2)}, u32[]{:S(2)}) collective-permute-start(bf16[16,8,128]{2,1,0:T(8,128)(2,1)S(1)} %get-tuple-element.28), channel_id=1, source_target_pairs={{0,4},{1,5},{2,6},{3,7},{4,0},{5,1},{6,2},{7,3},{8,12},{9,13},{10,... | collective-permute-start | bytes 98312 | tf_op jit(solution)/shard_map/ppermute | solution.py:169
  59.8 3.7 %collective-permute-start.22 = (bf16[16,8,128]{2,1,0:T(8,128)(2,1)S(1)}, bf16[16,8,128]{2,1,0:T(8,128)(2,1)S(1)}, u32[]{:S(2)}, u32[]{:S(2)}) collective-permute-start(bf16[16,8,128]{2,1,0:T(8,128)(2,1)S(1)} %get-tuple-element.28), channel_id=1, source_target_pairs={{0,5},{1,4},{2,7},{3,6},{4,1},{5,0},{6,3},{7,2},{8,13},{9,12},{10,... | collective-permute-start | bytes 98312 | tf_op jit(solution)/shard_map/ppermute | solution.py:169
